TPU v7x, 32 devices: a whole 2x2x4 slice. The times are simulated.
32 devices in a mesh: ctx: 8 (over z, x), dp: 4 (over y, core).
Axes of the slice: x: 2, y: 2, z: 4, core: 2. Of those that a mesh axis runs over, the one named last changes fastest.
Arguments:
- queries: bfloat16 [4, 2048, 1024], P('dp', 'ctx'), may hold values from -8 to 8
- keys: bfloat16 [4, 2048, 1024], P('dp', 'ctx'), may hold values from -8 to 8
- values: bfloat16 [4, 2048, 1024], P('dp', 'ctx'), may hold values from -6 to 6
- cotangent: bfloat16 [4, 2048, 2048], P('dp', 'ctx'), may hold values from -6 to 6
- proj_weight: bfloat16 [1024, 2048], P('dp'), may hold values from -0.1875 to 0.1875
- pattern: int32 [4, 8, 16, 2], P('dp'), may hold values 0 or 1
Outputs:
- projected: bfloat16 [4, 2048, 2048], P('dp', 'ctx')
- grad_query: bfloat16 [4, 2048, 1024], P('dp', 'ctx')
- grad_key: bfloat16 [4, 2048, 1024], P('dp', 'ctx')
- grad_value: bfloat16 [4, 2048, 1024], P('dp', 'ctx')
- grad_proj: float32 [1024, 2048], P('dp', 'ctx')
Inputs may be any that keep to these rules, and one draw needn't show every extreme that they name: `pattern`: entries with o = 0 or with q - o < 1 are not read.
All inputs are finite; a program needn't handle non-finite values. No bound on the sum of `pattern` on one device may be relied on, other than what follows from the above.
Results may differ from a plain program's by a relative error of at most 0.0085.
The roundings to bfloat16 on the way count: a program that leaves them out, or rounds other values in their place, can miss the bound.
Values may be sent and summed in bfloat16 or wider, within the bound.
No kernel may reach another device: no remote copies, remote signals or barrier semaphores. Data moves between devices by JAX's collectives and lax.ppermute only.
A program may use at most 128 MiB of HBM per device.

v0:
```python
import jax
import jax.numpy as jnp
from jax import lax
from jax.sharding import PartitionSpec as P

HEADS = 8
HDIM = 128
BLK = 128
BLK_DEV = 2
WIN = 2


masked_value = -1e30


def shifted(value, axis, steps):
    count = lax.axis_size(axis)
    leading, last = (max(0, -steps), min(count, count - steps))
    return lax.ppermute(value, axis, [(source, source + steps) for source in range(leading, last)])


def spread(block, axis, holder):
    block = jnp.where(lax.axis_index(axis) == holder, block, jnp.zeros_like(block))
    return lax.psum(block, axis)


def product(form, left, right):
    return jnp.einsum(form, left, right, preferred_element_type=jnp.float32)


def block_masks(pattern_rows, query_blocks):
    column = jnp.arange(WIN * BLK, dtype=jnp.int32)
    within = jnp.arange(BLK, dtype=jnp.int32)
    offsets = WIN - 1 - jnp.arange(WIN, dtype=jnp.int32)
    flipped = jnp.flip(pattern_rows, axis=2) == 1
    key_blocks = query_blocks[:, None] - offsets[None, :]
    permitted = (flipped | (offsets == 0)[None, None, :]) & (key_blocks >= 1)[:, None, :]
    expanded = jnp.repeat(permitted, BLK, axis=2)
    causal = (column[None, :] < (WIN - 1) * BLK) | (
        column[None, :] - (WIN - 1) * BLK <= within[:, None]
    )
    key_mask = expanded[:, :, None, :] & causal[None, None, :, :]
    sink_mask = (query_blocks[:, None, None] > 0) | (within[None, None, :] <= within[None, :, None])
    return (key_mask, sink_mask[:, None, :, :])


def attend_scores(queries_b, key_window, sink_keys, key_mask, sink_mask):
    inverse_root = HDIM ** (-0.5)
    scores = product("nqhd,nkhd->nhqk", queries_b, key_window) * inverse_root
    sink_scores = product("nqhd,khd->nhqk", queries_b, sink_keys) * inverse_root
    return (
        jnp.where(key_mask, scores, masked_value),
        jnp.where(sink_mask, sink_scores, masked_value),
    )


def forward_blocks(
    queries_b, key_window, value_window, sink_keys, sink_values, key_mask, sink_mask
):
    scores, sink_scores = attend_scores(queries_b, key_window, sink_keys, key_mask, sink_mask)
    row_max = jnp.maximum(jnp.max(scores, axis=-1), jnp.max(sink_scores, axis=-1))
    row_total = jnp.sum(jnp.exp(scores - row_max[..., None]), axis=-1) + jnp.sum(
        jnp.exp(sink_scores - row_max[..., None]), axis=-1
    )
    log_total = row_max + jnp.log(row_total)
    weights = jnp.exp(scores - log_total[..., None]).astype(jnp.bfloat16)
    sink_weights = jnp.exp(sink_scores - log_total[..., None]).astype(jnp.bfloat16)
    attended = product("nhqk,nkhd->nqhd", weights, value_window) + product(
        "nhqk,khd->nqhd", sink_weights, sink_values
    )
    return (attended.astype(jnp.bfloat16), log_total)


def backward_blocks(
    queries_b,
    key_window,
    value_window,
    sink_keys,
    sink_values,
    key_mask,
    sink_mask,
    log_total,
    out_grad,
    row_delta,
):
    inverse_root = HDIM ** (-0.5)
    scores, sink_scores = attend_scores(queries_b, key_window, sink_keys, key_mask, sink_mask)
    weights = jnp.exp(scores - log_total[..., None])
    sink_weights = jnp.exp(sink_scores - log_total[..., None])
    prob_grad = product("nqhd,nkhd->nhqk", out_grad, value_window)
    sink_prob_grad = product("nqhd,khd->nhqk", out_grad, sink_values)
    score_grad = (weights * (prob_grad - row_delta[..., None])).astype(jnp.bfloat16)
    sink_score_grad = (sink_weights * (sink_prob_grad - row_delta[..., None])).astype(jnp.bfloat16)
    query_grad = inverse_root * (
        product("nhqk,nkhd->nqhd", score_grad, key_window)
        + product("nhqk,khd->nqhd", sink_score_grad, sink_keys)
    )
    window_key_grad = inverse_root * product("nhqk,nqhd->nkhd", score_grad, queries_b)
    window_value_grad = product("nhqk,nqhd->nkhd", weights.astype(jnp.bfloat16), out_grad)
    sink_key_grad = inverse_root * product("nhqk,nqhd->khd", sink_score_grad, queries_b)
    sink_value_grad = product("nhqk,nqhd->khd", sink_weights.astype(jnp.bfloat16), out_grad)
    return (query_grad, window_key_grad, window_value_grad, sink_key_grad, sink_value_grad)


def make_windows(extended, first):
    pieces = [
        extended[(number + first) * BLK : (number + first + WIN) * BLK] for number in range(BLK_DEV)
    ]
    return jnp.stack(pieces).reshape(BLK_DEV, WIN * BLK, HEADS, HDIM)


def place_windows(window_grad):
    flat = window_grad.reshape(BLK_DEV, WIN * BLK, HEADS * HDIM)
    placed = jnp.zeros((2 * BLK_DEV * BLK, HEADS * HDIM), jnp.float32)
    for number in range(BLK_DEV):
        placed = placed + jnp.pad(
            flat[number], (((number + 1) * BLK, (2 * BLK_DEV - number - 1 - WIN) * BLK), (0, 0))
        )
    return placed


def body(queries, keys, values, cotangent, proj_weight, pattern):
    query_rows = queries[0]
    key_rows = keys[0]
    value_rows = values[0]
    grad_output = cotangent[0]
    pattern_doc = pattern[0]
    rows = query_rows.shape[0]
    width_heads = query_rows.shape[1]
    context_index = lax.axis_index("ctx")
    context_count = lax.axis_size("ctx")
    document_count = lax.axis_size("dp")
    prev_keys, prev_values = shifted((key_rows, value_rows), "ctx", 1)
    first_keys, first_values = (
        spread(key_rows[:BLK], "ctx", 0),
        spread(value_rows[:BLK], "ctx", 0),
    )
    full_weight = lax.all_gather(proj_weight, "dp", axis=0, tiled=True)
    query_blocks = context_index * BLK_DEV + jnp.arange(BLK_DEV, dtype=jnp.int32)
    pattern_rows = jnp.transpose(
        lax.dynamic_slice_in_dim(pattern_doc, context_index * BLK_DEV, BLK_DEV, 1), (1, 0, 2)
    )
    key_mask, sink_mask = block_masks(pattern_rows, query_blocks)
    key_window = make_windows(jnp.concatenate([prev_keys, key_rows], axis=0), 1)
    value_window = make_windows(jnp.concatenate([prev_values, value_rows], axis=0), 1)
    query_blocked = query_rows.reshape(BLK_DEV, BLK, HEADS, HDIM)
    sink_keys = first_keys.reshape(BLK, HEADS, HDIM)
    sink_values = first_values.reshape(BLK, HEADS, HDIM)
    attended, log_total = forward_blocks(
        query_blocked, key_window, value_window, sink_keys, sink_values, key_mask, sink_mask
    )
    attended_rows = attended.reshape(rows, width_heads)
    projected = jnp.dot(attended_rows, full_weight, preferred_element_type=jnp.float32).astype(
        jnp.bfloat16
    )
    grad_attended = lax.dot_general(
        grad_output, full_weight, (((1,), (1,)), ((), ())), preferred_element_type=jnp.float32
    ).astype(jnp.bfloat16)
    weight_scale = float(rows * context_count * document_count) ** (-0.5)
    partial_sum = lax.psum_scatter(
        lax.dot_general(
            attended_rows, grad_output, (((0,), (0,)), ((), ())), preferred_element_type=jnp.float32
        )
        * weight_scale,
        "dp",
        scatter_dimension=0,
        tiled=True,
    )
    grad_proj = lax.psum_scatter(partial_sum, "ctx", scatter_dimension=1, tiled=True)
    row_delta = jnp.sum(
        grad_attended.astype(jnp.float32).reshape(rows, HEADS, HDIM)
        * attended_rows.astype(jnp.float32).reshape(rows, HEADS, HDIM),
        axis=-1,
    )
    delta_blocked = jnp.transpose(row_delta.reshape(BLK_DEV, BLK, HEADS), (0, 2, 1))
    grad_blocked = grad_attended.reshape(BLK_DEV, BLK, HEADS, HDIM)
    query_grad, window_key, window_value, sink_key, sink_value = backward_blocks(
        query_blocked,
        key_window,
        value_window,
        sink_keys,
        sink_values,
        key_mask,
        sink_mask,
        log_total,
        grad_blocked,
        delta_blocked,
    )
    sink_key_sum, sink_value_sum = lax.psum((sink_key, sink_value), "ctx")
    placed_keys = place_windows(window_key)
    placed_values = place_windows(window_value)
    later_keys, later_values = shifted((placed_keys[:rows], placed_values[:rows]), "ctx", -1)
    own_key = placed_keys[rows:] + later_keys
    own_value = placed_values[rows:] + later_values
    leading = (context_index == 0).astype(jnp.float32)
    own_key = jnp.concatenate(
        [own_key[:BLK] + leading * sink_key_sum.reshape(BLK, width_heads), own_key[BLK:]], axis=0
    )
    own_value = jnp.concatenate(
        [own_value[:BLK] + leading * sink_value_sum.reshape(BLK, width_heads), own_value[BLK:]],
        axis=0,
    )
    return (
        projected[None],
        query_grad.reshape(rows, width_heads).astype(jnp.bfloat16)[None],
        own_key.astype(jnp.bfloat16)[None],
        own_value.astype(jnp.bfloat16)[None],
        grad_proj,
    )


def solution(mesh):
    return jax.shard_map(
        body,
        mesh=mesh,
        in_specs=(
            P("dp", "ctx", None),
            P("dp", "ctx", None),
            P("dp", "ctx", None),
            P("dp", "ctx", None),
            P("dp", None),
            P("dp", None, None, None),
        ),
        out_specs=(
            P("dp", "ctx", None),
            P("dp", "ctx", None),
            P("dp", "ctx", None),
            P("dp", "ctx", None),
            P("dp", "ctx"),
        ),
        check_vma=False,
    )
```

profile of v0, /device:TPU:0, one launch (start us, length us, event | category | flops | bytes accessed | tf_op | source)
XLA Modules:
  0.0 304.7 jit_solution(7784377283178281256)
XLA Ops:
  13.1 5.7 %collective-permute-start = (bf16[256,1024]{0,1:T(8,128)(2,1)S(1)}, bf16[256,1024]{0,1:T(8,128)(2,1)}, u32[]{:S(2)}, u32[]{:S(2)}) collective-permute-start(bf16[256,1024]{0,1:T(8,128)(2,1)S(1)} %bitcast.149), channel_id=1, source_target_pairs={{0,4},{4,8},{8,12},{12,16},{16,20},{20,24},{24,28},{1,5},{5,9},{9,... | collective-permute-start | bytes 1572872 | tf_op jit(solution)/shard_map/ppermute | solution.py:19
  18.8 3.4 %collective-permute-start.1 = (bf16[256,1024]{0,1:T(8,128)(2,1)S(1)}, bf16[256,1024]{0,1:T(8,128)(2,1)}, u32[]{:S(2)}, u32[]{:S(2)}) collective-permute-start(bf16[256,1024]{0,1:T(8,128)(2,1)S(1)} %bitcast.146), channel_id=1, source_target_pairs={{0,4},{4,8},{8,12},{12,16},{16,20},{20,24},{24,28},{1,5},{5,9},{9,... | collective-permute-start | bytes 1572872 | tf_op jit(solution)/shard_map/ppermute | solution.py:19
  26.2 5.9 %collective-permute-done = bf16[256,1024]{0,1:T(8,128)(2,1)} collective-permute-done((bf16[256,1024]{0,1:T(8,128)(2,1)S(1)}, bf16[256,1024]{0,1:T(8,128)(2,1)}, u32[]{:S(2)}, u32[]{:S(2)}) %collective-permute-start) | collective-permute-done | bytes 524320 | tf_op jit(solution)/shard_map/ppermute | solution.py:19
  34.1 9.0 %collective-permute-done.1 = bf16[256,1024]{0,1:T(8,128)(2,1)} collective-permute-done((bf16[256,1024]{0,1:T(8,128)(2,1)S(1)}, bf16[256,1024]{0,1:T(8,128)(2,1)}, u32[]{:S(2)}, u32[]{:S(2)}) %collective-permute-start.1) | collective-permute-done | bytes 524320 | tf_op jit(solution)/shard_map/ppermute | solution.py:19
  45.1 49.3 %all-reduce.11.cloned.1.call-done = (bf16[128,8,128]{2,0,1:T(8,128)(2,1)}, bf16[128,8,128]{2,0,1:T(8,128)(2,1)}) async-done(((bf16[128,8,128]{2,0,1:T(8,128)(2,1)}, bf16[128,8,128]{2,0,1:T(8,128)(2,1)}), (bf16[128,8,128]{2,0,1:T(8,128)(2,1)}, bf16[128,8,128]{2,0,1:T(8,128)(2,1)})) %all-reduce.11.cloned.1.call-update) | async-done | bytes 524304 | tf_op jit(solution)/shard_map/psum | solution.py:24
  95.7 2.4 fusion.48
  102.5 4.6 %convolution_multiply_fusion = f32[1024,2048]{1,0:T(8,128)} fusion(bf16[1,256,2048]{2,1,0:T(8,128)(2,1)S(1)} %copy-done, bf16[32,8,8,128]{3,2,1,0:T(8,128)(2,1)S(1)} %bitcast.156), kind=kOutput, calls=%fused_computation | convolution fusion | flops 1075838976 | bytes 9961472 | tf_op jit(solution)/shard_map/dot_general | solution.py:161
  107.2 2.3 copy.155
  109.5 3.5 %convolution_convert_fusion.1 = bf16[256,1024]{1,0:T(8,128)(2,1)S(1)} fusion(bf16[1024,2048]{1,0:T(8,128)(2,1)} %all-gather.2.cloned.1.call-done, bf16[1,256,2048]{2,1,0:T(8,128)(2,1)S(1)} %copy-done), kind=kOutput, calls=%fused_computation.30 | convolution fusion | flops 1074003968 | bytes 5767168 | tf_op jit(solution)/shard_map/dot_general | solution.py:156
  116.4 2.2 copy.174
  119.5 2.8 convolution_bitcast_fusion.6
  124.8 2.1 copy.172
  132.1 2.1 copy.164
  134.2 2.1 convert_element_type.79
  136.3 41.4 %reduce-scatter.3.cloned.1.call-done = f32[256,2048]{1,0:T(8,128)} async-done(((f32[1024,2048]{1,0:T(8,128)}), f32[256,2048]{1,0:T(8,128)}) %reduce-scatter.3.cloned.1.call-update) | async-done | bytes 2097168 | tf_op jit(solution)/shard_map/reduce_scatter | solution.py:160
  181.0 2.5 copy.169
  183.5 2.5 copy.168
  186.0 2.3 pad_add_fusion.1
  193.5 2.2 fusion
  195.8 9.9 %all-reduce.9.cloned.1.call-done = (f32[128,8,128]{2,0,1:T(8,128)}, f32[128,8,128]{2,0,1:T(8,128)}) async-done(((f32[128,8,128]{2,0,1:T(8,128)}, f32[128,8,128]{2,0,1:T(8,128)}), (f32[128,8,128]{2,0,1:T(8,128)}, f32[128,8,128]{2,0,1:T(8,128)})) %all-reduce.9.cloned.1.call-update) | async-done | bytes 1048592 | tf_op jit(solution)/shard_map/psum | solution.py:189
  209.6 7.0 %collective-permute-done.2 = f32[256,1024]{0,1:T(8,128)} collective-permute-done((f32[256,1024]{0,1:T(8,128)}, f32[256,1024]{0,1:T(8,128)}, u32[]{:S(2)}, u32[]{:S(2)}) %collective-permute-start.2) | collective-permute-done | bytes 1048608 | tf_op jit(solution)/shard_map/ppermute | solution.py:19
  218.9 2.1 copy.178
  224.9 18.4 %collective-permute-done.3 = f32[256,1024]{0,1:T(8,128)} collective-permute-done((f32[256,1024]{0,1:T(8,128)}, f32[256,1024]{0,1:T(8,128)}, u32[]{:S(2)}, u32[]{:S(2)}) %collective-permute-start.3) | collective-permute-done | bytes 1048608 | tf_op jit(solution)/shard_map/ppermute | solution.py:19
  245.9 51.6 %reduce-scatter.5.cloned.1.call-done = f32[256,256]{1,0:T(8,128)} async-done(((f32[256,2048]{1,0:T(8,128)}), f32[256,256]{1,0:T(8,128)}) %reduce-scatter.5.cloned.1.call-update) | async-done | bytes 262160 | tf_op jit(solution)/shard_map/reduce_scatter | solution.py:169
  (144 shorter events, 51.7 us)
Async XLA Ops:
  8.0 94.5 %copy-start = (bf16[1,256,2048]{2,1,0:T(8,128)(2,1)S(1)}, bf16[1,256,2048]{2,1,0:T(8,128)(2,1)}, u32[]{:S(2)}) copy-start(bf16[1,256,2048]{2,1,0:T(8,128)(2,1)} %param.9) | copy-start | bytes 3145732
  8.0 86.4 %all-reduce.11.cloned.1.call-start = ((), (), s32[]{:S(2)}) async-start(), calls=%async_computation.6 | async-start | bytes 1048576 | tf_op jit(solution)/shard_map/psum | solution.py:24
  10.7 12.5 %copy-start.28 = (bf16[1,256,1024]{2,1,0:T(8,128)(2,1)S(1)}, bf16[1,256,1024]{2,1,0:T(8,128)(2,1)}, u32[]{:S(2)}) copy-start(bf16[1,256,1024]{2,1,0:T(8,128)(2,1)} %param.6) | copy-start | bytes 1572868
  12.5 97.0 %all-gather.2.cloned.1.call-start = ((), (), s32[]{:S(2)}) async-start(), calls=%async_computation.2 | async-start | bytes 5242880 | tf_op jit(solution)/shard_map/all_gather | solution.py:138
  13.0 164.7 %reduce-scatter.3.cloned.1.call-start = ((), (), s32[]{:S(2)}) async-start(), calls=%async_computation.3 | async-start | bytes 10485760 | tf_op jit(solution)/shard_map/reduce_scatter | solution.py:160
  13.1 19.0 %collective-permute-start = (bf16[256,1024]{0,1:T(8,128)(2,1)S(1)}, bf16[256,1024]{0,1:T(8,128)(2,1)}, u32[]{:S(2)}, u32[]{:S(2)}) collective-permute-start(bf16[256,1024]{0,1:T(8,128)(2,1)S(1)} %bitcast.149), channel_id=1, source_target_pairs={{0,4},{4,8},{8,12},{12,16},{16,20},{20,24},{24,28},{1,5},{5,9},{9,... | collective-permute-start | bytes 1572872 | tf_op jit(solution)/shard_map/ppermute | solution.py:19
  18.8 24.3 %collective-permute-start.1 = (bf16[256,1024]{0,1:T(8,128)(2,1)S(1)}, bf16[256,1024]{0,1:T(8,128)(2,1)}, u32[]{:S(2)}, u32[]{:S(2)}) collective-permute-start(bf16[256,1024]{0,1:T(8,128)(2,1)S(1)} %bitcast.146), channel_id=1, source_target_pairs={{0,4},{4,8},{8,12},{12,16},{16,20},{20,24},{24,28},{1,5},{5,9},{9,... | collective-permute-start | bytes 1572872 | tf_op jit(solution)/shard_map/ppermute | solution.py:19
  23.3 71.1 %copy-start.10 = (bf16[32,8,8,128]{3,2,1,0:T(8,128)(2,1)}, bf16[32,8,8,128]{3,2,1,0:T(8,128)(2,1)S(1)}, u32[]{:S(2)}) copy-start(bf16[32,8,8,128]{3,2,1,0:T(8,128)(2,1)S(1)} %copy.199) | copy-start | bytes 1572868
  95.7 4.2 %copy-start.1 = (f32[2,8,128,128]{2,3,0,1:T(8,128)}, f32[2,8,128,128]{2,3,0,1:T(8,128)S(1)}, u32[]{:S(2)}) copy-start(f32[2,8,128,128]{2,3,0,1:T(8,128)S(1)} %get-tuple-element.31) | copy-start | bytes 3145732
  107.1 98.5 %all-reduce.9.cloned.1.call-start = ((), (), s32[]{:S(2)}) async-start(), calls=%async_computation.5 | async-start | bytes 2097152 | tf_op jit(solution)/shard_map/psum | solution.py:189
  118.6 3.6 %copy-start.2 = (f32[2,8,128,128]{2,3,0,1:T(8,128)S(1)}, f32[2,8,128,128]{2,3,0,1:T(8,128)}, u32[]{:S(2)}) copy-start(f32[2,8,128,128]{2,3,0,1:T(8,128)} %copy-done.1) | copy-start | bytes 3145732
  118.6 3.6 %copy-start.18 = (bf16[2,128,8,128]{1,3,0,2:T(8,128)(2,1)S(1)}, bf16[2,128,8,128]{1,3,0,2:T(8,128)(2,1)}, u32[]{:S(2)}) copy-start(bf16[2,128,8,128]{1,3,0,2:T(8,128)(2,1)} %copy.174) | copy-start | bytes 1572868
  119.5 3.9 %copy-start.11 = (bf16[32,8,8,128]{3,2,1,0:T(8,128)(2,1)S(1)}, bf16[32,8,8,128]{3,2,1,0:T(8,128)(2,1)}, u32[]{:S(2)}) copy-start(bf16[32,8,8,128]{3,2,1,0:T(8,128)(2,1)} %copy-done.10) | copy-start | bytes 1572868
  123.4 3.5 %copy-start.29 = (f32[256,8]{0,1:T(8,128)S(1)}, f32[256,8]{0,1:T(8,128)}, u32[]{:S(2)}) copy-start(f32[256,8]{0,1:T(8,128)} %copy.156) | copy-start | bytes 24580
  124.5 173.0 %reduce-scatter.5.cloned.1.call-start = ((), (), s32[]{:S(2)}) async-start(), calls=%async_computation.4 | async-start | bytes 2359296 | tf_op jit(solution)/shard_map/reduce_scatter | solution.py:169
  186.0 3.6 %copy-start.12 = (bf16[2,128,8,128]{1,3,2,0:T(8,128)(2,1)S(1)}, bf16[2,128,8,128]{1,3,2,0:T(8,128)(2,1)}, u32[]{:S(2)}) copy-start(bf16[2,128,8,128]{1,3,2,0:T(8,128)(2,1)} %copy.172) | copy-start | bytes 1572868
  188.3 28.2 %collective-permute-start.2 = (f32[256,1024]{0,1:T(8,128)}, f32[256,1024]{0,1:T(8,128)}, u32[]{:S(2)}, u32[]{:S(2)}) collective-permute-start(f32[256,1024]{0,1:T(8,128)} %pad_add_fusion.1), channel_id=1, source_target_pairs={{4,0},{8,4},{12,8},{16,12},{20,16},{24,20},{28,24},{5,1},{9,5},{13... | collective-permute-start | bytes 3145736 | tf_op jit(solution)/shard_map/ppermute | solution.py:19
  191.3 52.0 %collective-permute-start.3 = (f32[256,1024]{0,1:T(8,128)}, f32[256,1024]{0,1:T(8,128)}, u32[]{:S(2)}, u32[]{:S(2)}) collective-permute-start(f32[256,1024]{0,1:T(8,128)} %pad_add_fusion), channel_id=1, source_target_pairs={{4,0},{8,4},{12,8},{16,12},{20,16},{24,20},{28,24},{5,1},{9,5},{13... | collective-permute-start | bytes 3145736 | tf_op jit(solution)/shard_map/ppermute | solution.py:19
  195.8 20.8 %copy-start.4 = (f32[1,256,8,128]{1,3,2,0:T(8,128)S(1)}, f32[1,256,8,128]{1,3,2,0:T(8,128)}, u32[]{:S(2)}) copy-start(f32[1,256,8,128]{1,3,2,0:T(8,128)} %copy.169) | copy-start | bytes 3145732
  195.8 20.8 %copy-start.5 = (f32[1,256,8,128]{1,3,2,0:T(8,128)S(1)}, f32[1,256,8,128]{1,3,2,0:T(8,128)}, u32[]{:S(2)}) copy-start(f32[1,256,8,128]{1,3,2,0:T(8,128)} %copy.168) | copy-start | bytes 3145732
  209.6 8.4 %copy-start.22 = (f32[128,8,128]{0,2,1:T(8,128)S(1)}, f32[128,8,128]{0,2,1:T(8,128)}, u32[]{:S(2)}) copy-start(f32[128,8,128]{0,2,1:T(8,128)} %copy.171) | copy-start | bytes 1572868
  218.0 25.3 %copy-start.7 = (f32[1,256,8,128]{1,3,2,0:T(8,128)S(1)}, f32[1,256,8,128]{1,3,2,0:T(8,128)}, u32[]{:S(2)}) copy-start(f32[1,256,8,128]{1,3,2,0:T(8,128)} %copy-done.6) | copy-start | bytes 3145732
  218.0 25.3 %copy-start.9 = (f32[1,256,8,128]{1,3,2,0:T(8,128)S(1)}, f32[1,256,8,128]{1,3,2,0:T(8,128)}, u32[]{:S(2)}) copy-start(f32[1,256,8,128]{1,3,2,0:T(8,128)} %copy-done.8) | copy-start | bytes 3145732
  224.9 19.8 %copy-start.23 = (f32[128,8,128]{0,2,1:T(8,128)S(1)}, f32[128,8,128]{0,2,1:T(8,128)}, u32[]{:S(2)}) copy-start(f32[128,8,128]{0,2,1:T(8,128)} %copy.177) | copy-start | bytes 1572868
  (17 other events, 31.2 us)
Sparse Core Ops, SparseCore 0:
  12.9 81.4 all-reduce.10
  124.6 80.9 all-reduce.8
  209.8 87.7 reduce-scatter.4
Sparse Core Ops, SparseCore 1:
  14.5 37.0 all-gather.1
  107.2 70.4 reduce-scatter.2
where the time goes:
time: 306 us; the launch traced here: 305 us
  waiting for transfers between devices  193 us (63%)
  local copies, waits for them, and re-layouts  44.3 us (14%)
  matrix products  25 us (8%)
  between operations  15.7 us (5%)
  other arithmetic  14.2 us (5%)
  starting transfers between devices  12.3 us (4%)
    reduce_scatter x1, waiting for transfers between devices, body(): lax.psum_scatter(partial_sum, 'ctx', scatter_dimension=1, tiled=True)  51.6 us
    psum x1, waiting for transfers between devices, spread(): return lax.psum(block, axis)  49.3 us
    reduce_scatter x1, waiting for transfers between devices, body(): lax.psum_scatter(lax.dot_general(attended_rows, grad_output, (((0,), (0,)...  41.4 us
    ppermute x4, waiting for transfers between devices, shifted(): lax.ppermute(value, axis, [(source, source + steps) for source in range(l...  40.3 us
    dot_general x12, matrix products, product(): return jnp.einsum(form, left, right, preferred_element_type=jnp.float32)  14.7 us
    unnamed x71, local copies, waits for them, and re-layouts  13.7 us
    ppermute x4, starting transfers between devices, shifted(): lax.ppermute(value, axis, [(source, source + steps) for source in range(l...  11.9 us
    psum x1, waiting for transfers between devices, body(): sink_key_sum, sink_value_sum = lax.psum((sink_key, sink_value), 'ctx')  9.86 us
  transfers between devices with their start and end apart: 9, of which 8 were waited for; matrix products, arithmetic and copies ran while one was open for 24% of the time, Pallas kernels for 0%

commit v1 on v0

v1 whole, which is shorter than its diff:
```python
import functools

import jax
import jax.numpy as jnp
from jax import lax
from jax.experimental import pallas as pl
from jax.experimental.pallas import tpu as pltpu
from jax.sharding import PartitionSpec as P

HDIM = 128
BLK = 128
WIN = 2
HEADS_STEP = 2

MASKED = -1e30
ROOT = HDIM ** (-0.5)
F32 = jnp.float32
BF16 = jnp.bfloat16


def dot(left, right, left_dim, right_dim):
    return lax.dot_general(
        left, right, (((left_dim,), (right_dim,)), ((), ())), preferred_element_type=F32
    )


def probabilities(q, k_ext, k_sink, pattern_ref, head, first_block):
    blocks = q.shape[0] // BLK
    row = lax.broadcasted_iota(jnp.int32, (BLK, BLK), 0)
    column = lax.broadcasted_iota(jnp.int32, (BLK, BLK), 1)
    causal = column <= row
    sink_scores = dot(q, k_sink, 1, 1) * ROOT
    window, sink = [], []
    for number in range(blocks):
        here = slice(number * BLK, (number + 1) * BLK)
        block = first_block + number
        scores = dot(q[here], k_ext[number * BLK : (number + WIN) * BLK], 1, 1) * ROOT
        reached = jnp.logical_and(pattern_ref[0, head, block, 1] == 1, block >= 2)
        before = jnp.where(reached, scores[:, :BLK], MASKED)
        own = jnp.where(jnp.logical_and(causal, block >= 1), scores[:, BLK:], MASKED)
        first = jnp.where(jnp.logical_or(causal, block >= 1), sink_scores[here], MASKED)
        top = jnp.max(jnp.maximum(jnp.maximum(before, own), first), axis=1, keepdims=True)
        before = jnp.exp(before - top)
        own = jnp.exp(own - top)
        first = jnp.exp(first - top)
        total = jnp.sum(before + own + first, axis=1, keepdims=True)
        inverse = 1.0 / total
        window.append(jnp.concatenate([before * inverse, own * inverse], axis=1))
        sink.append(first * inverse)
    return window, jnp.concatenate(sink, axis=0)


def forward_kernel(q_ref, k_ref, v_ref, before_ref, sink_k_ref, sink_v_ref, pattern_ref, out_ref):
    rows = q_ref.shape[0]
    blocks = rows // BLK
    first_block = lax.axis_index("ctx") * blocks
    for local in range(q_ref.shape[1] // HDIM):
        cols = slice(local * HDIM, (local + 1) * HDIM)
        head = pl.program_id(0) * (q_ref.shape[1] // HDIM) + local
        k_ext = jnp.concatenate([before_ref[:BLK, cols], k_ref[:, cols]], axis=0)
        v_ext = jnp.concatenate([before_ref[BLK:, cols], v_ref[:, cols]], axis=0)
        window, sink = probabilities(
            q_ref[:, cols], k_ext, sink_k_ref[:, cols], pattern_ref, head, first_block
        )
        from_sink = dot(sink.astype(BF16), sink_v_ref[:, cols], 1, 0)
        for number in range(blocks):
            here = slice(number * BLK, (number + 1) * BLK)
            near = dot(
                window[number].astype(BF16), v_ext[number * BLK : (number + WIN) * BLK], 1, 0
            )
            out_ref[here, cols] = (near + from_sink[here]).astype(BF16)


def backward_kernel(
    q_ref,
    k_ref,
    v_ref,
    before_ref,
    sink_k_ref,
    sink_v_ref,
    pattern_ref,
    attn_ref,
    grad_ref,
    dq_ref,
    dk_ref,
    dv_ref,
    dbefore_ref,
    dsink_k_ref,
    dsink_v_ref,
):
    rows = q_ref.shape[0]
    blocks = rows // BLK
    first_block = lax.axis_index("ctx") * blocks
    for local in range(q_ref.shape[1] // HDIM):
        cols = slice(local * HDIM, (local + 1) * HDIM)
        head = pl.program_id(0) * (q_ref.shape[1] // HDIM) + local
        q = q_ref[:, cols]
        grad = grad_ref[:, cols]
        k_sink = sink_k_ref[:, cols]
        k_ext = jnp.concatenate([before_ref[:BLK, cols], k_ref[:, cols]], axis=0)
        v_ext = jnp.concatenate([before_ref[BLK:, cols], v_ref[:, cols]], axis=0)
        window, sink = probabilities(q, k_ext, k_sink, pattern_ref, head, first_block)
        delta = jnp.sum(grad.astype(F32) * attn_ref[:, cols].astype(F32), axis=1, keepdims=True)
        dprobs = dot(grad, sink_v_ref[:, cols], 1, 1)
        dscores = (sink * (dprobs - delta)).astype(BF16)
        dq_sink = dot(dscores, k_sink, 1, 0)
        dsink_k_ref[:, cols] = (dot(dscores, q, 0, 0) * ROOT).astype(dsink_k_ref.dtype)
        dsink_v_ref[:, cols] = dot(sink.astype(BF16), grad, 0, 0).astype(dsink_v_ref.dtype)
        dk_parts = [None] * (blocks + 1)
        dv_parts = [None] * (blocks + 1)
        for number in range(blocks):
            here = slice(number * BLK, (number + 1) * BLK)
            there = slice(number * BLK, (number + WIN) * BLK)
            dprobs = dot(grad[here], v_ext[there], 1, 1)
            dscores = (window[number] * (dprobs - delta[here])).astype(BF16)
            dq = dot(dscores, k_ext[there], 1, 0)
            dq_ref[here, cols] = ((dq + dq_sink[here]) * ROOT).astype(BF16)
            dk = dot(dscores, q[here], 0, 0) * ROOT
            dv = dot(window[number].astype(BF16), grad[here], 0, 0)
            for part in range(WIN):
                piece = slice(part * BLK, (part + 1) * BLK)
                at = number + part
                dk_parts[at] = dk[piece] if dk_parts[at] is None else dk_parts[at] + dk[piece]
                dv_parts[at] = dv[piece] if dv_parts[at] is None else dv_parts[at] + dv[piece]
        dbefore_ref[:BLK, cols] = dk_parts[0].astype(dbefore_ref.dtype)
        dbefore_ref[BLK:, cols] = dv_parts[0].astype(dbefore_ref.dtype)
        dk_ref[:, cols] = jnp.concatenate(dk_parts[1:], axis=0)
        dv_ref[:, cols] = jnp.concatenate(dv_parts[1:], axis=0)


def head_spec(rows):
    return pl.BlockSpec((rows, HEADS_STEP * HDIM), lambda step: (0, step))


def whole_smem(shape):
    return pl.BlockSpec(shape, lambda *_: (0,) * len(shape), memory_space=pltpu.SMEM)


def attention_specs(rows, pattern):
    return [
        head_spec(rows),
        head_spec(rows),
        head_spec(rows),
        head_spec(2 * BLK),
        head_spec(BLK),
        head_spec(BLK),
        whole_smem(pattern.shape),
    ]


def attention_forward(q, k, v, before, sink_k, sink_v, pattern):
    rows, width = q.shape
    return pl.pallas_call(
        forward_kernel,
        grid=(width // (HEADS_STEP * HDIM),),
        in_specs=attention_specs(rows, pattern),
        out_specs=head_spec(rows),
        out_shape=jax.ShapeDtypeStruct((rows, width), BF16),
        name="attention_forward",
    )(q, k, v, before, sink_k, sink_v, pattern)


def attention_backward(q, k, v, before, sink_k, sink_v, pattern, attn, grad):
    rows, width = q.shape
    shape = jax.ShapeDtypeStruct
    return pl.pallas_call(
        backward_kernel,
        grid=(width // (HEADS_STEP * HDIM),),
        in_specs=attention_specs(rows, pattern) + [head_spec(rows), head_spec(rows)],
        out_specs=[
            head_spec(rows),
            head_spec(rows),
            head_spec(rows),
            head_spec(2 * BLK),
            head_spec(BLK),
            head_spec(BLK),
        ],
        out_shape=[
            shape((rows, width), BF16),
            shape((rows, width), F32),
            shape((rows, width), F32),
            shape((2 * BLK, width), BF16),
            shape((BLK, width), F32),
            shape((BLK, width), F32),
        ],
        name="attention_backward",
    )(q, k, v, before, sink_k, sink_v, pattern, attn, grad)


def grad_attn_kernel(count, *refs):
    cot_ref, pieces, out_ref = refs[0], refs[1:-1], refs[-1]
    mine = lax.axis_index("dp")
    number = 0
    for piece in pieces:
        depth = piece.shape[1]
        for slot in range(piece.shape[0]):
            at = pl.multiple_of((mine ^ order_of(count)[number]) * depth, HDIM)
            out_ref[:, pl.ds(at, depth)] = dot(cot_ref[...], piece[slot], 1, 1).astype(BF16)
            number += 1


def projected_kernel(count, *refs):
    attn_ref, pieces, out_ref = refs[0], refs[1:-1], refs[-1]
    mine = lax.axis_index("dp")
    total, number = None, 0
    for piece in pieces:
        depth = piece.shape[1]
        for slot in range(piece.shape[0]):
            at = pl.multiple_of((mine ^ order_of(count)[number]) * depth, HDIM)
            term = dot(attn_ref[:, pl.ds(at, depth)], piece[slot], 1, 0)
            total = term if total is None else total + term
            number += 1
    out_ref[...] = total.astype(BF16)


def weight_grad_kernel(scale, pairs, *refs):
    lefts, rights, out_ref = refs[:pairs], refs[pairs : 2 * pairs], refs[-1]
    total = None
    for left, right in zip(lefts, rights):
        for slot in range(left.shape[0]):
            term = dot(left[slot], right[slot], 0, 0)
            total = term if total is None else total + term
    out_ref[0] = total * scale


def grad_attn_of(cot, pieces, count):
    rows = cot.shape[0]
    width = count * pieces[0].shape[1]
    return pl.pallas_call(
        functools.partial(grad_attn_kernel, count),
        out_shape=jax.ShapeDtypeStruct((rows, width), BF16),
        name="grad_attn",
    )(cot, *pieces)


def projected_of(attn, pieces, count):
    return pl.pallas_call(
        functools.partial(projected_kernel, count),
        out_shape=jax.ShapeDtypeStruct((attn.shape[0], pieces[0].shape[2]), BF16),
        name="projected",
    )(attn, *pieces)


def weight_grad_of(attn_pieces, cot_pieces, scale, count):
    features = attn_pieces[0].shape[2]
    wanted = cot_pieces[0].shape[2] // count
    columns = max(wanted, HDIM)
    chunks = cot_pieces[0].shape[2] // columns
    terms = pl.pallas_call(
        functools.partial(weight_grad_kernel, scale, len(attn_pieces)),
        grid=(chunks,),
        in_specs=[pl.BlockSpec(a.shape, lambda step: (0, 0, 0)) for a in attn_pieces]
        + [pl.BlockSpec(c.shape[:2] + (columns,), lambda step: (0, 0, step)) for c in cot_pieces],
        out_specs=pl.BlockSpec((1, features, columns), lambda step: (step, 0, 0)),
        out_shape=jax.ShapeDtypeStruct((chunks, features, columns), F32),
        name="weight_grad",
    )(*attn_pieces, *cot_pieces)
    if columns == wanted:
        return terms
    terms = terms.reshape(chunks, features, columns // wanted, wanted)
    return jnp.swapaxes(terms, 1, 2).reshape(count, features, wanted)


def bits_of(count):
    return [1 << place for place in range(count.bit_length() - 1)]


def order_of(count):
    order = [0]
    for bit in reversed(bits_of(count)):
        order += [one ^ bit for one in order]
    return order


def swap(value, axis, count, bit):
    return lax.ppermute(value, axis, [(one, one ^ bit) for one in range(count)])


def gather_pieces(value, axis, count):
    pieces = [value[None]]
    for bit in reversed(bits_of(count)):
        held = pieces[0] if len(pieces) == 1 else jnp.concatenate(pieces, axis=0)
        pieces.append(swap(held, axis, count, bit))
    return pieces


def exchange_columns(value, axis, count):
    mine = lax.axis_index(axis)
    columns = value.shape[1] // count
    pieces = [value[None]]
    for bit in reversed(bits_of(count)):
        half = bit * columns
        upper = (mine & bit) != 0
        keep = jnp.where(upper, half, 0)
        away = half - keep
        held = pieces[0] if len(pieces) == 1 else jnp.concatenate(pieces, axis=0)
        got = swap(lax.dynamic_slice_in_dim(held, away, half, 2), axis, count, bit)
        pieces = [lax.dynamic_slice_in_dim(one, keep, half, 2) for one in pieces] + [got]
    return pieces


def spread_first(value, axis, count, order):
    mine = lax.axis_index(axis)
    covered = 0
    for bit in order:
        pairs = [(one, one | bit) for one in range(count) if one & ~covered == 0]
        got = lax.ppermute(value, axis, pairs)
        value = jnp.where((mine & bit) != 0, got, value)
        covered |= bit
    return value


def sum_to_first(value, axis, count, order):
    done = 0
    for bit in order:
        pairs = [(one, one ^ bit) for one in range(count) if one & bit and one & done == 0]
        value = value + lax.ppermute(value.astype(BF16), axis, pairs).astype(F32)
        done |= bit
    return value


def sum_scatter(value, axis, count):
    mine = lax.axis_index(axis)
    bits = bits_of(count)
    value = value.reshape((2,) * len(bits) + value.shape[1:])
    for place, bit in enumerate(bits):
        dim = len(bits) - 1 - place
        here = jnp.where((mine & bit) != 0, 1, 0)
        away = lax.dynamic_index_in_dim(value, 1 - here, dim, keepdims=False)
        got = swap(away.astype(BF16), axis, count, bit)
        value = lax.dynamic_index_in_dim(value, here, dim, keepdims=False) + got.astype(F32)
    return value


def body(context_count, document_count, queries, keys, values, cotangent, proj_weight, pattern):
    q, k, v, cot = queries[0], keys[0], values[0], cotangent[0]
    rows, width = q.shape
    context = lax.axis_index("ctx")
    ctx_bits = bits_of(context_count)
    far_first = ctx_bits[:0:-1]

    last = jnp.concatenate([k[rows - BLK :], v[rows - BLK :]], axis=0)
    before = lax.ppermute(last, "ctx", [(one, one + 1) for one in range(context_count - 1)])
    sink_k = spread_first(k[:BLK], "ctx", context_count, ctx_bits[:1] + far_first)
    sink_v = spread_first(v[:BLK], "ctx", context_count, far_first + ctx_bits[:1])
    weights = gather_pieces(proj_weight, "dp", document_count)
    cots = gather_pieces(cot, "dp", document_count)

    grad_attn = grad_attn_of(cot, weights, document_count)
    attn = attention_forward(q, k, v, before, sink_k, sink_v, pattern)
    attns = exchange_columns(attn, "dp", document_count)
    dq, dk, dv, dbefore, dsink_k, dsink_v = attention_backward(
        q, k, v, before, sink_k, sink_v, pattern, attn, grad_attn
    )
    later = lax.ppermute(dbefore, "ctx", [(one + 1, one) for one in range(context_count - 1)])
    sink_k_sum = sum_to_first(dsink_k, "ctx", context_count, ctx_bits)
    sink_v_sum = sum_to_first(dsink_v, "ctx", context_count, ctx_bits[1:] + ctx_bits[:1])
    projected = projected_of(attn, weights, document_count)
    scale = float(rows * context_count * document_count) ** (-0.5)
    terms = weight_grad_of(attns, cots, scale, context_count)
    grad_proj = sum_scatter(terms, "ctx", context_count)

    def joined(own, back, first):
        first = jnp.where(context == 0, first, 0.0)
        head = own[:BLK] + first
        tail = own[rows - BLK :] + back.astype(F32)
        return jnp.concatenate([head, own[BLK : rows - BLK], tail], axis=0).astype(BF16)

    return (
        projected[None],
        dq[None],
        joined(dk, later[:BLK], sink_k_sum)[None],
        joined(dv, later[BLK:], sink_v_sum)[None],
        grad_proj,
    )


def solution(mesh):
    return jax.shard_map(
        functools.partial(body, mesh.shape["ctx"], mesh.shape["dp"]),
        mesh=mesh,
        in_specs=(
            P("dp", "ctx", None),
            P("dp", "ctx", None),
            P("dp", "ctx", None),
            P("dp", "ctx", None),
            P("dp", None),
            P("dp", None, None, None),
        ),
        out_specs=(
            P("dp", "ctx", None),
            P("dp", "ctx", None),
            P("dp", "ctx", None),
            P("dp", "ctx", None),
            P("dp", "ctx"),
        ),
        check_vma=False,
    )
```

time: 306 us -> 181 us (0.59)
  waiting for transfers between devices: 193 us -> 75.1 us
  Pallas kernels: 0 us -> 34.6 us
  local copies, waits for them, and re-layouts: 44.3 us -> 9.97 us
  starting transfers between devices: 12.3 us -> 41.8 us
  matrix products: 25 us -> 0 us
  between operations: 15.7 us -> 1.06 us
    reduce_scatter x2 -> x0, waiting for transfers between devices: 93 us -> none  [the longest x1 51.6 us: body(): lax.psum_scatter(partial_sum, 'ctx', scatter_dimension=1, tiled=True)]
    psum x2 -> x0, waiting for transfers between devices: 59.2 us -> none  [the longest x1 49.3 us: spread(): return lax.psum(block, axis)]
    ppermute x4 -> x23, waiting for transfers between devices: 40.3 us -> 75.1 us  [the longest x9 48 us: swap(): return lax.ppermute(value, axis, [(one, one ^ bit) for one in range(count)])]
    pallas_call x0 -> x5, Pallas kernels: none -> 34.6 us  [the longest x1 10.9 us: attention_backward(): pl.pallas_call(backward_kernel, grid=(width // (HEADS_STEP * HDIM),), in_...]
    ppermute x4 -> x23, starting transfers between devices: 11.9 us -> 41.8 us  [the longest x6 19.7 us: spread_first(): got = lax.ppermute(value, axis, pairs)]
    dot_general x15 -> x0, matrix products: 25 us -> none  [the longest x12 14.7 us: product(): return jnp.einsum(form, left, right, preferred_element_type=jnp.float32)]
    unnamed x71 -> x31, local copies, waits for them, and re-layouts: 13.7 us -> 2.32 us
    reshape x4 -> x0, local copies, waits for them, and re-layouts: 6.04 us -> none  [the longest x2 4.34 us: body(): grad_blocked = grad_attended.reshape(BLK_DEV, BLK, HEADS, HDIM)]
  transfers between devices with their start and end apart: 9 -> 23, of which waited for: 8 -> 11; matrix products, arithmetic and copies ran while one was open for 24% -> 14% of each run, Pallas kernels for 0% -> 19%
where the time goes in v1:
time: 181 us; the launch traced here: 179 us
  waiting for transfers between devices  75.1 us (41%)
  starting transfers between devices  41.8 us (23%)
  Pallas kernels  34.6 us (19%)
  other arithmetic  17 us (9%)
  local copies, waits for them, and re-layouts  9.97 us (6%)
    ppermute x9, waiting for transfers between devices, swap(): return lax.ppermute(value, axis, [(one, one ^ bit) for one in range(count)])  48 us
    ppermute x6, starting transfers between devices, spread_first(): got = lax.ppermute(value, axis, pairs)  19.7 us
    ppermute x6, waiting for transfers between devices, sum_to_first(): value = value + lax.ppermute(value.astype(BF16), axis, pairs).astype(F32)  16.3 us
    ppermute x9, starting transfers between devices, swap(): return lax.ppermute(value, axis, [(one, one ^ bit) for one in range(count)])  11.4 us
    pallas_call x1, Pallas kernels, attention_backward(): pl.pallas_call(backward_kernel, grid=(width // (HEADS_STEP * HDIM),), in_...  10.9 us
    ppermute x6, waiting for transfers between devices, spread_first(): got = lax.ppermute(value, axis, pairs)  10.7 us
    ppermute x6, starting transfers between devices, sum_to_first(): value = value + lax.ppermute(value.astype(BF16), axis, pairs).astype(F32)  7.86 us
    pallas_call x1, Pallas kernels, weight_grad_of(): pl.pallas_call(functools.partial(weight_grad_kernel, scale, len(attn_piec...  7.56 us
  transfers between devices with their start and end apart: 23, of which 11 were waited for; matrix products, arithmetic and copies ran while one was open for 14% of the time, Pallas kernels for 19%

profile of v1, /device:TPU:0, one launch (start us, length us, event | category | flops | bytes accessed | tf_op | source)
XLA Modules:
  0.0 179.4 jit_solution(9144297868229953863)
XLA Ops:
  0.7 3.1 %collective-permute-start.7 = (bf16[1,256,2048]{2,1,0:T(8,128)(2,1)}, bf16[1,256,2048]{2,1,0:T(8,128)(2,1)S(1)}, u32[]{:S(2)}, u32[]{:S(2)}) collective-permute-start(bf16[1,256,2048]{2,1,0:T(8,128)(2,1)} %bitcast.47), channel_id=1, source_target_pairs={{0,2},{1,3},{2,0},{3,1},{4,6},{5,7},{6,4},{7,5},{8,10},{9,11},{10,... | collective-permute-start | bytes 3145736 | tf_op jit(solution)/shard_map/ppermute | solution.py:276
  5.9 3.8 %collective-permute-start.1 = (bf16[128,1024]{1,0:T(8,128)(2,1)S(1)}, bf16[128,1024]{1,0:T(8,128)(2,1)S(1)}, u32[]{:S(2)}, u32[]{:S(2)}) collective-permute-start(bf16[128,1024]{1,0:T(8,128)(2,1)S(1)} %get-tuple-element.28), channel_id=1, source_target_pairs={{0,4},{1,5},{2,6},{3,7}} | collective-permute-start | bytes 786440 | tf_op jit(solution)/shard_map/ppermute | solution.py:307
  9.7 2.5 %collective-permute-start.4 = (bf16[128,1024]{1,0:T(8,128)(2,1)}, bf16[128,1024]{1,0:T(8,128)(2,1)}, u32[]{:S(2)}, u32[]{:S(2)}) collective-permute-start(bf16[128,1024]{1,0:T(8,128)(2,1)} %get-tuple-element.23), channel_id=1, source_target_pairs={{0,16},{1,17},{2,18},{3,19}} | collective-permute-start | bytes 786440 | tf_op jit(solution)/shard_map/ppermute | solution.py:307
  12.2 2.5 %collective-permute-done.1 = bf16[128,1024]{1,0:T(8,128)(2,1)S(1)} collective-permute-done((bf16[128,1024]{1,0:T(8,128)(2,1)S(1)}, bf16[128,1024]{1,0:T(8,128)(2,1)S(1)}, u32[]{:S(2)}, u32[]{:S(2)}) %collective-permute-start.1) | collective-permute-done | bytes 262176 | tf_op jit(solution)/shard_map/ppermute | solution.py:307
  16.9 11.1 %collective-permute-done.7.refs_2_ = bf16[1,256,2048]{2,1,0:T(8,128)(2,1)S(1)} collective-permute-done((bf16[1,256,2048]{2,1,0:T(8,128)(2,1)}, bf16[1,256,2048]{2,1,0:T(8,128)(2,1)S(1)}, u32[]{:S(2)}, u32[]{:S(2)}) %collective-permute-start.7) | collective-permute-done | bytes 1048608 | tf_op jit(solution)/shard_map/ppermute | solution.py:276
  29.7 19.9 %collective-permute-done.18.refs_4_ = bf16[1,256,2048]{2,1,0:T(8,128)(2,1)} collective-permute-done((bf16[1,256,2048]{2,1,0:T(8,128)(2,1)}, bf16[1,256,2048]{2,1,0:T(8,128)(2,1)}, u32[]{:S(2)}, u32[]{:S(2)}) %collective-permute-start.18) | collective-permute-done | bytes 1048608 | tf_op jit(solution)/shard_map/ppermute | solution.py:276
  49.7 2.8 %pad_maximum_fusion.1 = bf16[2,256,2048]{2,1,0:T(8,128)(2,1)} fusion(bf16[1,256,2048]{2,1,0:T(8,128)(2,1)} %collective-permute-done.18.refs_4_, bf16[1,256,2048]{2,1,0:T(8,128)(2,1)S(1)} %copy-done), kind=kLoop, calls=%fused_computation.1 | loop fusion | flops 1048576 | bytes 4194304 | tf_op jit(solution)/shard_map/concatenate | solution.py:282
  52.5 3.7 %collective-permute-start.5 = (bf16[128,1024]{1,0:T(8,128)(2,1)S(1)}, bf16[128,1024]{1,0:T(8,128)(2,1)S(1)}, u32[]{:S(2)}, u32[]{:S(2)}) collective-permute-start(bf16[128,1024]{1,0:T(8,128)(2,1)S(1)} %broadcast_select_fusion.2), channel_id=1, source_target_pairs={{0,8},{16,24},{1,9},{17,25},{2,10},{18,26},{3,11},{19,27}} | collective-permute-start | bytes 786440 | tf_op jit(solution)/shard_map/ppermute | solution.py:307
  57.7 2.8 %collective-permute-start.3 = (bf16[128,1024]{1,0:T(8,128)(2,1)S(1)}, bf16[128,1024]{1,0:T(8,128)(2,1)S(1)}, u32[]{:S(2)}, u32[]{:S(2)}) collective-permute-start(bf16[128,1024]{1,0:T(8,128)(2,1)S(1)} %broadcast_select_fusion.3), channel_id=1, source_target_pairs={{0,8},{4,12},{16,24},{20,28},{1,9},{5,13},{17,25},{21,29},{2,10},{... | collective-permute-start | bytes 786440 | tf_op jit(solution)/shard_map/ppermute | solution.py:307
  62.9 4.8 %collective-permute-start.6 = (bf16[128,1024]{1,0:T(8,128)(2,1)S(1)}, bf16[128,1024]{1,0:T(8,128)(2,1)S(1)}, u32[]{:S(2)}, u32[]{:S(2)}) collective-permute-start(bf16[128,1024]{1,0:T(8,128)(2,1)S(1)} %broadcast_select_fusion.4), channel_id=1, source_target_pairs={{0,4},{8,12},{16,20},{24,28},{1,5},{9,13},{17,21},{25,29},{2,6},{1... | collective-permute-start | bytes 786440 | tf_op jit(solution)/shard_map/ppermute | solution.py:307
  69.3 5.8 %collective-permute-done.6 = bf16[128,1024]{1,0:T(8,128)(2,1)S(1)} collective-permute-done((bf16[128,1024]{1,0:T(8,128)(2,1)S(1)}, bf16[128,1024]{1,0:T(8,128)(2,1)S(1)}, u32[]{:S(2)}, u32[]{:S(2)}) %collective-permute-start.6) | collective-permute-done | bytes 262176 | tf_op jit(solution)/shard_map/ppermute | solution.py:307
  76.6 6.7 %attention_forward.1.refs_0_.attn_ref = bf16[256,1024]{1,0:T(8,128)(2,1)} custom-call(bf16[256,1024]{1,0:T(8,128)(2,1)} %bitcast.57, bf16[256,1024]{1,0:T(8,128)(2,1)} %bitcast.51, bf16[256,1024]{1,0:T(8,128)(2,1)} %bitcast.53, bf16[256,1024]{1,0:T(8,128)(2,1)} %copy-done.8, bf16[128,1024]{1,0:T(8,128)(2,1)} %broadcast_select_fusion.5.sink_k_ref, ...), custom_call_target="tpu_custom_call" | custom-call | tf_op jit(solution)/shard_map/attention_forward/pallas_call | solution.py:153
  85.9 6.3 %collective-permute-done.16 = bf16[1,256,512]{2,1,0:T(8,128)(2,1)S(1)} collective-permute-done((bf16[1,256,512]{2,1,0:T(8,128)(2,1)S(1)}, bf16[1,256,512]{2,1,0:T(8,128)(2,1)S(1)}, u32[]{:S(2)}, u32[]{:S(2)}) %collective-permute-start.16) | collective-permute-done | bytes 262176 | tf_op jit(solution)/shard_map/ppermute | solution.py:276
  94.0 4.7 %grad_attn.1.grad_ref = bf16[256,1024]{1,0:T(8,128)(2,1)} custom-call(bf16[256,2048]{1,0:T(8,128)(2,1)} %bitcast.46, bf16[1,256,2048]{2,1,0:T(8,128)(2,1)} %bitcast.48, bf16[1,256,2048]{2,1,0:T(8,128)(2,1)} %copy-done.2, bf16[2,256,2048]{2,1,0:T(8,128)(2,1)} %collective-permute-done.8.refs_3_), custom_call_target="tpu_custom_call" | custom-call | tf_op jit(solution)/shard_map/grad_attn/pallas_call | solution.py:229
  98.7 10.9 %attention_backward.1 = (bf16[256,1024]{1,0:T(8,128)(2,1)}, f32[256,1024]{1,0:T(8,128)}, f32[256,1024]{1,0:T(8,128)}, bf16[256,1024]{1,0:T(8,128)(2,1)}, f32[128,1024]{1,0:T(8,128)}, /*index=5*/f32[128,1024]{1,0:T(8,128)}) custom-call(bf16[256,1024]{1,0:T(8,128)(2,1)} %bitcast.58, bf16[256,1024]{1,0:T(8,128)(2,1)} %bitcast.52, bf16[256,1024]{1,0:T(8,128)(2,1)} %bitcast.54, ...), custom_call_target="tpu_custom_call" | custom-call | tf_op jit(solution)/shard_map/attention_backward/pallas_call | solution.py:166
  114.1 7.6 %weight_grad.1 = f32[8,256,256]{2,1,0:T(8,128)} custom-call(bf16[1,256,256]{2,1,0:T(8,128)(2,1)} %dynamic-slice_bitcast_fusion.2.refs_0_, bf16[1,256,256]{2,1,0:T(8,128)(2,1)} %constant_dynamic-slice_fusion.2.refs_1_, bf16[2,256,256]{2,1,0:T(8,128)(2,1)} %copy-done.13, bf16[1,256,2048]{2,1,0:T(8,128)(2,1)} %refs_3_.1, ...), custom_call_target="tpu_custom_call" | custom-call | tf_op jit(solution)/shard_map/weight_grad/pallas_call | solution.py:249
  123.7 2.7 %collective-permute-start.20 = (bf16[2,2,256,256]{3,2,0,1:T(8,128)(2,1)}, bf16[2,2,256,256]{3,2,0,1:T(8,128)(2,1)}, u32[]{:S(2)}, u32[]{:S(2)}) collective-permute-start(bf16[2,2,256,256]{3,2,0,1:T(8,128)(2,1)} %fusion), channel_id=1, source_target_pairs={{0,4},{4,0},{8,12},{12,8},{16,20},{20,16},{24,28},{28,24},{1,5},{5... | collective-permute-start | bytes 1572872 | tf_op jit(solution)/shard_map/ppermute | solution.py:276
  129.8 4.8 %projected.1 = bf16[256,2048]{1,0:T(8,128)(2,1)} custom-call(bf16[256,1024]{1,0:T(8,128)(2,1)} %attention_forward.1.refs_0_.attn_ref, bf16[1,256,2048]{2,1,0:T(8,128)(2,1)} %bitcast.49, bf16[1,256,2048]{2,1,0:T(8,128)(2,1)} %copy-done.2, bf16[2,256,2048]{2,1,0:T(8,128)(2,1)} %collective-permute-done.8.refs_3_), custom_call_target="tpu_custom_call" | custom-call | tf_op jit(solution)/shard_map/projected/pallas_call | solution.py:237
  136.0 2.5 %collective-permute-done.13 = bf16[128,1024]{1,0:T(8,128)(2,1)} collective-permute-done((bf16[128,1024]{1,0:T(8,128)(2,1)}, bf16[128,1024]{1,0:T(8,128)(2,1)}, u32[]{:S(2)}, u32[]{:S(2)}) %collective-permute-start.13) | collective-permute-done | bytes 262176 | tf_op jit(solution)/shard_map/ppermute | solution.py:317
  140.8 7.2 %collective-permute-done.20 = bf16[2,2,256,256]{3,2,0,1:T(8,128)(2,1)} collective-permute-done((bf16[2,2,256,256]{3,2,0,1:T(8,128)(2,1)}, bf16[2,2,256,256]{3,2,0,1:T(8,128)(2,1)}, u32[]{:S(2)}, u32[]{:S(2)}) %collective-permute-start.20) | collective-permute-done | bytes 524320 | tf_op jit(solution)/shard_map/ppermute | solution.py:276
  149.1 3.9 %collective-permute-start.21 = (bf16[2,256,256]{2,1,0:T(8,128)(2,1)S(1)}, bf16[2,256,256]{2,1,0:T(8,128)(2,1)S(1)}, u32[]{:S(2)}, u32[]{:S(2)}) collective-permute-start(bf16[2,256,256]{2,1,0:T(8,128)(2,1)S(1)} %fusion.7), channel_id=1, source_target_pairs={{0,8},{4,12},{8,0},{12,4},{16,24},{20,28},{24,16},{28,20},{1,9},{5... | collective-permute-start | bytes 786440 | tf_op jit(solution)/shard_map/ppermute | solution.py:276
  153.0 7.9 %collective-permute-done.10 = bf16[128,1024]{1,0:T(8,128)(2,1)S(1)} collective-permute-done((bf16[128,1024]{1,0:T(8,128)(2,1)S(1)}, bf16[128,1024]{1,0:T(8,128)(2,1)S(1)}, u32[]{:S(2)}, u32[]{:S(2)}) %collective-permute-start.10) | collective-permute-done | bytes 262176 | tf_op jit(solution)/shard_map/ppermute | solution.py:317
  164.8 3.6 %collective-permute-done.21 = bf16[2,256,256]{2,1,0:T(8,128)(2,1)S(1)} collective-permute-done((bf16[2,256,256]{2,1,0:T(8,128)(2,1)S(1)}, bf16[2,256,256]{2,1,0:T(8,128)(2,1)S(1)}, u32[]{:S(2)}, u32[]{:S(2)}) %collective-permute-start.21) | collective-permute-done | bytes 262176 | tf_op jit(solution)/shard_map/ppermute | solution.py:276
  168.5 5.9 %collective-permute-done.11 = bf16[128,1024]{1,0:T(8,128)(2,1)S(1)} collective-permute-done((bf16[128,1024]{1,0:T(8,128)(2,1)S(1)}, bf16[128,1024]{1,0:T(8,128)(2,1)S(1)}, u32[]{:S(2)}, u32[]{:S(2)}) %collective-permute-start.11) | collective-permute-done | bytes 262176 | tf_op jit(solution)/shard_map/ppermute | solution.py:317
  (88 shorter events, 41.3 us)
Async XLA Ops:
  0.7 27.3 %collective-permute-start.7 = (bf16[1,256,2048]{2,1,0:T(8,128)(2,1)}, bf16[1,256,2048]{2,1,0:T(8,128)(2,1)S(1)}, u32[]{:S(2)}, u32[]{:S(2)}) collective-permute-start(bf16[1,256,2048]{2,1,0:T(8,128)(2,1)} %bitcast.47), channel_id=1, source_target_pairs={{0,2},{1,3},{2,0},{3,1},{4,6},{5,7},{6,4},{7,5},{8,10},{9,11},{10,... | collective-permute-start | bytes 3145736 | tf_op jit(solution)/shard_map/ppermute | solution.py:276
  3.7 45.9 %collective-permute-start.18 = (bf16[1,256,2048]{2,1,0:T(8,128)(2,1)}, bf16[1,256,2048]{2,1,0:T(8,128)(2,1)}, u32[]{:S(2)}, u32[]{:S(2)}) collective-permute-start(bf16[1,256,2048]{2,1,0:T(8,128)(2,1)} %refs_3_.1), channel_id=1, source_target_pairs={{0,2},{1,3},{2,0},{3,1},{4,6},{5,7},{6,4},{7,5},{8,10},{9,11},{10,... | collective-permute-start | bytes 3145736 | tf_op jit(solution)/shard_map/ppermute | solution.py:276
  5.9 8.8 %collective-permute-start.1 = (bf16[128,1024]{1,0:T(8,128)(2,1)S(1)}, bf16[128,1024]{1,0:T(8,128)(2,1)S(1)}, u32[]{:S(2)}, u32[]{:S(2)}) collective-permute-start(bf16[128,1024]{1,0:T(8,128)(2,1)S(1)} %get-tuple-element.28), channel_id=1, source_target_pairs={{0,4},{1,5},{2,6},{3,7}} | collective-permute-start | bytes 786440 | tf_op jit(solution)/shard_map/ppermute | solution.py:307
  9.7 42.8 %collective-permute-start.4 = (bf16[128,1024]{1,0:T(8,128)(2,1)}, bf16[128,1024]{1,0:T(8,128)(2,1)}, u32[]{:S(2)}, u32[]{:S(2)}) collective-permute-start(bf16[128,1024]{1,0:T(8,128)(2,1)} %get-tuple-element.23), channel_id=1, source_target_pairs={{0,16},{1,17},{2,18},{3,19}} | collective-permute-start | bytes 786440 | tf_op jit(solution)/shard_map/ppermute | solution.py:307
  14.7 34.9 %copy-start = (bf16[1,256,2048]{2,1,0:T(8,128)(2,1)S(1)}, bf16[1,256,2048]{2,1,0:T(8,128)(2,1)}, u32[]{:S(2)}) copy-start(bf16[1,256,2048]{2,1,0:T(8,128)(2,1)} %refs_3_.1) | copy-start | bytes 3145732
  14.7 42.9 %collective-permute-start.2 = (bf16[128,1024]{1,0:T(8,128)(2,1)S(1)}, bf16[128,1024]{1,0:T(8,128)(2,1)}, u32[]{:S(2)}, u32[]{:S(2)}) collective-permute-start(bf16[128,1024]{1,0:T(8,128)(2,1)S(1)} %broadcast_select_fusion.1), channel_id=1, source_target_pairs={{0,16},{4,20},{1,17},{5,21},{2,18},{6,22},{3,19},{7,23}} | collective-permute-start | bytes 786440 | tf_op jit(solution)/shard_map/ppermute | solution.py:307
  29.7 64.4 %collective-permute-start.8 = (bf16[2,256,2048]{2,1,0:T(8,128)(2,1)}, bf16[2,256,2048]{2,1,0:T(8,128)(2,1)}, u32[]{:S(2)}, u32[]{:S(2)}) collective-permute-start(bf16[2,256,2048]{2,1,0:T(8,128)(2,1)} %pad_maximum_fusion), channel_id=1, source_target_pairs={{0,1},{1,0},{2,3},{3,2},{4,5},{5,4},{6,7},{7,6},{8,9},{9,8},{10,11... | collective-permute-start | bytes 6291464 | tf_op jit(solution)/shard_map/ppermute | solution.py:276
  52.5 60.9 %collective-permute-start.19 = (bf16[2,256,2048]{2,1,0:T(8,128)(2,1)}, bf16[2,256,2048]{2,1,0:T(8,128)(2,1)}, u32[]{:S(2)}, u32[]{:S(2)}) collective-permute-start(bf16[2,256,2048]{2,1,0:T(8,128)(2,1)} %pad_maximum_fusion.1), channel_id=1, source_target_pairs={{0,1},{1,0},{2,3},{3,2},{4,5},{5,4},{6,7},{7,6},{8,9},{9,8},{10,11... | collective-permute-start | bytes 6291464 | tf_op jit(solution)/shard_map/ppermute | solution.py:276
  52.5 10.4 %collective-permute-start.5 = (bf16[128,1024]{1,0:T(8,128)(2,1)S(1)}, bf16[128,1024]{1,0:T(8,128)(2,1)S(1)}, u32[]{:S(2)}, u32[]{:S(2)}) collective-permute-start(bf16[128,1024]{1,0:T(8,128)(2,1)S(1)} %broadcast_select_fusion.2), channel_id=1, source_target_pairs={{0,8},{16,24},{1,9},{17,25},{2,10},{18,26},{3,11},{19,27}} | collective-permute-start | bytes 786440 | tf_op jit(solution)/shard_map/ppermute | solution.py:307
  56.3 19.5 %collective-permute-start = (bf16[256,1024]{1,0:T(8,128)(2,1)S(1)}, bf16[256,1024]{1,0:T(8,128)(2,1)S(1)}, u32[]{:S(2)}, u32[]{:S(2)}) collective-permute-start(bf16[256,1024]{1,0:T(8,128)(2,1)S(1)} %pad_maximum_fusion.2), channel_id=1, source_target_pairs={{0,4},{4,8},{8,12},{12,16},{16,20},{20,24},{24,28},{1,5},{5,9},{9,... | collective-permute-start | bytes 1572872 | tf_op jit(solution)/shard_map/ppermute | solution.py:343
  57.7 10.8 %collective-permute-start.3 = (bf16[128,1024]{1,0:T(8,128)(2,1)S(1)}, bf16[128,1024]{1,0:T(8,128)(2,1)S(1)}, u32[]{:S(2)}, u32[]{:S(2)}) collective-permute-start(bf16[128,1024]{1,0:T(8,128)(2,1)S(1)} %broadcast_select_fusion.3), channel_id=1, source_target_pairs={{0,8},{4,12},{16,24},{20,28},{1,9},{5,13},{17,25},{21,29},{2,10},{... | collective-permute-start | bytes 786440 | tf_op jit(solution)/shard_map/ppermute | solution.py:307
  62.9 12.1 %collective-permute-start.6 = (bf16[128,1024]{1,0:T(8,128)(2,1)S(1)}, bf16[128,1024]{1,0:T(8,128)(2,1)S(1)}, u32[]{:S(2)}, u32[]{:S(2)}) collective-permute-start(bf16[128,1024]{1,0:T(8,128)(2,1)S(1)} %broadcast_select_fusion.4), channel_id=1, source_target_pairs={{0,4},{8,12},{16,20},{24,28},{1,5},{9,13},{17,21},{25,29},{2,6},{1... | collective-permute-start | bytes 786440 | tf_op jit(solution)/shard_map/ppermute | solution.py:307
  84.3 7.9 %collective-permute-start.16 = (bf16[1,256,512]{2,1,0:T(8,128)(2,1)S(1)}, bf16[1,256,512]{2,1,0:T(8,128)(2,1)S(1)}, u32[]{:S(2)}, u32[]{:S(2)}) collective-permute-start(bf16[1,256,512]{2,1,0:T(8,128)(2,1)S(1)} %get-tuple-element.22), channel_id=1, source_target_pairs={{0,2},{1,3},{2,0},{3,1},{4,6},{5,7},{6,4},{7,5},{8,10},{9,11},{10,... | collective-permute-start | bytes 786440 | tf_op jit(solution)/shard_map/ppermute | solution.py:276
  92.2 21.1 %collective-permute-start.17 = (bf16[2,256,256]{2,1,0:T(8,128)(2,1)S(1)}, bf16[2,256,256]{2,1,0:T(8,128)(2,1)S(1)}, u32[]{:S(2)}, u32[]{:S(2)}) collective-permute-start(bf16[2,256,256]{2,1,0:T(8,128)(2,1)S(1)} %fusion.8), channel_id=1, source_target_pairs={{0,1},{1,0},{2,3},{3,2},{4,5},{5,4},{6,7},{7,6},{8,9},{9,8},{10,11... | collective-permute-start | bytes 786440 | tf_op jit(solution)/shard_map/ppermute | solution.py:276
  111.4 23.2 %collective-permute-start.9 = (bf16[128,1024]{1,0:T(8,128)(2,1)}, bf16[128,1024]{1,0:T(8,128)(2,1)S(1)}, u32[]{:S(2)}, u32[]{:S(2)}) collective-permute-start(bf16[128,1024]{1,0:T(8,128)(2,1)} %convert_element_type.85), channel_id=1, source_target_pairs={{4,0},{12,8},{20,16},{28,24},{5,1},{13,9},{21,17},{29,25},{6,2},{1... | collective-permute-start | bytes 786440 | tf_op jit(solution)/shard_map/ppermute | solution.py:317
  123.7 24.2 %collective-permute-start.20 = (bf16[2,2,256,256]{3,2,0,1:T(8,128)(2,1)}, bf16[2,2,256,256]{3,2,0,1:T(8,128)(2,1)}, u32[]{:S(2)}, u32[]{:S(2)}) collective-permute-start(bf16[2,2,256,256]{3,2,0,1:T(8,128)(2,1)} %fusion), channel_id=1, source_target_pairs={{0,4},{4,0},{8,12},{12,8},{16,20},{20,16},{24,28},{28,24},{1,5},{5... | collective-permute-start | bytes 1572872 | tf_op jit(solution)/shard_map/ppermute | solution.py:276
  127.1 11.4 %collective-permute-start.13 = (bf16[128,1024]{1,0:T(8,128)(2,1)}, bf16[128,1024]{1,0:T(8,128)(2,1)}, u32[]{:S(2)}, u32[]{:S(2)}) collective-permute-start(bf16[128,1024]{1,0:T(8,128)(2,1)} %convert_element_type.92), channel_id=1, source_target_pairs={{8,0},{12,4},{24,16},{28,20},{9,1},{13,5},{25,17},{29,21},{10,2},{... | collective-permute-start | bytes 786440 | tf_op jit(solution)/shard_map/ppermute | solution.py:317
  128.4 40.1 %collective-permute-start.12 = (bf16[256,1024]{1,0:T(8,128)(2,1)}, bf16[256,1024]{1,0:T(8,128)(2,1)}, u32[]{:S(2)}, u32[]{:S(2)}) collective-permute-start(bf16[256,1024]{1,0:T(8,128)(2,1)} %get-tuple-element.14), channel_id=1, source_target_pairs={{4,0},{8,4},{12,8},{16,12},{20,16},{24,20},{28,24},{5,1},{9,5},{13... | collective-permute-start | bytes 1572872 | tf_op jit(solution)/shard_map/ppermute | solution.py:355
  134.7 26.2 %collective-permute-start.10 = (bf16[128,1024]{1,0:T(8,128)(2,1)S(1)}, bf16[128,1024]{1,0:T(8,128)(2,1)S(1)}, u32[]{:S(2)}, u32[]{:S(2)}) collective-permute-start(bf16[128,1024]{1,0:T(8,128)(2,1)S(1)} %fusion.1), channel_id=1, source_target_pairs={{8,0},{24,16},{9,1},{25,17},{10,2},{26,18},{11,3},{27,19}} | collective-permute-start | bytes 786440 | tf_op jit(solution)/shard_map/ppermute | solution.py:317
  139.5 22.8 %collective-permute-start.14 = (bf16[128,1024]{1,0:T(8,128)(2,1)S(1)}, bf16[128,1024]{1,0:T(8,128)(2,1)S(1)}, u32[]{:S(2)}, u32[]{:S(2)}) collective-permute-start(bf16[128,1024]{1,0:T(8,128)(2,1)S(1)} %fusion.2), channel_id=1, source_target_pairs={{16,0},{20,4},{17,1},{21,5},{18,2},{22,6},{19,3},{23,7}} | collective-permute-start | bytes 786440 | tf_op jit(solution)/shard_map/ppermute | solution.py:317
  149.1 19.2 %collective-permute-start.21 = (bf16[2,256,256]{2,1,0:T(8,128)(2,1)S(1)}, bf16[2,256,256]{2,1,0:T(8,128)(2,1)S(1)}, u32[]{:S(2)}, u32[]{:S(2)}) collective-permute-start(bf16[2,256,256]{2,1,0:T(8,128)(2,1)S(1)} %fusion.7), channel_id=1, source_target_pairs={{0,8},{4,12},{8,0},{12,4},{16,24},{20,28},{24,16},{28,20},{1,9},{5... | collective-permute-start | bytes 786440 | tf_op jit(solution)/shard_map/ppermute | solution.py:276
  161.0 13.5 %collective-permute-start.11 = (bf16[128,1024]{1,0:T(8,128)(2,1)S(1)}, bf16[128,1024]{1,0:T(8,128)(2,1)S(1)}, u32[]{:S(2)}, u32[]{:S(2)}) collective-permute-start(bf16[128,1024]{1,0:T(8,128)(2,1)S(1)} %fusion.9), channel_id=1, source_target_pairs={{16,0},{17,1},{18,2},{19,3}} | collective-permute-start | bytes 786440 | tf_op jit(solution)/shard_map/ppermute | solution.py:317
  163.4 12.4 %collective-permute-start.15 = (bf16[128,1024]{1,0:T(8,128)(2,1)S(1)}, bf16[128,1024]{1,0:T(8,128)(2,1)S(1)}, u32[]{:S(2)}, u32[]{:S(2)}) collective-permute-start(bf16[128,1024]{1,0:T(8,128)(2,1)S(1)} %fusion.10), channel_id=1, source_target_pairs={{4,0},{5,1},{6,2},{7,3}} | collective-permute-start | bytes 786440 | tf_op jit(solution)/shard_map/ppermute | solution.py:317
  168.5 10.3 %collective-permute-start.22 = (bf16[256,256]{1,0:T(8,128)(2,1)S(1)}, bf16[256,256]{1,0:T(8,128)(2,1)S(1)}, u32[]{:S(2)}, u32[]{:S(2)}) collective-permute-start(bf16[256,256]{1,0:T(8,128)(2,1)S(1)} %fusion.11), channel_id=1, source_target_pairs={{0,16},{4,20},{8,24},{12,28},{16,0},{20,4},{24,8},{28,12},{1,17},{... | collective-permute-start | bytes 393224 | tf_op jit(solution)/shard_map/ppermute | solution.py:276
  (14 other events, 210.9 us)

commit v2 on v1

--- a/solution.py
+++ b/solution.py
@@ -7,8 +7,10 @@
 from jax.experimental.pallas import tpu as pltpu
 from jax.sharding import PartitionSpec as P
 
+
 HDIM = 128
 BLK = 128
+
 WIN = 2
 HEADS_STEP = 2
 
@@ -50,7 +52,18 @@
     return window, jnp.concatenate(sink, axis=0)
 
 
-def forward_kernel(q_ref, k_ref, v_ref, before_ref, sink_k_ref, sink_v_ref, pattern_ref, out_ref):
+def forward_kernel(
+    count,
+    q_ref,
+    k_ref,
+    v_ref,
+    before_ref,
+    sink_k_ref,
+    sink_v_ref,
+    pattern_ref,
+    out_ref,
+    *away_refs,
+):
     rows = q_ref.shape[0]
     blocks = rows // BLK
     first_block = lax.axis_index("ctx") * blocks
@@ -68,7 +81,16 @@
             near = dot(
                 window[number].astype(BF16), v_ext[number * BLK : (number + WIN) * BLK], 1, 0
             )
-            out_ref[here, cols] = (near + from_sink[here]).astype(BF16)
+            at = pl.multiple_of(head * HDIM, HDIM)
+            out_ref[here, pl.ds(at, HDIM)] = (near + from_sink[here]).astype(BF16)
+
+    @pl.when(pl.program_id(0) == pl.num_programs(0) - 1)
+    def _():
+        mine = lax.axis_index("dp")
+        columns = out_ref.shape[1] // count
+        for bit, away_ref in zip(reversed(bits_of(count)), away_refs):
+            at = pl.multiple_of(((mine ^ bit) & ~(bit - 1)) * columns, HDIM)
+            away_ref[0] = out_ref[:, pl.ds(at, bit * columns)]
 
 
 def backward_kernel(
@@ -85,8 +107,8 @@
     dk_ref,
     dv_ref,
     dbefore_ref,
-    dsink_k_ref,
-    dsink_v_ref,
+    kept_ref,
+    sent_ref,
 ):
     rows = q_ref.shape[0]
     blocks = rows // BLK
@@ -104,8 +126,11 @@
         dprobs = dot(grad, sink_v_ref[:, cols], 1, 1)
         dscores = (sink * (dprobs - delta)).astype(BF16)
         dq_sink = dot(dscores, k_sink, 1, 0)
-        dsink_k_ref[:, cols] = (dot(dscores, q, 0, 0) * ROOT).astype(dsink_k_ref.dtype)
-        dsink_v_ref[:, cols] = dot(sink.astype(BF16), grad, 0, 0).astype(dsink_v_ref.dtype)
+        dsink_k = dot(dscores, q, 0, 0) * ROOT
+        dsink_v = dot(sink.astype(BF16), grad, 0, 0)
+        odd = (lax.axis_index("ctx") & 1) != 0
+        kept_ref[:, cols] = jnp.where(odd, dsink_v, dsink_k)
+        sent_ref[:, cols] = jnp.where(odd, dsink_k, dsink_v).astype(BF16)
         dk_parts = [None] * (blocks + 1)
         dv_parts = [None] * (blocks + 1)
         for number in range(blocks):
@@ -148,14 +173,21 @@
     ]
 
 
-def attention_forward(q, k, v, before, sink_k, sink_v, pattern):
+def attention_forward(count, q, k, v, before, sink_k, sink_v, pattern):
     rows, width = q.shape
+    away = [bit * width // count for bit in reversed(bits_of(count))]
     return pl.pallas_call(
-        forward_kernel,
+        functools.partial(forward_kernel, count),
         grid=(width // (HEADS_STEP * HDIM),),
         in_specs=attention_specs(rows, pattern),
-        out_specs=head_spec(rows),
-        out_shape=jax.ShapeDtypeStruct((rows, width), BF16),
+        out_specs=[
+            pl.BlockSpec((rows, width), lambda step: (0, 0)),
+            *(pl.BlockSpec((1, rows, one), lambda step: (0, 0, 0)) for one in away),
+        ],
+        out_shape=[
+            jax.ShapeDtypeStruct((rows, width), BF16),
+            *(jax.ShapeDtypeStruct((1, rows, one), BF16) for one in away),
+        ],
         name="attention_forward",
     )(q, k, v, before, sink_k, sink_v, pattern)
 
@@ -181,7 +213,7 @@
             shape((rows, width), F32),
             shape((2 * BLK, width), BF16),
             shape((BLK, width), F32),
-            shape((BLK, width), F32),
+            shape((BLK, width), BF16),
         ],
         name="attention_backward",
     )(q, k, v, before, sink_k, sink_v, pattern, attn, grad)
@@ -214,11 +246,44 @@
 
 
 def weight_grad_kernel(scale, pairs, *refs):
+    lefts, rights = refs[:pairs], refs[pairs : 2 * pairs]
+    keep_ref, away_ref, left_scr = refs[2 * pairs :]
+    mine = lax.axis_index("dp")
+    features = left_scr.shape[0]
+    rows = lefts[0].shape[-2]
+
+    @pl.when(pl.program_id(0) == 0)
+    def _():
+        number = 0
+        for left in lefts:
+            shared = left.shape[-1] // features
+            at = pl.multiple_of((mine & (shared - 1)) * features, HDIM)
+            for slot in range(left.shape[0]):
+                left_scr[:, number * rows : (number + 1) * rows] = left[
+                    slot, :, pl.ds(at, features)
+                ].T
+                number += 1
+
+    columns = keep_ref.shape[2]
+    upper = (lax.axis_index("ctx") & 1) != 0
+    for out_ref, here in ((away_ref, jnp.where(upper, 0, columns)), (keep_ref, jnp.where(upper, columns, 0))):
+        here = pl.multiple_of(here, HDIM)
+        right = jnp.concatenate(
+            [one[slot, :, pl.ds(here, columns)] for one in rights for slot in range(one.shape[0])],
+            axis=0,
+        )
+        out_ref[0] = (dot(left_scr[...], right, 1, 0) * scale).astype(out_ref.dtype)
+
+
+def plain_weight_grad_kernel(scale, pairs, *refs):
     lefts, rights, out_ref = refs[:pairs], refs[pairs : 2 * pairs], refs[-1]
+    mine = lax.axis_index("dp")
+    features = out_ref.shape[1]
     total = None
     for left, right in zip(lefts, rights):
+        at = pl.multiple_of((mine & (left.shape[-1] // features - 1)) * features, HDIM)
         for slot in range(left.shape[0]):
-            term = dot(left[slot], right[slot], 0, 0)
+            term = dot(left[slot, :, pl.ds(at, features)], right[slot], 0, 0)
             total = term if total is None else total + term
     out_ref[0] = total * scale
 
@@ -241,13 +306,40 @@
     )(attn, *pieces)
 
 
-def weight_grad_of(attn_pieces, cot_pieces, scale, count):
-    features = attn_pieces[0].shape[2]
+def weight_grad_of(attn_pieces, cot_pieces, scale, document_count, count):
+    features = attn_pieces[0].shape[2] // document_count
     wanted = cot_pieces[0].shape[2] // count
-    columns = max(wanted, HDIM)
+    if wanted % HDIM:
+        return plain_weight_grad_of(attn_pieces, cot_pieces, scale, document_count, count)
+    rows = attn_pieces[0].shape[1]
+    places = len(bits_of(count)) - 1
+
+    def reversed_bits(step):
+        return sum(((step >> place) & 1) << (places - 1 - place) for place in range(places))
+
+    out = pl.BlockSpec((1, features, wanted), lambda step: (reversed_bits(step), 0, 0))
+    return pl.pallas_call(
+        functools.partial(weight_grad_kernel, scale, len(attn_pieces)),
+        grid=(count // 2,),
+        in_specs=[pl.BlockSpec(a.shape, lambda step: (0, 0, 0)) for a in attn_pieces]
+        + [pl.BlockSpec(c.shape[:2] + (2 * wanted,), lambda step: (0, 0, step)) for c in cot_pieces],
+        out_specs=[out, out],
+        out_shape=[
+            jax.ShapeDtypeStruct((count // 2, features, wanted), F32),
+            jax.ShapeDtypeStruct((count // 2, features, wanted), BF16),
+        ],
+        scratch_shapes=[pltpu.VMEM((features, document_count * rows), BF16)],
+        name="weight_grad",
+    )(*attn_pieces, *cot_pieces)
+
+
+def plain_weight_grad_of(attn_pieces, cot_pieces, scale, document_count, count):
+    features = attn_pieces[0].shape[2] // document_count
+    wanted = cot_pieces[0].shape[2] // count
+    columns = HDIM
     chunks = cot_pieces[0].shape[2] // columns
     terms = pl.pallas_call(
-        functools.partial(weight_grad_kernel, scale, len(attn_pieces)),
+        functools.partial(plain_weight_grad_kernel, scale, len(attn_pieces)),
         grid=(chunks,),
         in_specs=[pl.BlockSpec(a.shape, lambda step: (0, 0, 0)) for a in attn_pieces]
         + [pl.BlockSpec(c.shape[:2] + (columns,), lambda step: (0, 0, step)) for c in cot_pieces],
@@ -255,10 +347,49 @@
         out_shape=jax.ShapeDtypeStruct((chunks, features, columns), F32),
         name="weight_grad",
     )(*attn_pieces, *cot_pieces)
-    if columns == wanted:
-        return terms
     terms = terms.reshape(chunks, features, columns // wanted, wanted)
-    return jnp.swapaxes(terms, 1, 2).reshape(count, features, wanted)
+    places = len(bits_of(count))
+    terms = jnp.swapaxes(terms, 1, 2).reshape((2,) * places + (features, wanted))
+    terms = terms.transpose(tuple(reversed(range(places))) + (places, places + 1))
+    terms = terms.reshape(2, count // 2, features, wanted)
+    here = lax.axis_index("ctx") & 1
+    keep = lax.dynamic_index_in_dim(terms, here, 0, keepdims=False)
+    return keep, lax.dynamic_index_in_dim(terms, 1 - here, 0, keepdims=False).astype(BF16)
+
+
+def joined_kernel(dk_ref, dv_ref, later_ref, out_k_ref, out_v_ref):
+    rows = dk_ref.shape[0]
+    for own, out, at in ((dk_ref, out_k_ref, 0), (dv_ref, out_v_ref, BLK)):
+        out[: rows - BLK] = own[: rows - BLK].astype(BF16)
+        out[rows - BLK :] = (own[rows - BLK :] + later_ref[at : at + BLK].astype(F32)).astype(BF16)
+
+
+def joined(dk, dv, later):
+    shape = jax.ShapeDtypeStruct(dk.shape, BF16)
+    return pl.pallas_call(joined_kernel, out_shape=[shape, shape], name="joined")(dk, dv, later)
+
+
+def finish_kernel(part_k_ref, part_v_ref, own_k_ref, own_v_ref, total_ref, got_ref, out_k_ref, out_v_ref):
+    del part_k_ref, part_v_ref
+    first = lax.axis_index("ctx") == 0
+    out_k_ref[...] = (own_k_ref[...] + jnp.where(first, total_ref[...], 0.0)).astype(BF16)
+    out_v_ref[...] = (own_v_ref[...] + jnp.where(first, got_ref[...].astype(F32), 0.0)).astype(BF16)
+
+
+def finish(part_k, part_v, own_k, own_v, total, got):
+    width = own_k.shape[1]
+    block = pl.BlockSpec((BLK, width), lambda step: (0, 0))
+    whole = pl.BlockSpec(memory_space=pl.ANY)
+    shape = jax.ShapeDtypeStruct(part_k.shape, BF16)
+    return pl.pallas_call(
+        finish_kernel,
+        grid=(1,),
+        in_specs=[whole, whole, block, block, block, block],
+        out_specs=[block, block],
+        out_shape=[shape, shape],
+        input_output_aliases={0: 0, 1: 1},
+        name="finish",
+    )(part_k, part_v, own_k, own_v, total, got)
 
 
 def bits_of(count):
@@ -276,26 +407,13 @@
     return lax.ppermute(value, axis, [(one, one ^ bit) for one in range(count)])
 
 
-def gather_pieces(value, axis, count):
+def gather_pieces(value, axis, count, away=None):
     pieces = [value[None]]
-    for bit in reversed(bits_of(count)):
-        held = pieces[0] if len(pieces) == 1 else jnp.concatenate(pieces, axis=0)
-        pieces.append(swap(held, axis, count, bit))
-    return pieces
-
-
-def exchange_columns(value, axis, count):
-    mine = lax.axis_index(axis)
-    columns = value.shape[1] // count
-    pieces = [value[None]]
-    for bit in reversed(bits_of(count)):
-        half = bit * columns
-        upper = (mine & bit) != 0
-        keep = jnp.where(upper, half, 0)
-        away = half - keep
-        held = pieces[0] if len(pieces) == 1 else jnp.concatenate(pieces, axis=0)
-        got = swap(lax.dynamic_slice_in_dim(held, away, half, 2), axis, count, bit)
-        pieces = [lax.dynamic_slice_in_dim(one, keep, half, 2) for one in pieces] + [got]
+    for place, bit in enumerate(reversed(bits_of(count))):
+        got = []
+        for number, one in enumerate(pieces):
+            got.append(swap(away[place] if away and not number else one, axis, count, bit))
+        pieces += got
     return pieces
 
 
@@ -310,74 +428,66 @@
     return value
 
 
-def sum_to_first(value, axis, count, order):
+def sum_to_first(kept, sent, axis, count):
+    bits = bits_of(count)
+    kept = kept + swap(sent, axis, count, 1).astype(F32)
     done = 0
-    for bit in order:
+    for bit in bits[1:]:
         pairs = [(one, one ^ bit) for one in range(count) if one & bit and one & done == 0]
-        value = value + lax.ppermute(value.astype(BF16), axis, pairs).astype(F32)
+        kept = kept + lax.ppermute(kept.astype(BF16), axis, pairs).astype(F32)
         done |= bit
-    return value
-
-
-def sum_scatter(value, axis, count):
+    return kept, lax.ppermute(kept.astype(BF16), axis, [(1, 0)])
+
+
+def sum_scatter(keep, away, axis, count):
     mine = lax.axis_index(axis)
     bits = bits_of(count)
-    value = value.reshape((2,) * len(bits) + value.shape[1:])
+    keep = keep.reshape((2,) * (len(bits) - 1) + keep.shape[1:])
+    away = away.reshape(keep.shape)
     for place, bit in enumerate(bits):
-        dim = len(bits) - 1 - place
-        here = jnp.where((mine & bit) != 0, 1, 0)
-        away = lax.dynamic_index_in_dim(value, 1 - here, dim, keepdims=False)
-        got = swap(away.astype(BF16), axis, count, bit)
-        value = lax.dynamic_index_in_dim(value, here, dim, keepdims=False) + got.astype(F32)
-    return value
+        if place:
+            here = jnp.where((mine & bit) != 0, 1, 0)
+            away = lax.dynamic_index_in_dim(keep, 1 - here, 0, keepdims=False).astype(BF16)
+            keep = lax.dynamic_index_in_dim(keep, here, 0, keepdims=False)
+        keep = keep + swap(away, axis, count, bit).astype(F32)
+    return keep
 
 
 def body(context_count, document_count, queries, keys, values, cotangent, proj_weight, pattern):
     q, k, v, cot = queries[0], keys[0], values[0], cotangent[0]
-    rows, width = q.shape
-    context = lax.axis_index("ctx")
-    ctx_bits = bits_of(context_count)
-    far_first = ctx_bits[:0:-1]
+    rows, _ = q.shape
+    bits = bits_of(context_count)
+    far_first = bits[:0:-1]
 
     last = jnp.concatenate([k[rows - BLK :], v[rows - BLK :]], axis=0)
     before = lax.ppermute(last, "ctx", [(one, one + 1) for one in range(context_count - 1)])
-    sink_k = spread_first(k[:BLK], "ctx", context_count, ctx_bits[:1] + far_first)
-    sink_v = spread_first(v[:BLK], "ctx", context_count, far_first + ctx_bits[:1])
+    sink_k = spread_first(k[:BLK], "ctx", context_count, bits[:1] + far_first)
+    sink_v = spread_first(v[:BLK], "ctx", context_count, far_first + bits[:1])
     weights = gather_pieces(proj_weight, "dp", document_count)
     cots = gather_pieces(cot, "dp", document_count)
-
     grad_attn = grad_attn_of(cot, weights, document_count)
-    attn = attention_forward(q, k, v, before, sink_k, sink_v, pattern)
-    attns = exchange_columns(attn, "dp", document_count)
-    dq, dk, dv, dbefore, dsink_k, dsink_v = attention_backward(
+    attn, *away = attention_forward(
+        document_count, q, k, v, before, sink_k, sink_v, pattern
+    )
+    attns = gather_pieces(attn, "dp", document_count, away)
+    dq, dk, dv, dbefore, kept, sent = attention_backward(
         q, k, v, before, sink_k, sink_v, pattern, attn, grad_attn
     )
     later = lax.ppermute(dbefore, "ctx", [(one + 1, one) for one in range(context_count - 1)])
-    sink_k_sum = sum_to_first(dsink_k, "ctx", context_count, ctx_bits)
-    sink_v_sum = sum_to_first(dsink_v, "ctx", context_count, ctx_bits[1:] + ctx_bits[:1])
+    total, got = sum_to_first(kept, sent, "ctx", context_count)
     projected = projected_of(attn, weights, document_count)
     scale = float(rows * context_count * document_count) ** (-0.5)
-    terms = weight_grad_of(attns, cots, scale, context_count)
-    grad_proj = sum_scatter(terms, "ctx", context_count)
-
-    def joined(own, back, first):
-        first = jnp.where(context == 0, first, 0.0)
-        head = own[:BLK] + first
-        tail = own[rows - BLK :] + back.astype(F32)
-        return jnp.concatenate([head, own[BLK : rows - BLK], tail], axis=0).astype(BF16)
-
-    return (
-        projected[None],
-        dq[None],
-        joined(dk, later[:BLK], sink_k_sum)[None],
-        joined(dv, later[BLK:], sink_v_sum)[None],
-        grad_proj,
-    )
+    keep, send = weight_grad_of(attns, cots, scale, document_count, context_count)
+    grad_proj = sum_scatter(keep, send, "ctx", context_count)
+    grad_k, grad_v = joined(dk, dv, later)
+    grad_k, grad_v = finish(grad_k, grad_v, dk, dv, total, got)
+    return projected[None], dq[None], grad_k[None], grad_v[None], grad_proj
 
 
 def solution(mesh):
+    sizes = mesh.shape["ctx"], mesh.shape["dp"]
     return jax.shard_map(
-        functools.partial(body, mesh.shape["ctx"], mesh.shape["dp"]),
+        functools.partial(body, *sizes),
         mesh=mesh,
         in_specs=(
             P("dp", "ctx", None),

time: 181 us -> 156 us (0.86)
  starting transfers between devices: 41.8 us -> 31.2 us
  other arithmetic: 17 us -> 8.16 us
  local copies, waits for them, and re-layouts: 9.97 us -> 6.23 us
  waiting for transfers between devices: 75.1 us -> 71.7 us
  Pallas kernels: 34.6 us -> 37.5 us
    concatenate x7 -> x0, other arithmetic: 8.72 us -> none  [the longest x2 4.5 us: gather_pieces(): held = pieces[0] if len(pieces) == 1 else jnp.concatenate(pieces, axis=0)]
    ppermute x9 -> x13, waiting for transfers between devices: 48 us -> 40.8 us  [swap(): return lax.ppermute(value, axis, [(one, one ^ bit) for one in range(count)])]
    ppermute x6, starting transfers between devices: 19.7 us -> 14.2 us  [spread_first(): got = lax.ppermute(value, axis, pairs)]
    pallas_call x1 -> x3, Pallas kernels: 6.67 us -> 11.9 us  [the longest x1 6.93 us: attention_forward(): pl.pallas_call(functools.partial(forward_kernel, count), grid=(width // (...]
    ppermute x6 -> x3, starting transfers between devices: 7.86 us -> 3.86 us  [the longest x2 2.58 us: sum_to_first(): kept = kept + lax.ppermute(kept.astype(BF16), axis, pairs).astype(F32)]
    dynamic_slice x3 -> x0, local copies, waits for them, and re-layouts: 3.44 us -> none  [exchange_columns(): lax.dynamic_slice_in_dim(one, keep, half, 2)]
    convert_element_type x6 -> x3, other arithmetic: 4.73 us -> 2.13 us  [the longest x2 1.19 us: sum_to_first(): kept = kept + lax.ppermute(kept.astype(BF16), axis, pairs).astype(F32)]
    convert_element_type x3 -> x2, local copies, waits for them, and re-layouts: 2.13 us -> 0.06 us  [sum_scatter(): lax.dynamic_index_in_dim(keep, 1 - here, 0, keepdims=False).astype(BF16)]
  transfers between devices with their start and end apart: 23 -> 24, of which waited for: 11 -> 13; matrix products, arithmetic and copies ran while one was open for 14% -> 6% of each run, Pallas kernels for 19% -> 23%
where the time goes in v2:
time: 156 us
  waiting for transfers between devices  71.7 us (46%)
  Pallas kernels  37.5 us (24%)
  starting transfers between devices  31.2 us (20%)
  other arithmetic  8.16 us (5%)
  local copies, waits for them, and re-layouts  6.23 us (4%)
    ppermute x13, waiting for transfers between devices, swap(): return lax.ppermute(value, axis, [(one, one ^ bit) for one in range(count)])  40.8 us
    ppermute x2, waiting for transfers between devices, sum_to_first(): kept = kept + lax.ppermute(kept.astype(BF16), axis, pairs).astype(F32)  18.1 us
    ppermute x6, starting transfers between devices, spread_first(): got = lax.ppermute(value, axis, pairs)  14.2 us
    ppermute x6, waiting for transfers between devices, spread_first(): got = lax.ppermute(value, axis, pairs)  12.8 us
    pallas_call x1, Pallas kernels, attention_backward(): pl.pallas_call(backward_kernel, grid=(width // (HEADS_STEP * HDIM),), in_...  10.9 us
    ppermute x13, starting transfers between devices, swap(): return lax.ppermute(value, axis, [(one, one ^ bit) for one in range(count)])  9.74 us
    pallas_call x1, Pallas kernels, attention_forward(): pl.pallas_call(functools.partial(forward_kernel, count), grid=(width // (...  6.93 us
    pallas_call x1, Pallas kernels, weight_grad_of(): pl.pallas_call(functools.partial(weight_grad_kernel, scale, len(attn_piec...  5.54 us
  transfers between devices with their start and end apart: 24, of which 13 were waited for; matrix products, arithmetic and copies ran while one was open for 6% of the time, Pallas kernels for 23%

profile of v2, /device:TPU:0, one launch (start us, length us, event | category | flops | bytes accessed | tf_op | source)
XLA Modules:
  0.0 155.7 jit_solution(8243176354071444398)
XLA Ops:
  0.7 2.2 %slice_bitcast_fusion = (bf16[128,1024]{1,0:T(8,128)(2,1)S(1)}, bf16[128,1024]{1,0:T(8,128)(2,1)}, bf16[128,1024]{1,0:T(8,128)(2,1)}, bf16[128,1024]{1,0:T(8,128)(2,1)S(1)}) fusion(bf16[1,256,1024]{2,1,0:T(8,128)(2,1)} %param.8, bf16[1,256,1024]{2,1,0:T(8,128)(2,1)} %param.7), kind=kLoop, calls=%fused_computation.11 | loop fusion | bytes 2097152 | tf_op jit(solution)/shard_map/slice | solution.py:465
  2.8 5.0 %collective-permute-start.1 = (bf16[128,1024]{1,0:T(8,128)(2,1)S(1)}, bf16[128,1024]{1,0:T(8,128)(2,1)S(1)}, u32[]{:S(2)}, u32[]{:S(2)}) collective-permute-start(bf16[128,1024]{1,0:T(8,128)(2,1)S(1)} %get-tuple-element.42), channel_id=1, source_target_pairs={{0,4},{1,5},{2,6},{3,7}} | collective-permute-start | bytes 786440 | tf_op jit(solution)/shard_map/ppermute | solution.py:425
  16.3 2.0 %collective-permute-start.5 = (bf16[128,1024]{1,0:T(8,128)(2,1)S(1)}, bf16[128,1024]{1,0:T(8,128)(2,1)}, u32[]{:S(2)}, u32[]{:S(2)}) collective-permute-start(bf16[128,1024]{1,0:T(8,128)(2,1)S(1)} %broadcast_select_fusion.2), channel_id=1, source_target_pairs={{0,8},{16,24},{1,9},{17,25},{2,10},{18,26},{3,11},{19,27}} | collective-permute-start | bytes 786440 | tf_op jit(solution)/shard_map/ppermute | solution.py:425
  18.3 3.6 %collective-permute-done.2 = bf16[128,1024]{1,0:T(8,128)(2,1)S(1)} collective-permute-done((bf16[128,1024]{1,0:T(8,128)(2,1)S(1)}, bf16[128,1024]{1,0:T(8,128)(2,1)S(1)}, u32[]{:S(2)}, u32[]{:S(2)}) %collective-permute-start.2) | collective-permute-done | bytes 262176 | tf_op jit(solution)/shard_map/ppermute | solution.py:425
  21.9 2.1 %collective-permute-start.3 = (bf16[128,1024]{1,0:T(8,128)(2,1)S(1)}, bf16[128,1024]{1,0:T(8,128)(2,1)}, u32[]{:S(2)}, u32[]{:S(2)}) collective-permute-start(bf16[128,1024]{1,0:T(8,128)(2,1)S(1)} %broadcast_select_fusion.3), channel_id=1, source_target_pairs={{0,8},{4,12},{16,24},{20,28},{1,9},{5,13},{17,25},{21,29},{2,10},{... | collective-permute-start | bytes 786440 | tf_op jit(solution)/shard_map/ppermute | solution.py:425
  24.1 3.4 %collective-permute-done.5 = bf16[128,1024]{1,0:T(8,128)(2,1)} collective-permute-done((bf16[128,1024]{1,0:T(8,128)(2,1)S(1)}, bf16[128,1024]{1,0:T(8,128)(2,1)}, u32[]{:S(2)}, u32[]{:S(2)}) %collective-permute-start.5) | collective-permute-done | bytes 262176 | tf_op jit(solution)/shard_map/ppermute | solution.py:425
  28.2 2.0 %collective-permute-start.6 = (bf16[128,1024]{1,0:T(8,128)(2,1)}, bf16[128,1024]{1,0:T(8,128)(2,1)}, u32[]{:S(2)}, u32[]{:S(2)}) collective-permute-start(bf16[128,1024]{1,0:T(8,128)(2,1)} %broadcast_select_fusion.4), channel_id=1, source_target_pairs={{0,4},{8,12},{16,20},{24,28},{1,5},{9,13},{17,21},{25,29},{2,6},{1... | collective-permute-start | bytes 786440 | tf_op jit(solution)/shard_map/ppermute | solution.py:425
  31.1 2.1 %collective-permute-start = (bf16[256,1024]{1,0:T(8,128)(2,1)}, bf16[256,1024]{1,0:T(8,128)(2,1)}, u32[]{:S(2)}, u32[]{:S(2)}) collective-permute-start(bf16[256,1024]{1,0:T(8,128)(2,1)} %pad_maximum_fusion), channel_id=1, source_target_pairs={{0,4},{4,8},{8,12},{12,16},{16,20},{20,24},{24,28},{1,5},{5,9},{9,... | collective-permute-start | bytes 1572872 | tf_op jit(solution)/shard_map/ppermute | solution.py:463
  33.9 2.6 %collective-permute-done.6 = bf16[128,1024]{1,0:T(8,128)(2,1)} collective-permute-done((bf16[128,1024]{1,0:T(8,128)(2,1)}, bf16[128,1024]{1,0:T(8,128)(2,1)}, u32[]{:S(2)}, u32[]{:S(2)}) %collective-permute-start.6) | collective-permute-done | bytes 262176 | tf_op jit(solution)/shard_map/ppermute | solution.py:425
  37.0 20.1 %collective-permute-done.18.refs_5_ = bf16[1,256,2048]{2,1,0:T(8,128)(2,1)} collective-permute-done((bf16[1,256,2048]{2,1,0:T(8,128)(2,1)S(1)}, bf16[1,256,2048]{2,1,0:T(8,128)(2,1)}, u32[]{:S(2)}, u32[]{:S(2)}) %collective-permute-start.18) | collective-permute-done | bytes 1048608 | tf_op jit(solution)/shard_map/ppermute | solution.py:407
  59.6 6.9 %attention_forward.1 = (bf16[256,1024]{1,0:T(8,128)(2,1)}, bf16[1,256,512]{2,1,0:T(8,128)(2,1)}, bf16[1,256,256]{2,1,0:T(8,128)(2,1)}) custom-call(bf16[256,1024]{1,0:T(8,128)(2,1)} %bitcast.42, bf16[256,1024]{1,0:T(8,128)(2,1)} %bitcast.32, bf16[256,1024]{1,0:T(8,128)(2,1)} %bitcast.34, bf16[256,1024]{1,0:T(8,128)(2,1)} %collective-permute-done.before_ref, ...), custom_call_target="tpu_custom_call" | custom-call | tf_op jit(solution)/shard_map/attention_forward/pallas_call | solution.py:179
  69.7 7.3 %collective-permute-done.15.refs_1_ = bf16[1,256,512]{2,1,0:T(8,128)(2,1)S(1)} collective-permute-done((bf16[1,256,512]{2,1,0:T(8,128)(2,1)}, bf16[1,256,512]{2,1,0:T(8,128)(2,1)S(1)}, u32[]{:S(2)}, u32[]{:S(2)}) %collective-permute-start.15) | collective-permute-done | bytes 262176 | tf_op jit(solution)/shard_map/ppermute | solution.py:407
  79.2 5.5 %weight_grad.1 = (f32[4,256,256]{2,1,0:T(8,128)}, bf16[4,256,256]{2,1,0:T(8,128)(2,1)}) custom-call(bf16[1,256,1024]{2,1,0:T(8,128)(2,1)} %bitcast.36, bf16[1,256,512]{2,1,0:T(8,128)(2,1)} %copy-done.11, bf16[1,256,256]{2,1,0:T(8,128)(2,1)} %copy-done.13, bf16[1,256,512]{2,1,0:T(8,128)(2,1)} %copy-done.12, bf16[1,256,2048]{2,1,0:T(8,128)(2,1)} %refs_4_.1, ...), custom_call_target="tpu_custom_call" | custom-call | tf_op jit(solution)/shard_map/weight_grad/pallas_call | solution.py:321
  85.8 4.6 %grad_attn.1.grad_ref = bf16[256,1024]{1,0:T(8,128)(2,1)} custom-call(bf16[256,2048]{1,0:T(8,128)(2,1)} %bitcast.37, bf16[1,256,2048]{2,1,0:T(8,128)(2,1)} %bitcast.39, bf16[1,256,2048]{2,1,0:T(8,128)(2,1)} %collective-permute-done.7.refs_2_, bf16[1,256,2048]{2,1,0:T(8,128)(2,1)} %copy-done.5, bf16[1,256,2048]{2,1,0:T(8,128)(2,1)} %collective-permute-done.9.refs_4_), custom_call_target="tpu_custom_call" | custom-call | tf_op jit(solution)/shard_map/grad_attn/pallas_call | solution.py:294
  90.4 10.9 %attention_backward.1 = (bf16[256,1024]{1,0:T(8,128)(2,1)}, f32[256,1024]{1,0:T(8,128)}, f32[256,1024]{1,0:T(8,128)}, bf16[256,1024]{1,0:T(8,128)(2,1)}, f32[128,1024]{1,0:T(8,128)}, /*index=5*/bf16[128,1024]{1,0:T(8,128)(2,1)}) custom-call(bf16[256,1024]{1,0:T(8,128)(2,1)} %bitcast.43, bf16[256,1024]{1,0:T(8,128)(2,1)} %bitcast.33, ...), custom_call_target="tpu_custom_call" | custom-call | tf_op jit(solution)/shard_map/attention_backward/pallas_call | solution.py:198
  101.3 2.1 %collective-permute-start.11 = (bf16[128,1024]{1,0:T(8,128)(2,1)}, bf16[128,1024]{1,0:T(8,128)(2,1)S(1)}, u32[]{:S(2)}, u32[]{:S(2)}) collective-permute-start(bf16[128,1024]{1,0:T(8,128)(2,1)} %get-tuple-element.28), channel_id=1, source_target_pairs={{0,4},{4,0},{8,12},{12,8},{16,20},{20,16},{24,28},{28,24},{1,5},{5... | collective-permute-start | bytes 786440 | tf_op jit(solution)/shard_map/ppermute | solution.py:407
  103.3 6.5 %collective-permute-done.11 = bf16[128,1024]{1,0:T(8,128)(2,1)S(1)} collective-permute-done((bf16[128,1024]{1,0:T(8,128)(2,1)}, bf16[128,1024]{1,0:T(8,128)(2,1)S(1)}, u32[]{:S(2)}, u32[]{:S(2)}) %collective-permute-start.11) | collective-permute-done | bytes 262176 | tf_op jit(solution)/shard_map/ppermute | solution.py:407
  113.5 2.7 %collective-permute-start.22 = (bf16[2,256,256]{2,1,0:T(8,128)(2,1)S(1)}, bf16[2,256,256]{2,1,0:T(8,128)(2,1)S(1)}, u32[]{:S(2)}, u32[]{:S(2)}) collective-permute-start(bf16[2,256,256]{2,1,0:T(8,128)(2,1)S(1)} %fusion.1), channel_id=1, source_target_pairs={{0,8},{4,12},{8,0},{12,4},{16,24},{20,28},{24,16},{28,20},{1,9},{5... | collective-permute-start | bytes 786440 | tf_op jit(solution)/shard_map/ppermute | solution.py:407
  117.5 4.5 %collective-permute-done.12 = bf16[128,1024]{1,0:T(8,128)(2,1)S(1)} collective-permute-done((bf16[128,1024]{1,0:T(8,128)(2,1)S(1)}, bf16[128,1024]{1,0:T(8,128)(2,1)S(1)}, u32[]{:S(2)}, u32[]{:S(2)}) %collective-permute-start.12) | collective-permute-done | bytes 262176 | tf_op jit(solution)/shard_map/ppermute | solution.py:437
  123.5 4.2 %collective-permute-done.22 = bf16[2,256,256]{2,1,0:T(8,128)(2,1)S(1)} collective-permute-done((bf16[2,256,256]{2,1,0:T(8,128)(2,1)S(1)}, bf16[2,256,256]{2,1,0:T(8,128)(2,1)S(1)}, u32[]{:S(2)}, u32[]{:S(2)}) %collective-permute-start.22) | collective-permute-done | bytes 262176 | tf_op jit(solution)/shard_map/ppermute | solution.py:407
  128.1 13.5 %collective-permute-done.13 = bf16[128,1024]{1,0:T(8,128)(2,1)S(1)} collective-permute-done((bf16[128,1024]{1,0:T(8,128)(2,1)S(1)}, bf16[128,1024]{1,0:T(8,128)(2,1)S(1)}, u32[]{:S(2)}, u32[]{:S(2)}) %collective-permute-start.13) | collective-permute-done | bytes 262176 | tf_op jit(solution)/shard_map/ppermute | solution.py:437
  143.9 4.6 %projected.1 = bf16[256,2048]{1,0:T(8,128)(2,1)} custom-call(bf16[256,1024]{1,0:T(8,128)(2,1)} %get-tuple-element.20.refs_0_.attn_ref, bf16[1,256,2048]{2,1,0:T(8,128)(2,1)} %bitcast.40, bf16[1,256,2048]{2,1,0:T(8,128)(2,1)} %collective-permute-done.7.refs_2_, bf16[1,256,2048]{2,1,0:T(8,128)(2,1)} %copy-done.5, ...), custom_call_target="tpu_custom_call" | custom-call | tf_op jit(solution)/shard_map/projected/pallas_call | solution.py:302
  149.2 2.7 %joined.1 = (bf16[256,1024]{1,0:T(8,128)(2,1)}, bf16[256,1024]{1,0:T(8,128)(2,1)}) custom-call(f32[256,1024]{1,0:T(8,128)} %get-tuple-element.22.dk_ref.own_k_ref, f32[256,1024]{1,0:T(8,128)} %get-tuple-element.23.dv_ref.own_v_ref, bf16[256,1024]{1,0:T(8,128)(2,1)} %copy-done.9), custom_call_target="tpu_custom_call" | custom-call | tf_op jit(solution)/shard_map/joined/pallas_call | solution.py:369
  153.4 2.3 %finish.1 = (bf16[256,1024]{1,0:T(8,128)(2,1)}, bf16[256,1024]{1,0:T(8,128)(2,1)}) custom-call(bf16[256,1024]{1,0:T(8,128)(2,1)} %get-tuple-element.25.part_k_ref, bf16[256,1024]{1,0:T(8,128)(2,1)} %get-tuple-element.26.part_v_ref, f32[256,1024]{1,0:T(8,128)} %get-tuple-element.22.dk_ref.own_k_ref, ...), custom_call_target="tpu_custom_call", output_to_operand_aliasing={{0}: (0, {}), {1}: (1, {})} | custom-call | tf_op jit(solution)/shard_map/finish/pallas_call | solution.py:384
  (78 shorter events, 31.3 us)
Async XLA Ops:
  2.8 10.5 %collective-permute-start.1 = (bf16[128,1024]{1,0:T(8,128)(2,1)S(1)}, bf16[128,1024]{1,0:T(8,128)(2,1)S(1)}, u32[]{:S(2)}, u32[]{:S(2)}) collective-permute-start(bf16[128,1024]{1,0:T(8,128)(2,1)S(1)} %get-tuple-element.42), channel_id=1, source_target_pairs={{0,4},{1,5},{2,6},{3,7}} | collective-permute-start | bytes 786440 | tf_op jit(solution)/shard_map/ppermute | solution.py:425
  7.9 8.4 %collective-permute-start.4 = (bf16[128,1024]{1,0:T(8,128)(2,1)S(1)}, bf16[128,1024]{1,0:T(8,128)(2,1)S(1)}, u32[]{:S(2)}, u32[]{:S(2)}) collective-permute-start(bf16[128,1024]{1,0:T(8,128)(2,1)S(1)} %get-tuple-element.37), channel_id=1, source_target_pairs={{0,16},{1,17},{2,18},{3,19}} | collective-permute-start | bytes 786440 | tf_op jit(solution)/shard_map/ppermute | solution.py:425
  9.6 26.9 %collective-permute-start.7 = (bf16[1,256,2048]{2,1,0:T(8,128)(2,1)}, bf16[1,256,2048]{2,1,0:T(8,128)(2,1)}, u32[]{:S(2)}, u32[]{:S(2)}) collective-permute-start(bf16[1,256,2048]{2,1,0:T(8,128)(2,1)} %bitcast.38), channel_id=1, source_target_pairs={{0,2},{1,3},{2,0},{3,1},{4,6},{5,7},{6,4},{7,5},{8,10},{9,11},{10,... | collective-permute-start | bytes 3145736 | tf_op jit(solution)/shard_map/ppermute | solution.py:407
  11.2 45.9 %collective-permute-start.18 = (bf16[1,256,2048]{2,1,0:T(8,128)(2,1)S(1)}, bf16[1,256,2048]{2,1,0:T(8,128)(2,1)}, u32[]{:S(2)}, u32[]{:S(2)}) collective-permute-start(bf16[1,256,2048]{2,1,0:T(8,128)(2,1)S(1)} %copy-done.3), channel_id=1, source_target_pairs={{0,2},{1,3},{2,0},{3,1},{4,6},{5,7},{6,4},{7,5},{8,10},{9,11},{10,... | collective-permute-start | bytes 3145736 | tf_op jit(solution)/shard_map/ppermute | solution.py:407
  13.4 8.5 %collective-permute-start.2 = (bf16[128,1024]{1,0:T(8,128)(2,1)S(1)}, bf16[128,1024]{1,0:T(8,128)(2,1)S(1)}, u32[]{:S(2)}, u32[]{:S(2)}) collective-permute-start(bf16[128,1024]{1,0:T(8,128)(2,1)S(1)} %broadcast_select_fusion.1), channel_id=1, source_target_pairs={{0,16},{4,20},{1,17},{5,21},{2,18},{6,22},{3,19},{7,23}} | collective-permute-start | bytes 786440 | tf_op jit(solution)/shard_map/ppermute | solution.py:425
  16.3 11.2 %collective-permute-start.5 = (bf16[128,1024]{1,0:T(8,128)(2,1)S(1)}, bf16[128,1024]{1,0:T(8,128)(2,1)}, u32[]{:S(2)}, u32[]{:S(2)}) collective-permute-start(bf16[128,1024]{1,0:T(8,128)(2,1)S(1)} %broadcast_select_fusion.2), channel_id=1, source_target_pairs={{0,8},{16,24},{1,9},{17,25},{2,10},{18,26},{3,11},{19,27}} | collective-permute-start | bytes 786440 | tf_op jit(solution)/shard_map/ppermute | solution.py:425
  21.9 12.0 %collective-permute-start.3 = (bf16[128,1024]{1,0:T(8,128)(2,1)S(1)}, bf16[128,1024]{1,0:T(8,128)(2,1)}, u32[]{:S(2)}, u32[]{:S(2)}) collective-permute-start(bf16[128,1024]{1,0:T(8,128)(2,1)S(1)} %broadcast_select_fusion.3), channel_id=1, source_target_pairs={{0,8},{4,12},{16,24},{20,28},{1,9},{5,13},{17,25},{21,29},{2,10},{... | collective-permute-start | bytes 786440 | tf_op jit(solution)/shard_map/ppermute | solution.py:425
  28.2 8.3 %collective-permute-start.6 = (bf16[128,1024]{1,0:T(8,128)(2,1)}, bf16[128,1024]{1,0:T(8,128)(2,1)}, u32[]{:S(2)}, u32[]{:S(2)}) collective-permute-start(bf16[128,1024]{1,0:T(8,128)(2,1)} %broadcast_select_fusion.4), channel_id=1, source_target_pairs={{0,4},{8,12},{16,20},{24,28},{1,5},{9,13},{17,21},{25,29},{2,6},{1... | collective-permute-start | bytes 786440 | tf_op jit(solution)/shard_map/ppermute | solution.py:425
  31.1 28.5 %collective-permute-start = (bf16[256,1024]{1,0:T(8,128)(2,1)}, bf16[256,1024]{1,0:T(8,128)(2,1)}, u32[]{:S(2)}, u32[]{:S(2)}) collective-permute-start(bf16[256,1024]{1,0:T(8,128)(2,1)} %pad_maximum_fusion), channel_id=1, source_target_pairs={{0,4},{4,8},{8,12},{12,16},{16,20},{20,24},{24,28},{1,5},{5,9},{9,... | collective-permute-start | bytes 1572872 | tf_op jit(solution)/shard_map/ppermute | solution.py:463
  33.9 50.9 %collective-permute-start.8 = (bf16[1,256,2048]{2,1,0:T(8,128)(2,1)S(1)}, bf16[1,256,2048]{2,1,0:T(8,128)(2,1)S(1)}, u32[]{:S(2)}, u32[]{:S(2)}) collective-permute-start(bf16[1,256,2048]{2,1,0:T(8,128)(2,1)S(1)} %bitcast.41), channel_id=1, source_target_pairs={{0,1},{1,0},{2,3},{3,2},{4,5},{5,4},{6,7},{7,6},{8,9},{9,8},{10,11... | collective-permute-start | bytes 3145736 | tf_op jit(solution)/shard_map/ppermute | solution.py:407
  36.5 40.5 %collective-permute-start.19 = (bf16[1,256,2048]{2,1,0:T(8,128)(2,1)S(1)}, bf16[1,256,2048]{2,1,0:T(8,128)(2,1)}, u32[]{:S(2)}, u32[]{:S(2)}) collective-permute-start(bf16[1,256,2048]{2,1,0:T(8,128)(2,1)S(1)} %copy-done.3), channel_id=1, source_target_pairs={{0,1},{1,0},{2,3},{3,2},{4,5},{5,4},{6,7},{7,6},{8,9},{9,8},{10,11... | collective-permute-start | bytes 3145736 | tf_op jit(solution)/shard_map/ppermute | solution.py:407
  36.5 48.3 %collective-permute-start.9 = (bf16[1,256,2048]{2,1,0:T(8,128)(2,1)}, bf16[1,256,2048]{2,1,0:T(8,128)(2,1)}, u32[]{:S(2)}, u32[]{:S(2)}) collective-permute-start(bf16[1,256,2048]{2,1,0:T(8,128)(2,1)} %collective-permute-done.7.refs_2_), channel_id=1, source_target_pairs={{0,1},{1,0},{2,3},{3,2},{4,5},{5,4},{6,7},{7,6},{8,9},{9,8},{10,11... | collective-permute-start | bytes 3145736 | tf_op jit(solution)/shard_map/ppermute | solution.py:407
  57.1 22.1 %collective-permute-start.20 = (bf16[1,256,2048]{2,1,0:T(8,128)(2,1)}, bf16[1,256,2048]{2,1,0:T(8,128)(2,1)}, u32[]{:S(2)}, u32[]{:S(2)}) collective-permute-start(bf16[1,256,2048]{2,1,0:T(8,128)(2,1)} %collective-permute-done.18.refs_5_), channel_id=1, source_target_pairs={{0,1},{1,0},{2,3},{3,2},{4,5},{5,4},{6,7},{7,6},{8,9},{9,8},{10,11... | collective-permute-start | bytes 3145736 | tf_op jit(solution)/shard_map/ppermute | solution.py:407
  66.5 1.7 %collective-permute-start.16 = (bf16[1,256,256]{2,1,0:T(8,128)(2,1)}, bf16[1,256,256]{2,1,0:T(8,128)(2,1)S(1)}, u32[]{:S(2)}, u32[]{:S(2)}) collective-permute-start(bf16[1,256,256]{2,1,0:T(8,128)(2,1)} %get-tuple-element.32), channel_id=1, source_target_pairs={{0,1},{1,0},{2,3},{3,2},{4,5},{5,4},{6,7},{7,6},{8,9},{9,8},{10,11... | collective-permute-start | bytes 393224 | tf_op jit(solution)/shard_map/ppermute | solution.py:407
  68.2 8.8 %collective-permute-start.15 = (bf16[1,256,512]{2,1,0:T(8,128)(2,1)}, bf16[1,256,512]{2,1,0:T(8,128)(2,1)S(1)}, u32[]{:S(2)}, u32[]{:S(2)}) collective-permute-start(bf16[1,256,512]{2,1,0:T(8,128)(2,1)} %get-tuple-element.31), channel_id=1, source_target_pairs={{0,2},{1,3},{2,0},{3,1},{4,6},{5,7},{6,4},{7,5},{8,10},{9,11},{10,... | collective-permute-start | bytes 786440 | tf_op jit(solution)/shard_map/ppermute | solution.py:407
  77.0 1.5 collective-permute-start.17
  84.8 27.5 %collective-permute-start.21 = (bf16[2,2,256,256]{3,2,1,0:T(8,128)(2,1)}, bf16[2,2,256,256]{3,2,1,0:T(8,128)(2,1)}, u32[]{:S(2)}, u32[]{:S(2)}) collective-permute-start(bf16[2,2,256,256]{3,2,1,0:T(8,128)(2,1)} %bitcast.49), channel_id=1, source_target_pairs={{0,4},{4,0},{8,12},{12,8},{16,20},{20,16},{24,28},{28,24},{1,5},{5... | collective-permute-start | bytes 1572872 | tf_op jit(solution)/shard_map/ppermute | solution.py:407
  101.3 8.6 %collective-permute-start.11 = (bf16[128,1024]{1,0:T(8,128)(2,1)}, bf16[128,1024]{1,0:T(8,128)(2,1)S(1)}, u32[]{:S(2)}, u32[]{:S(2)}) collective-permute-start(bf16[128,1024]{1,0:T(8,128)(2,1)} %get-tuple-element.28), channel_id=1, source_target_pairs={{0,4},{4,0},{8,12},{12,8},{16,20},{20,16},{24,28},{28,24},{1,5},{5... | collective-permute-start | bytes 786440 | tf_op jit(solution)/shard_map/ppermute | solution.py:407
  111.0 11.1 %collective-permute-start.12 = (bf16[128,1024]{1,0:T(8,128)(2,1)S(1)}, bf16[128,1024]{1,0:T(8,128)(2,1)S(1)}, u32[]{:S(2)}, u32[]{:S(2)}) collective-permute-start(bf16[128,1024]{1,0:T(8,128)(2,1)S(1)} %fusion), channel_id=1, source_target_pairs={{8,0},{12,4},{24,16},{28,20},{9,1},{13,5},{25,17},{29,21},{10,2},{... | collective-permute-start | bytes 786440 | tf_op jit(solution)/shard_map/ppermute | solution.py:437
  113.5 14.2 %collective-permute-start.22 = (bf16[2,256,256]{2,1,0:T(8,128)(2,1)S(1)}, bf16[2,256,256]{2,1,0:T(8,128)(2,1)S(1)}, u32[]{:S(2)}, u32[]{:S(2)}) collective-permute-start(bf16[2,256,256]{2,1,0:T(8,128)(2,1)S(1)} %fusion.1), channel_id=1, source_target_pairs={{0,8},{4,12},{8,0},{12,4},{16,24},{20,28},{24,16},{28,20},{1,9},{5... | collective-permute-start | bytes 786440 | tf_op jit(solution)/shard_map/ppermute | solution.py:407
  116.2 32.2 %collective-permute-start.10 = (bf16[256,1024]{1,0:T(8,128)(2,1)}, bf16[256,1024]{1,0:T(8,128)(2,1)S(1)}, u32[]{:S(2)}, u32[]{:S(2)}) collective-permute-start(bf16[256,1024]{1,0:T(8,128)(2,1)} %get-tuple-element.24), channel_id=1, source_target_pairs={{4,0},{8,4},{12,8},{16,12},{20,16},{24,20},{28,24},{5,1},{9,5},{13... | collective-permute-start | bytes 1572872 | tf_op jit(solution)/shard_map/ppermute | solution.py:476
  122.2 19.5 %collective-permute-start.13 = (bf16[128,1024]{1,0:T(8,128)(2,1)S(1)}, bf16[128,1024]{1,0:T(8,128)(2,1)S(1)}, u32[]{:S(2)}, u32[]{:S(2)}) collective-permute-start(bf16[128,1024]{1,0:T(8,128)(2,1)S(1)} %fusion.2), channel_id=1, source_target_pairs={{16,0},{20,4},{17,1},{21,5},{18,2},{22,6},{19,3},{23,7}} | collective-permute-start | bytes 786440 | tf_op jit(solution)/shard_map/ppermute | solution.py:437
  127.8 24.2 %collective-permute-start.23 = (bf16[256,256]{1,0:T(8,128)(2,1)S(1)}, bf16[256,256]{1,0:T(8,128)(2,1)S(1)}, u32[]{:S(2)}, u32[]{:S(2)}) collective-permute-start(bf16[256,256]{1,0:T(8,128)(2,1)S(1)} %fusion.3), channel_id=1, source_target_pairs={{0,16},{4,20},{8,24},{12,28},{16,0},{20,4},{24,8},{28,12},{1,17},{... | collective-permute-start | bytes 393224 | tf_op jit(solution)/shard_map/ppermute | solution.py:407
  142.6 10.1 %collective-permute-start.14 = (bf16[128,1024]{1,0:T(8,128)(2,1)S(1)}, bf16[128,1024]{1,0:T(8,128)(2,1)S(1)}, u32[]{:S(2)}, u32[]{:S(2)}) collective-permute-start(bf16[128,1024]{1,0:T(8,128)(2,1)S(1)} %get-tuple-element.35), channel_id=1, source_target_pairs={{4,0},{5,1},{6,2},{7,3}} | collective-permute-start | bytes 786440 | tf_op jit(solution)/shard_map/ppermute | solution.py:439
  (15 other events, 104.5 us)

commit v3 on v2

--- a/solution.py
+++ b/solution.py
@@ -1,4 +1,5 @@
 import functools
+import math
 
 import jax
 import jax.numpy as jnp
@@ -12,8 +13,10 @@
 BLK = 128
 
 WIN = 2
-HEADS_STEP = 2
-
+HEADS_STEP = 4
+
+ROWS_STEP = 64
+LOG2_E = math.log2(math.e)
 MASKED = -1e30
 ROOT = HDIM ** (-0.5)
 F32 = jnp.float32
@@ -26,63 +29,101 @@
     )
 
 
-def probabilities(q, k_ext, k_sink, pattern_ref, head, first_block):
-    blocks = q.shape[0] // BLK
-    row = lax.broadcasted_iota(jnp.int32, (BLK, BLK), 0)
-    column = lax.broadcasted_iota(jnp.int32, (BLK, BLK), 1)
-    causal = column <= row
-    sink_scores = dot(q, k_sink, 1, 1) * ROOT
-    window, sink = [], []
-    for number in range(blocks):
-        here = slice(number * BLK, (number + 1) * BLK)
-        block = first_block + number
-        scores = dot(q[here], k_ext[number * BLK : (number + WIN) * BLK], 1, 1) * ROOT
-        reached = jnp.logical_and(pattern_ref[0, head, block, 1] == 1, block >= 2)
-        before = jnp.where(reached, scores[:, :BLK], MASKED)
-        own = jnp.where(jnp.logical_and(causal, block >= 1), scores[:, BLK:], MASKED)
-        first = jnp.where(jnp.logical_or(causal, block >= 1), sink_scores[here], MASKED)
-        top = jnp.max(jnp.maximum(jnp.maximum(before, own), first), axis=1, keepdims=True)
-        before = jnp.exp(before - top)
-        own = jnp.exp(own - top)
-        first = jnp.exp(first - top)
-        total = jnp.sum(before + own + first, axis=1, keepdims=True)
-        inverse = 1.0 / total
-        window.append(jnp.concatenate([before * inverse, own * inverse], axis=1))
-        sink.append(first * inverse)
-    return window, jnp.concatenate(sink, axis=0)
+def sink_of(kept, got, bit):
+    return jnp.where((lax.axis_index("ctx") & bit) != 0, got, kept)
+
+
+def softmax_rows(scores_ref, at, pattern_ref, head, block, first_row):
+    scores = scores_ref[at]
+    shape = (scores.shape[0], BLK)
+    causal = lax.broadcasted_iota(jnp.int32, shape, 1) <= (
+        lax.broadcasted_iota(jnp.int32, shape, 0) + first_row
+    )
+    reached = jnp.logical_and(pattern_ref[0, head, block, 1] == 1, block >= 2)
+    before = jnp.where(reached, scores[:, :BLK], MASKED)
+    own = jnp.where(jnp.logical_and(causal, block >= 1), scores[:, BLK : 2 * BLK], MASKED)
+    first = jnp.where(jnp.logical_or(causal, block >= 1), scores[:, 2 * BLK :], MASKED)
+    top = jnp.max(jnp.maximum(jnp.maximum(before, own), first), axis=1, keepdims=True)
+    parts = [jnp.exp2((one - top) * (ROOT * LOG2_E)) for one in (before, own, first)]
+    total = jnp.sum(parts[0] + parts[1] + parts[2], axis=1, keepdims=True)
+    return parts, top, 1.0 / total
 
 
 def forward_kernel(
     count,
+    last_bits,
     q_ref,
     k_ref,
     v_ref,
     before_ref,
-    sink_k_ref,
-    sink_v_ref,
+    kept_k_ref,
+    kept_v_ref,
+    got_k_ref,
+    got_v_ref,
     pattern_ref,
+    grad_ref,
     out_ref,
-    *away_refs,
+    probs_ref,
+    stats_ref,
+    *rest,
 ):
+    away_refs, (scores_ref, rounded_ref) = rest[:-2], rest[-2:]
     rows = q_ref.shape[0]
     blocks = rows // BLK
+    heads = q_ref.shape[1] // HDIM
+    total_heads = out_ref.shape[1] // HDIM
     first_block = lax.axis_index("ctx") * blocks
-    for local in range(q_ref.shape[1] // HDIM):
+    first_head = pl.program_id(0) * heads
+
+    @pl.when(pl.program_id(0) == 0)
+    def _():
+        stats_ref[...] = jnp.zeros_like(stats_ref)
+
+    for local in range(heads):
         cols = slice(local * HDIM, (local + 1) * HDIM)
-        head = pl.program_id(0) * (q_ref.shape[1] // HDIM) + local
         k_ext = jnp.concatenate([before_ref[:BLK, cols], k_ref[:, cols]], axis=0)
-        v_ext = jnp.concatenate([before_ref[BLK:, cols], v_ref[:, cols]], axis=0)
-        window, sink = probabilities(
-            q_ref[:, cols], k_ext, sink_k_ref[:, cols], pattern_ref, head, first_block
-        )
-        from_sink = dot(sink.astype(BF16), sink_v_ref[:, cols], 1, 0)
+        k_sink = sink_of(kept_k_ref[:, cols], got_k_ref[:, cols], last_bits[0])
+        scores_ref[local, :, 2 * BLK :] = dot(q_ref[:, cols], k_sink, 1, 1)
         for number in range(blocks):
             here = slice(number * BLK, (number + 1) * BLK)
-            near = dot(
-                window[number].astype(BF16), v_ext[number * BLK : (number + WIN) * BLK], 1, 0
+            there = slice(number * BLK, (number + WIN) * BLK)
+            scores_ref[local, here, : 2 * BLK] = dot(q_ref[here, cols], k_ext[there], 1, 1)
+    lane = lax.broadcasted_iota(jnp.int32, (ROWS_STEP, BLK), 1)
+    for local in range(heads):
+        cols = slice(local * HDIM, (local + 1) * HDIM)
+        head = first_head + local
+        for row in range(0, rows, ROWS_STEP):
+            at = slice(row, row + ROWS_STEP)
+            parts, top, inverse = softmax_rows(
+                scores_ref.at[local], at, pattern_ref, head, first_block + row // BLK, row % BLK
             )
-            at = pl.multiple_of(head * HDIM, HDIM)
-            out_ref[here, pl.ds(at, HDIM)] = (near + from_sink[here]).astype(BF16)
+            for place, part in enumerate(parts):
+                there = slice(place * BLK, (place + 1) * BLK)
+                part = part * inverse
+                probs_ref[local, at, there] = part
+                rounded_ref[local, at, there] = part.astype(BF16)
+            if row < BLK:
+                stats = stats_ref[at]
+                stats = jnp.where(lane == head, top, stats)
+                stats_ref[at] = jnp.where(lane == head + total_heads, inverse, stats)
+    for local in range(heads):
+        cols = slice(local * HDIM, (local + 1) * HDIM)
+        head = first_head + local
+        v_ext = jnp.concatenate([before_ref[BLK:, cols], v_ref[:, cols]], axis=0)
+        v_sink = sink_of(kept_v_ref[:, cols], got_v_ref[:, cols], last_bits[1])
+        from_sink = dot(rounded_ref[local, :, 2 * BLK :], v_sink, 1, 0)
+        for number in range(blocks):
+            here = slice(number * BLK, (number + 1) * BLK)
+            there = slice(number * BLK, (number + WIN) * BLK)
+            near = dot(rounded_ref[local, here, : 2 * BLK], v_ext[there], 1, 0)
+            attended = (near + from_sink[here]).astype(BF16)
+            out_ref[here, pl.ds(pl.multiple_of(head * HDIM, HDIM), HDIM)] = attended
+            if number == 0:
+                delta = jnp.sum(
+                    grad_ref[:BLK, cols].astype(F32) * attended.astype(F32), axis=1, keepdims=True
+                )
+                wide = lax.broadcasted_iota(jnp.int32, (BLK, BLK), 1)
+                stats_ref[...] = jnp.where(wide == head + 2 * total_heads, delta, stats_ref[...])
 
     @pl.when(pl.program_id(0) == pl.num_programs(0) - 1)
     def _():
@@ -94,63 +135,113 @@
 
 
 def backward_kernel(
+    last_bits,
     q_ref,
     k_ref,
     v_ref,
     before_ref,
-    sink_k_ref,
-    sink_v_ref,
-    pattern_ref,
+    kept_k_ref,
+    kept_v_ref,
+    got_k_ref,
+    got_v_ref,
+    probs_ref,
     attn_ref,
     grad_ref,
     dq_ref,
     dk_ref,
     dv_ref,
-    dbefore_ref,
     kept_ref,
     sent_ref,
+    dprobs_ref,
+    dscores_ref,
+    rounded_ref,
 ):
     rows = q_ref.shape[0]
     blocks = rows // BLK
-    first_block = lax.axis_index("ctx") * blocks
-    for local in range(q_ref.shape[1] // HDIM):
+    heads = q_ref.shape[1] // HDIM
+    for local in range(heads):
         cols = slice(local * HDIM, (local + 1) * HDIM)
-        head = pl.program_id(0) * (q_ref.shape[1] // HDIM) + local
-        q = q_ref[:, cols]
-        grad = grad_ref[:, cols]
-        k_sink = sink_k_ref[:, cols]
-        k_ext = jnp.concatenate([before_ref[:BLK, cols], k_ref[:, cols]], axis=0)
         v_ext = jnp.concatenate([before_ref[BLK:, cols], v_ref[:, cols]], axis=0)
-        window, sink = probabilities(q, k_ext, k_sink, pattern_ref, head, first_block)
-        delta = jnp.sum(grad.astype(F32) * attn_ref[:, cols].astype(F32), axis=1, keepdims=True)
-        dprobs = dot(grad, sink_v_ref[:, cols], 1, 1)
-        dscores = (sink * (dprobs - delta)).astype(BF16)
-        dq_sink = dot(dscores, k_sink, 1, 0)
-        dsink_k = dot(dscores, q, 0, 0) * ROOT
-        dsink_v = dot(sink.astype(BF16), grad, 0, 0)
-        odd = (lax.axis_index("ctx") & 1) != 0
-        kept_ref[:, cols] = jnp.where(odd, dsink_v, dsink_k)
-        sent_ref[:, cols] = jnp.where(odd, dsink_k, dsink_v).astype(BF16)
-        dk_parts = [None] * (blocks + 1)
-        dv_parts = [None] * (blocks + 1)
+        v_sink = sink_of(kept_v_ref[:, cols], got_v_ref[:, cols], last_bits[1])
+        dprobs_ref[local, :, 2 * BLK :] = dot(grad_ref[:, cols], v_sink, 1, 1)
         for number in range(blocks):
             here = slice(number * BLK, (number + 1) * BLK)
             there = slice(number * BLK, (number + WIN) * BLK)
-            dprobs = dot(grad[here], v_ext[there], 1, 1)
-            dscores = (window[number] * (dprobs - delta[here])).astype(BF16)
-            dq = dot(dscores, k_ext[there], 1, 0)
+            dprobs_ref[local, here, : 2 * BLK] = dot(grad_ref[here, cols], v_ext[there], 1, 1)
+    for local in range(heads):
+        cols = slice(local * HDIM, (local + 1) * HDIM)
+        for row in range(0, rows, ROWS_STEP):
+            at = slice(row, row + ROWS_STEP)
+            delta = jnp.sum(
+                grad_ref[at, cols].astype(F32) * attn_ref[at, cols].astype(F32),
+                axis=1,
+                keepdims=True,
+            )
+            probs = probs_ref[local, at]
+            dscores_ref[local, at] = (probs * (dprobs_ref[local, at] - delta)).astype(BF16)
+            rounded_ref[local, at] = probs.astype(BF16)
+    odd = (lax.axis_index("ctx") & 1) != 0
+    for local in range(heads):
+        cols = slice(local * HDIM, (local + 1) * HDIM)
+        q = q_ref[:, cols]
+        grad = grad_ref[:, cols]
+        k_ext = jnp.concatenate([before_ref[:BLK, cols], k_ref[:, cols]], axis=0)
+        k_sink = sink_of(kept_k_ref[:, cols], got_k_ref[:, cols], last_bits[0])
+        dq_sink = dot(dscores_ref[local, :, 2 * BLK :], k_sink, 1, 0)
+        for number in range(blocks):
+            here = slice(number * BLK, (number + 1) * BLK)
+            there = slice(number * BLK, (number + WIN) * BLK)
+            dq = dot(dscores_ref[local, here, : 2 * BLK], k_ext[there], 1, 0)
             dq_ref[here, cols] = ((dq + dq_sink[here]) * ROOT).astype(BF16)
-            dk = dot(dscores, q[here], 0, 0) * ROOT
-            dv = dot(window[number].astype(BF16), grad[here], 0, 0)
-            for part in range(WIN):
-                piece = slice(part * BLK, (part + 1) * BLK)
-                at = number + part
-                dk_parts[at] = dk[piece] if dk_parts[at] is None else dk_parts[at] + dk[piece]
-                dv_parts[at] = dv[piece] if dv_parts[at] is None else dv_parts[at] + dv[piece]
-        dbefore_ref[:BLK, cols] = dk_parts[0].astype(dbefore_ref.dtype)
-        dbefore_ref[BLK:, cols] = dv_parts[0].astype(dbefore_ref.dtype)
-        dk_ref[:, cols] = jnp.concatenate(dk_parts[1:], axis=0)
-        dv_ref[:, cols] = jnp.concatenate(dv_parts[1:], axis=0)
+        dsink_k = dot(dscores_ref[local, :, 2 * BLK :], q, 0, 0) * ROOT
+        dsink_v = dot(rounded_ref[local, :, 2 * BLK :], grad, 0, 0)
+        kept_ref[:, cols] = jnp.where(odd, dsink_v, dsink_k)
+        sent_ref[:, cols] = jnp.where(odd, dsink_k, dsink_v).astype(BF16)
+        for number in range(blocks):
+            here = slice(number * BLK, (number + 1) * BLK)
+            own = slice(BLK, 2 * BLK)
+            dk = dot(dscores_ref[local, here, own], q[here], 0, 0)
+            dv = dot(rounded_ref[local, here, own], grad[here], 0, 0)
+            if number + 1 < blocks:
+                above = slice((number + 1) * BLK, (number + 2) * BLK)
+                dk += dot(dscores_ref[local, above, :BLK], q[above], 0, 0)
+                dv += dot(rounded_ref[local, above, :BLK], grad[above], 0, 0)
+            dk_ref[here, cols] = dk * ROOT
+            dv_ref[here, cols] = dv
+
+
+def next_kernel(
+    k_ref, v_ref, next_ref, stats_ref, pattern_ref, dk_ref, dv_ref, out_k_ref, out_v_ref
+):
+    rows = k_ref.shape[0]
+    last = slice(rows - BLK, rows)
+    heads = k_ref.shape[1] // HDIM
+    total_heads = pl.num_programs(0) * heads
+    block = (lax.axis_index("ctx") + 1) * (rows // BLK)
+    inside = jnp.minimum(block, pattern_ref.shape[2] - 1)
+    lane = lax.broadcasted_iota(jnp.int32, (BLK, BLK), 1)
+    stats = stats_ref[...]
+
+    def column(index):
+        return jnp.sum(jnp.where(lane == index, stats, 0.0), axis=1, keepdims=True)
+
+    for local in range(heads):
+        cols = slice(local * HDIM, (local + 1) * HDIM)
+        head = pl.program_id(0) * heads + local
+        top, inverse, delta = (column(head + kind * total_heads) for kind in range(3))
+        q, grad = next_ref[:BLK, cols], next_ref[BLK:, cols]
+        scores = dot(q, k_ref[last, cols], 1, 1)
+        reached = jnp.logical_and(pattern_ref[0, head, inside, 1] == 1, block >= 2)
+        probs = jnp.exp2((scores - top) * (ROOT * LOG2_E)) * inverse
+        probs = jnp.where(reached, probs, 0.0)
+        dprobs = dot(grad, v_ref[last, cols], 1, 1)
+        dscores = (probs * (dprobs - delta)).astype(BF16)
+        dk = dk_ref[last, cols] + dot(dscores, q, 0, 0) * ROOT
+        dv = dv_ref[last, cols] + dot(probs.astype(BF16), grad, 0, 0)
+        out_k_ref[last, cols] = dk.astype(BF16)
+        out_v_ref[last, cols] = dv.astype(BF16)
+    out_k_ref[: rows - BLK] = dk_ref[: rows - BLK].astype(BF16)
+    out_v_ref[: rows - BLK] = dv_ref[: rows - BLK].astype(BF16)
 
 
 def head_spec(rows):
@@ -161,7 +252,7 @@
     return pl.BlockSpec(shape, lambda *_: (0,) * len(shape), memory_space=pltpu.SMEM)
 
 
-def attention_specs(rows, pattern):
+def attention_specs(rows):
     return [
         head_spec(rows),
         head_spec(rows),
@@ -169,41 +260,56 @@
         head_spec(2 * BLK),
         head_spec(BLK),
         head_spec(BLK),
-        whole_smem(pattern.shape),
+        head_spec(BLK),
+        head_spec(BLK),
     ]
 
 
-def attention_forward(count, q, k, v, before, sink_k, sink_v, pattern):
+def probs_spec(rows):
+    return pl.BlockSpec((HEADS_STEP, rows, (WIN + 1) * BLK), lambda step: (step, 0, 0))
+
+
+def attention_forward(count, last_bits, q, k, v, before, sinks, pattern, grad):
     rows, width = q.shape
+    heads = width // HDIM
     away = [bit * width // count for bit in reversed(bits_of(count))]
+    shape = jax.ShapeDtypeStruct
     return pl.pallas_call(
-        functools.partial(forward_kernel, count),
-        grid=(width // (HEADS_STEP * HDIM),),
-        in_specs=attention_specs(rows, pattern),
+        functools.partial(forward_kernel, count, last_bits),
+        grid=(heads // HEADS_STEP,),
+        in_specs=attention_specs(rows) + [whole_smem(pattern.shape), head_spec(rows)],
         out_specs=[
             pl.BlockSpec((rows, width), lambda step: (0, 0)),
+            probs_spec(rows),
+            pl.BlockSpec((BLK, BLK), lambda step: (0, 0)),
             *(pl.BlockSpec((1, rows, one), lambda step: (0, 0, 0)) for one in away),
         ],
         out_shape=[
-            jax.ShapeDtypeStruct((rows, width), BF16),
-            *(jax.ShapeDtypeStruct((1, rows, one), BF16) for one in away),
+            shape((rows, width), BF16),
+            shape((heads, rows, (WIN + 1) * BLK), F32),
+            shape((BLK, BLK), F32),
+            *(shape((1, rows, one), BF16) for one in away),
+        ],
+        scratch_shapes=[
+            pltpu.VMEM((HEADS_STEP, rows, (WIN + 1) * BLK), F32),
+            pltpu.VMEM((HEADS_STEP, rows, (WIN + 1) * BLK), BF16),
         ],
         name="attention_forward",
-    )(q, k, v, before, sink_k, sink_v, pattern)
-
-
-def attention_backward(q, k, v, before, sink_k, sink_v, pattern, attn, grad):
+    )(q, k, v, before, *sinks, pattern, grad)
+
+
+def attention_backward(last_bits, q, k, v, before, sinks, probs, attn, grad):
     rows, width = q.shape
     shape = jax.ShapeDtypeStruct
+    scratch = (HEADS_STEP, rows, (WIN + 1) * BLK)
     return pl.pallas_call(
-        backward_kernel,
+        functools.partial(backward_kernel, last_bits),
         grid=(width // (HEADS_STEP * HDIM),),
-        in_specs=attention_specs(rows, pattern) + [head_spec(rows), head_spec(rows)],
+        in_specs=attention_specs(rows) + [probs_spec(rows), head_spec(rows), head_spec(rows)],
         out_specs=[
             head_spec(rows),
             head_spec(rows),
             head_spec(rows),
-            head_spec(2 * BLK),
             head_spec(BLK),
             head_spec(BLK),
         ],
@@ -211,16 +317,41 @@
             shape((rows, width), BF16),
             shape((rows, width), F32),
             shape((rows, width), F32),
-            shape((2 * BLK, width), BF16),
             shape((BLK, width), F32),
             shape((BLK, width), BF16),
         ],
+        scratch_shapes=[
+            pltpu.VMEM(scratch, F32),
+            pltpu.VMEM(scratch, BF16),
+            pltpu.VMEM(scratch, BF16),
+        ],
         name="attention_backward",
-    )(q, k, v, before, sink_k, sink_v, pattern, attn, grad)
+    )(q, k, v, before, *sinks, probs, attn, grad)
+
+
+def next_backward(k, v, following, stats, pattern, dk, dv):
+    rows, width = k.shape
+    shape = jax.ShapeDtypeStruct((rows, width), BF16)
+    return pl.pallas_call(
+        next_kernel,
+        grid=(width // (HEADS_STEP * HDIM),),
+        in_specs=[
+            head_spec(rows),
+            head_spec(rows),
+            head_spec(2 * BLK),
+            pl.BlockSpec((BLK, BLK), lambda step: (0, 0)),
+            whole_smem(pattern.shape),
+            head_spec(rows),
+            head_spec(rows),
+        ],
+        out_specs=[head_spec(rows), head_spec(rows)],
+        out_shape=[shape, shape],
+        name="next_backward",
+    )(k, v, following, stats, pattern, dk, dv)
 
 
 def grad_attn_kernel(count, *refs):
-    cot_ref, pieces, out_ref = refs[0], refs[1:-1], refs[-1]
+    cot_ref, q_ref, pieces, out_ref, back_ref = refs[0], refs[1], refs[2:-2], refs[-2], refs[-1]
     mine = lax.axis_index("dp")
     number = 0
     for piece in pieces:
@@ -229,6 +360,8 @@
             at = pl.multiple_of((mine ^ order_of(count)[number]) * depth, HDIM)
             out_ref[:, pl.ds(at, depth)] = dot(cot_ref[...], piece[slot], 1, 1).astype(BF16)
             number += 1
+    back_ref[:BLK] = q_ref[:BLK]
+    back_ref[BLK:] = out_ref[:BLK]
 
 
 def projected_kernel(count, *refs):
@@ -288,14 +421,17 @@
     out_ref[0] = total * scale
 
 
-def grad_attn_of(cot, pieces, count):
+def grad_attn_of(cot, q, pieces, count):
     rows = cot.shape[0]
     width = count * pieces[0].shape[1]
     return pl.pallas_call(
         functools.partial(grad_attn_kernel, count),
-        out_shape=jax.ShapeDtypeStruct((rows, width), BF16),
+        out_shape=[
+            jax.ShapeDtypeStruct((rows, width), BF16),
+            jax.ShapeDtypeStruct((2 * BLK, width), BF16),
+        ],
         name="grad_attn",
-    )(cot, *pieces)
+    )(cot, q, *pieces)
 
 
 def projected_of(attn, pieces, count):
@@ -357,18 +493,6 @@
     return keep, lax.dynamic_index_in_dim(terms, 1 - here, 0, keepdims=False).astype(BF16)
 
 
-def joined_kernel(dk_ref, dv_ref, later_ref, out_k_ref, out_v_ref):
-    rows = dk_ref.shape[0]
-    for own, out, at in ((dk_ref, out_k_ref, 0), (dv_ref, out_v_ref, BLK)):
-        out[: rows - BLK] = own[: rows - BLK].astype(BF16)
-        out[rows - BLK :] = (own[rows - BLK :] + later_ref[at : at + BLK].astype(F32)).astype(BF16)
-
-
-def joined(dk, dv, later):
-    shape = jax.ShapeDtypeStruct(dk.shape, BF16)
-    return pl.pallas_call(joined_kernel, out_shape=[shape, shape], name="joined")(dk, dv, later)
-
-
 def finish_kernel(part_k_ref, part_v_ref, own_k_ref, own_v_ref, total_ref, got_ref, out_k_ref, out_v_ref):
     del part_k_ref, part_v_ref
     first = lax.axis_index("ctx") == 0
@@ -420,12 +544,14 @@
 def spread_first(value, axis, count, order):
     mine = lax.axis_index(axis)
     covered = 0
-    for bit in order:
+    got = None
+    for place, bit in enumerate(order):
+        if place:
+            value = jnp.where((mine & order[place - 1]) != 0, got, value)
         pairs = [(one, one | bit) for one in range(count) if one & ~covered == 0]
         got = lax.ppermute(value, axis, pairs)
-        value = jnp.where((mine & bit) != 0, got, value)
         covered |= bit
-    return value
+    return value, got
 
 
 def sum_to_first(kept, sent, axis, count):
@@ -461,25 +587,28 @@
 
     last = jnp.concatenate([k[rows - BLK :], v[rows - BLK :]], axis=0)
     before = lax.ppermute(last, "ctx", [(one, one + 1) for one in range(context_count - 1)])
-    sink_k = spread_first(k[:BLK], "ctx", context_count, bits[:1] + far_first)
-    sink_v = spread_first(v[:BLK], "ctx", context_count, far_first + bits[:1])
+    order_k, order_v = bits[:1] + far_first, far_first + bits[:1]
+    last_bits = order_k[-1], order_v[-1]
+    kept_k, got_k = spread_first(k[:BLK], "ctx", context_count, order_k)
+    kept_v, got_v = spread_first(v[:BLK], "ctx", context_count, order_v)
+    sinks = kept_k, kept_v, got_k, got_v
     weights = gather_pieces(proj_weight, "dp", document_count)
     cots = gather_pieces(cot, "dp", document_count)
-    grad_attn = grad_attn_of(cot, weights, document_count)
-    attn, *away = attention_forward(
-        document_count, q, k, v, before, sink_k, sink_v, pattern
+    back = [(one + 1, one) for one in range(context_count - 1)]
+    grad_attn, following = grad_attn_of(cot, q, weights, document_count)
+    following = lax.ppermute(following, "ctx", back)
+    attn, probs, stats, *away = attention_forward(document_count, last_bits, q, k, v, before, sinks, pattern, grad_attn)
+    attns = gather_pieces(attn, "dp", document_count, away)
+    stats = lax.ppermute(stats, "ctx", back)
+    dq, dk, dv, kept, sent = attention_backward(
+        last_bits, q, k, v, before, sinks, probs, attn, grad_attn
     )
-    attns = gather_pieces(attn, "dp", document_count, away)
-    dq, dk, dv, dbefore, kept, sent = attention_backward(
-        q, k, v, before, sink_k, sink_v, pattern, attn, grad_attn
-    )
-    later = lax.ppermute(dbefore, "ctx", [(one + 1, one) for one in range(context_count - 1)])
     total, got = sum_to_first(kept, sent, "ctx", context_count)
     projected = projected_of(attn, weights, document_count)
     scale = float(rows * context_count * document_count) ** (-0.5)
     keep, send = weight_grad_of(attns, cots, scale, document_count, context_count)
     grad_proj = sum_scatter(keep, send, "ctx", context_count)
-    grad_k, grad_v = joined(dk, dv, later)
+    grad_k, grad_v = next_backward(k, v, following, stats, pattern, dk, dv)
     grad_k, grad_v = finish(grad_k, grad_v, dk, dv, total, got)
     return projected[None], dq[None], grad_k[None], grad_v[None], grad_proj
 

time: 156 us -> 148 us (0.949)
  waiting for transfers between devices: 71.7 us -> 56.5 us
  starting transfers between devices: 31.2 us -> 43.2 us
  Pallas kernels: 37.5 us -> 33.5 us
  other arithmetic: 8.16 us -> 6.29 us
    ppermute x2, waiting for transfers between devices: 18.1 us -> 8.45 us  [sum_to_first(): kept = kept + lax.ppermute(kept.astype(BF16), axis, pairs).astype(F32)]
    ppermute x6, starting transfers between devices: 14.2 us -> 22.2 us  [spread_first(): got = lax.ppermute(value, axis, pairs)]
    ppermute x6, waiting for transfers between devices: 12.8 us -> 7.09 us  [spread_first(): got = lax.ppermute(value, axis, pairs)]
    pallas_call x4, Pallas kernels: 25.1 us -> 21.1 us  [the longest x1 5.71 us: attention_forward(): pl.pallas_call(functools.partial(forward_kernel, count, last_bits), grid=...]
    ppermute x13, starting transfers between devices: 9.74 us -> 13.3 us  [swap(): return lax.ppermute(value, axis, [(one, one ^ bit) for one in range(count)])]
    select_n x6 -> x4, other arithmetic: 3.26 us -> 2.22 us  [spread_first(): value = jnp.where(mine & order[place - 1] != 0, got, value)]
    unnamed x31 -> x35, local copies, waits for them, and re-layouts: 3.98 us -> 3.88 us
  transfers between devices with their start and end apart: 24 -> 25, of which waited for: 13 -> 10; matrix products, arithmetic and copies ran while one was open for 6% -> 6% of each run, Pallas kernels for 23% -> 23%
where the time goes in v3:
time: 148 us; the launch traced here: 146 us
  waiting for transfers between devices  56.5 us (38%)
  starting transfers between devices  43.2 us (29%)
  Pallas kernels  33.5 us (23%)
  other arithmetic  6.29 us (4%)
  local copies, waits for them, and re-layouts  5.93 us (4%)
    ppermute x13, waiting for transfers between devices, swap(): return lax.ppermute(value, axis, [(one, one ^ bit) for one in range(count)])  40.3 us
    ppermute x6, starting transfers between devices, spread_first(): got = lax.ppermute(value, axis, pairs)  22.2 us
    ppermute x13, starting transfers between devices, swap(): return lax.ppermute(value, axis, [(one, one ^ bit) for one in range(count)])  13.3 us
    ppermute x2, waiting for transfers between devices, sum_to_first(): kept = kept + lax.ppermute(kept.astype(BF16), axis, pairs).astype(F32)  8.45 us
    ppermute x6, waiting for transfers between devices, spread_first(): got = lax.ppermute(value, axis, pairs)  7.09 us
    pallas_call x1, Pallas kernels, attention_forward(): pl.pallas_call(functools.partial(forward_kernel, count, last_bits), grid=...  5.71 us
    pallas_call x1, Pallas kernels, attention_backward(): pl.pallas_call(functools.partial(backward_kernel, last_bits), grid=(width...  5.6 us
    pallas_call x1, Pallas kernels, weight_grad_of(): pl.pallas_call(functools.partial(weight_grad_kernel, scale, len(attn_piec...  5.56 us
  transfers between devices with their start and end apart: 25, of which 10 were waited for; matrix products, arithmetic and copies ran while one was open for 6% of the time, Pallas kernels for 23%

profile of v3, /device:TPU:0, one launch (start us, length us, event | category | flops | bytes accessed | tf_op | source)
XLA Modules:
  0.0 146.5 jit_solution(15940361438195811536)
XLA Ops:
  0.7 3.1 %collective-permute-start.7 = (bf16[1,256,2048]{2,1,0:T(8,128)(2,1)}, bf16[1,256,2048]{2,1,0:T(8,128)(2,1)S(1)}, u32[]{:S(2)}, u32[]{:S(2)}) collective-permute-start(bf16[1,256,2048]{2,1,0:T(8,128)(2,1)} %bitcast.43), channel_id=1, source_target_pairs={{0,2},{1,3},{2,0},{3,1},{4,6},{5,7},{6,4},{7,5},{8,10},{9,11},{10,... | collective-permute-start | bytes 3145736 | tf_op jit(solution)/shard_map/ppermute | solution.py:531
  3.8 2.0 %slice_bitcast_fusion = (bf16[128,1024]{1,0:T(8,128)(2,1)}, bf16[128,1024]{1,0:T(8,128)(2,1)S(1)}, bf16[128,1024]{1,0:T(8,128)(2,1)S(1)}, bf16[128,1024]{1,0:T(8,128)(2,1)S(1)}) fusion(bf16[1,256,1024]{2,1,0:T(8,128)(2,1)} %param.8, bf16[1,256,1024]{2,1,0:T(8,128)(2,1)} %param.7), kind=kLoop, calls=%fused_computation.11 | loop fusion | bytes 2097152 | tf_op jit(solution)/shard_map/slice | solution.py:593
  5.8 3.8 %collective-permute-start.1 = (bf16[128,1024]{1,0:T(8,128)(2,1)S(1)}, bf16[128,1024]{1,0:T(8,128)(2,1)S(1)}, u32[]{:S(2)}, u32[]{:S(2)}) collective-permute-start(bf16[128,1024]{1,0:T(8,128)(2,1)S(1)} %get-tuple-element.48), channel_id=1, source_target_pairs={{0,4},{1,5},{2,6},{3,7}} | collective-permute-start | bytes 786440 | tf_op jit(solution)/shard_map/ppermute | solution.py:552
  11.5 16.4 %collective-permute-done.7.refs_3_.refs_2_ = bf16[1,256,2048]{2,1,0:T(8,128)(2,1)S(1)} collective-permute-done((bf16[1,256,2048]{2,1,0:T(8,128)(2,1)}, bf16[1,256,2048]{2,1,0:T(8,128)(2,1)S(1)}, u32[]{:S(2)}, u32[]{:S(2)}) %collective-permute-start.7) | collective-permute-done | bytes 1048608 | tf_op jit(solution)/shard_map/ppermute | solution.py:531
  29.1 5.7 %collective-permute-start.2 = (bf16[128,1024]{1,0:T(8,128)(2,1)S(1)}, bf16[128,1024]{1,0:T(8,128)(2,1)}, u32[]{:S(2)}, u32[]{:S(2)}) collective-permute-start(bf16[128,1024]{1,0:T(8,128)(2,1)S(1)} %broadcast_select_fusion.1), channel_id=1, source_target_pairs={{0,16},{4,20},{1,17},{5,21},{2,18},{6,22},{3,19},{7,23}} | collective-permute-start | bytes 786440 | tf_op jit(solution)/shard_map/ppermute | solution.py:552
  35.8 2.0 %collective-permute-start.4 = (bf16[128,1024]{1,0:T(8,128)(2,1)S(1)}, bf16[128,1024]{1,0:T(8,128)(2,1)}, u32[]{:S(2)}, u32[]{:S(2)}) collective-permute-start(bf16[128,1024]{1,0:T(8,128)(2,1)S(1)} %broadcast_select_fusion.2), channel_id=1, source_target_pairs={{0,8},{16,24},{1,9},{17,25},{2,10},{18,26},{3,11},{19,27}} | collective-permute-start | bytes 786440 | tf_op jit(solution)/shard_map/ppermute | solution.py:552
  38.7 2.1 %collective-permute-done.2 = bf16[128,1024]{1,0:T(8,128)(2,1)} collective-permute-done((bf16[128,1024]{1,0:T(8,128)(2,1)S(1)}, bf16[128,1024]{1,0:T(8,128)(2,1)}, u32[]{:S(2)}, u32[]{:S(2)}) %collective-permute-start.2) | collective-permute-done | bytes 262176 | tf_op jit(solution)/shard_map/ppermute | solution.py:552
  40.8 5.0 %collective-permute-done.4 = bf16[128,1024]{1,0:T(8,128)(2,1)} collective-permute-done((bf16[128,1024]{1,0:T(8,128)(2,1)S(1)}, bf16[128,1024]{1,0:T(8,128)(2,1)}, u32[]{:S(2)}, u32[]{:S(2)}) %collective-permute-start.4) | collective-permute-done | bytes 262176 | tf_op jit(solution)/shard_map/ppermute | solution.py:552
  47.1 2.6 %collective-permute-done.19.refs_5_ = bf16[1,256,2048]{2,1,0:T(8,128)(2,1)} collective-permute-done((bf16[1,256,2048]{2,1,0:T(8,128)(2,1)}, bf16[1,256,2048]{2,1,0:T(8,128)(2,1)}, u32[]{:S(2)}, u32[]{:S(2)}) %collective-permute-start.19) | collective-permute-done | bytes 1048608 | tf_op jit(solution)/shard_map/ppermute | solution.py:531
  49.8 4.8 %collective-permute-start.5 = (bf16[128,1024]{1,0:T(8,128)(2,1)S(1)}, bf16[128,1024]{1,0:T(8,128)(2,1)S(1)}, u32[]{:S(2)}, u32[]{:S(2)}) collective-permute-start(bf16[128,1024]{1,0:T(8,128)(2,1)S(1)} %broadcast_select_fusion.3.kept_k_ref), channel_id=1, source_target_pairs={{0,8},{4,12},{16,24},{20,28},{1,9},{5,13},{17,25},{21,29},{2,10},{... | collective-permute-start | bytes 786440 | tf_op jit(solution)/shard_map/ppermute | solution.py:552
  54.6 4.1 %collective-permute-start.6 = (bf16[128,1024]{1,0:T(8,128)(2,1)S(1)}, bf16[128,1024]{1,0:T(8,128)(2,1)}, u32[]{:S(2)}, u32[]{:S(2)}) collective-permute-start(bf16[128,1024]{1,0:T(8,128)(2,1)S(1)} %broadcast_select_fusion.kept_v_ref), channel_id=1, source_target_pairs={{0,4},{8,12},{16,20},{24,28},{1,5},{9,13},{17,21},{25,29},{2,6},{1... | collective-permute-start | bytes 786440 | tf_op jit(solution)/shard_map/ppermute | solution.py:552
  59.4 5.0 %grad_attn.1 = (bf16[256,1024]{1,0:T(8,128)(2,1)}, bf16[256,1024]{1,0:T(8,128)(2,1)}) custom-call(bf16[256,2048]{1,0:T(8,128)(2,1)} %bitcast.42, bf16[256,1024]{1,0:T(8,128)(2,1)} %bitcast.38, bf16[1,256,2048]{2,1,0:T(8,128)(2,1)} %bitcast.45, bf16[1,256,2048]{2,1,0:T(8,128)(2,1)} %copy-done.2, bf16[1,256,2048]{2,1,0:T(8,128)(2,1)} %collective-permute-done.8.refs_4_.refs_3_, ...), custom_call_target="tpu_custom_call" | custom-call | tf_op jit(solution)/shard_map/grad_attn/pallas_call | solution.py:427
  65.3 5.7 %attention_forward.1 = (bf16[256,1024]{1,0:T(8,128)(2,1)}, f32[8,256,384]{2,1,0:T(8,128)}, f32[128,128]{1,0:T(8,128)}, bf16[1,256,512]{2,1,0:T(8,128)(2,1)}, bf16[1,256,256]{2,1,0:T(8,128)(2,1)}) custom-call(bf16[256,1024]{1,0:T(8,128)(2,1)} %bitcast.39, bf16[256,1024]{1,0:T(8,128)(2,1)} %bitcast.32, bf16[256,1024]{1,0:T(8,128)(2,1)} %bitcast.35, ...), custom_call_target="tpu_custom_call" | custom-call | tf_op jit(solution)/shard_map/attention_forward/pallas_call | solution.py:277
  72.6 6.8 %collective-permute-done.16.refs_1_ = bf16[1,256,512]{2,1,0:T(8,128)(2,1)S(1)} collective-permute-done((bf16[1,256,512]{2,1,0:T(8,128)(2,1)}, bf16[1,256,512]{2,1,0:T(8,128)(2,1)S(1)}, u32[]{:S(2)}, u32[]{:S(2)}) %collective-permute-start.16) | collective-permute-done | bytes 262176 | tf_op jit(solution)/shard_map/ppermute | solution.py:531
  79.4 5.6 %attention_backward.1 = (bf16[256,1024]{1,0:T(8,128)(2,1)}, f32[256,1024]{1,0:T(8,128)}, f32[256,1024]{1,0:T(8,128)}, f32[128,1024]{1,0:T(8,128)}, bf16[128,1024]{1,0:T(8,128)(2,1)}) custom-call(bf16[256,1024]{1,0:T(8,128)(2,1)} %bitcast.40, bf16[256,1024]{1,0:T(8,128)(2,1)} %bitcast.33, bf16[256,1024]{1,0:T(8,128)(2,1)} %bitcast.36, ...), custom_call_target="tpu_custom_call" | custom-call | tf_op jit(solution)/shard_map/attention_backward/pallas_call | solution.py:305
  85.0 2.5 %collective-permute-start.12 = (bf16[128,1024]{1,0:T(8,128)(2,1)}, bf16[128,1024]{1,0:T(8,128)(2,1)S(1)}, u32[]{:S(2)}, u32[]{:S(2)}) collective-permute-start(bf16[128,1024]{1,0:T(8,128)(2,1)} %get-tuple-element.34), channel_id=1, source_target_pairs={{0,4},{4,0},{8,12},{12,8},{16,20},{20,16},{24,28},{28,24},{1,5},{5... | collective-permute-start | bytes 786440 | tf_op jit(solution)/shard_map/ppermute | solution.py:531
  89.6 5.6 %weight_grad.1 = (f32[4,256,256]{2,1,0:T(8,128)}, bf16[4,256,256]{2,1,0:T(8,128)(2,1)}) custom-call(bf16[1,256,1024]{2,1,0:T(8,128)(2,1)} %bitcast.41, bf16[1,256,512]{2,1,0:T(8,128)(2,1)} %copy-done.9, bf16[1,256,256]{2,1,0:T(8,128)(2,1)} %copy-done.11, bf16[1,256,512]{2,1,0:T(8,128)(2,1)} %copy-done.10, bf16[1,256,2048]{2,1,0:T(8,128)(2,1)} %refs_4_.1, ...), custom_call_target="tpu_custom_call" | custom-call | tf_op jit(solution)/shard_map/weight_grad/pallas_call | solution.py:457
  98.0 8.5 %collective-permute-done.13 = bf16[128,1024]{1,0:T(8,128)(2,1)S(1)} collective-permute-done((bf16[128,1024]{1,0:T(8,128)(2,1)S(1)}, bf16[128,1024]{1,0:T(8,128)(2,1)S(1)}, u32[]{:S(2)}, u32[]{:S(2)}) %collective-permute-start.13) | collective-permute-done | bytes 262176 | tf_op jit(solution)/shard_map/ppermute | solution.py:563
  107.9 9.5 %collective-permute-done.22 = bf16[2,2,256,256]{3,2,1,0:T(8,128)(2,1)S(1)} collective-permute-done((bf16[2,2,256,256]{3,2,1,0:T(8,128)(2,1)}, bf16[2,2,256,256]{3,2,1,0:T(8,128)(2,1)S(1)}, u32[]{:S(2)}, u32[]{:S(2)}) %collective-permute-start.22) | collective-permute-done | bytes 524320 | tf_op jit(solution)/shard_map/ppermute | solution.py:531
  118.8 3.9 %collective-permute-start.23 = (bf16[2,256,256]{2,1,0:T(8,128)(2,1)S(1)}, bf16[2,256,256]{2,1,0:T(8,128)(2,1)S(1)}, u32[]{:S(2)}, u32[]{:S(2)}) collective-permute-start(bf16[2,256,256]{2,1,0:T(8,128)(2,1)S(1)} %fusion.1), channel_id=1, source_target_pairs={{0,8},{4,12},{8,0},{12,4},{16,24},{20,28},{24,16},{28,20},{1,9},{5... | collective-permute-start | bytes 786440 | tf_op jit(solution)/shard_map/ppermute | solution.py:531
  124.9 3.8 %collective-permute-done.23 = bf16[2,256,256]{2,1,0:T(8,128)(2,1)S(1)} collective-permute-done((bf16[2,256,256]{2,1,0:T(8,128)(2,1)S(1)}, bf16[2,256,256]{2,1,0:T(8,128)(2,1)S(1)}, u32[]{:S(2)}, u32[]{:S(2)}) %collective-permute-start.23) | collective-permute-done | bytes 262176 | tf_op jit(solution)/shard_map/ppermute | solution.py:531
  131.8 4.6 %projected.1 = bf16[256,2048]{1,0:T(8,128)(2,1)} custom-call(bf16[256,1024]{1,0:T(8,128)(2,1)} %get-tuple-element.24.refs_0_.attn_ref, bf16[1,256,2048]{2,1,0:T(8,128)(2,1)} %bitcast.46, bf16[1,256,2048]{2,1,0:T(8,128)(2,1)} %copy-done.2, bf16[1,256,2048]{2,1,0:T(8,128)(2,1)} %collective-permute-done.8.refs_4_.refs_3_, ...), custom_call_target="tpu_custom_call" | custom-call | tf_op jit(solution)/shard_map/projected/pallas_call | solution.py:438
  137.9 4.9 %next_backward.1 = (bf16[256,1024]{1,0:T(8,128)(2,1)}, bf16[256,1024]{1,0:T(8,128)(2,1)}) custom-call(bf16[256,1024]{1,0:T(8,128)(2,1)} %bitcast.34, bf16[256,1024]{1,0:T(8,128)(2,1)} %bitcast.37, bf16[256,1024]{1,0:T(8,128)(2,1)} %copy-done.7, f32[128,128]{1,0:T(8,128)} %copy-done.12, s32[1,8,16,2]{3,2,1,0:T(8,128)} %copy.13.pattern_ref, ...), custom_call_target="tpu_custom_call" | custom-call | tf_op jit(solution)/shard_map/next_backward/pallas_call | solution.py:335
  143.4 2.3 %finish.1 = (bf16[256,1024]{1,0:T(8,128)(2,1)}, bf16[256,1024]{1,0:T(8,128)(2,1)}) custom-call(bf16[256,1024]{1,0:T(8,128)(2,1)} %get-tuple-element.31.part_k_ref, bf16[256,1024]{1,0:T(8,128)(2,1)} %get-tuple-element.32.part_v_ref, f32[256,1024]{1,0:T(8,128)} %get-tuple-element.29.dk_ref.own_k_ref, ...), custom_call_target="tpu_custom_call", output_to_operand_aliasing={{0}: (0, {}), {1}: (1, {})} | custom-call | tf_op jit(solution)/shard_map/finish/pallas_call | solution.py:508
  (82 shorter events, 25.5 us)
Async XLA Ops:
  0.7 27.3 %collective-permute-start.7 = (bf16[1,256,2048]{2,1,0:T(8,128)(2,1)}, bf16[1,256,2048]{2,1,0:T(8,128)(2,1)S(1)}, u32[]{:S(2)}, u32[]{:S(2)}) collective-permute-start(bf16[1,256,2048]{2,1,0:T(8,128)(2,1)} %bitcast.43), channel_id=1, source_target_pairs={{0,2},{1,3},{2,0},{3,1},{4,6},{5,7},{6,4},{7,5},{8,10},{9,11},{10,... | collective-permute-start | bytes 3145736 | tf_op jit(solution)/shard_map/ppermute | solution.py:531
  3.7 45.9 %collective-permute-start.19 = (bf16[1,256,2048]{2,1,0:T(8,128)(2,1)}, bf16[1,256,2048]{2,1,0:T(8,128)(2,1)}, u32[]{:S(2)}, u32[]{:S(2)}) collective-permute-start(bf16[1,256,2048]{2,1,0:T(8,128)(2,1)} %refs_4_.1), channel_id=1, source_target_pairs={{0,2},{1,3},{2,0},{3,1},{4,6},{5,7},{6,4},{7,5},{8,10},{9,11},{10,... | collective-permute-start | bytes 3145736 | tf_op jit(solution)/shard_map/ppermute | solution.py:531
  5.8 22.2 %collective-permute-start.1 = (bf16[128,1024]{1,0:T(8,128)(2,1)S(1)}, bf16[128,1024]{1,0:T(8,128)(2,1)S(1)}, u32[]{:S(2)}, u32[]{:S(2)}) collective-permute-start(bf16[128,1024]{1,0:T(8,128)(2,1)S(1)} %get-tuple-element.48), channel_id=1, source_target_pairs={{0,4},{1,5},{2,6},{3,7}} | collective-permute-start | bytes 786440 | tf_op jit(solution)/shard_map/ppermute | solution.py:552
  9.6 25.2 %collective-permute-start.3 = (bf16[128,1024]{1,0:T(8,128)(2,1)}, bf16[128,1024]{1,0:T(8,128)(2,1)S(1)}, u32[]{:S(2)}, u32[]{:S(2)}) collective-permute-start(bf16[128,1024]{1,0:T(8,128)(2,1)} %get-tuple-element.43), channel_id=1, source_target_pairs={{0,16},{1,17},{2,18},{3,19}} | collective-permute-start | bytes 786440 | tf_op jit(solution)/shard_map/ppermute | solution.py:552
  11.4 38.4 %collective-permute-start.8 = (bf16[1,256,2048]{2,1,0:T(8,128)(2,1)}, bf16[1,256,2048]{2,1,0:T(8,128)(2,1)}, u32[]{:S(2)}, u32[]{:S(2)}) collective-permute-start(bf16[1,256,2048]{2,1,0:T(8,128)(2,1)} %bitcast.44), channel_id=1, source_target_pairs={{0,1},{1,0},{2,3},{3,2},{4,5},{5,4},{6,7},{7,6},{8,9},{9,8},{10,11... | collective-permute-start | bytes 3145736 | tf_op jit(solution)/shard_map/ppermute | solution.py:531
  27.9 26.6 %collective-permute-start.9 = (bf16[1,256,2048]{2,1,0:T(8,128)(2,1)S(1)}, bf16[1,256,2048]{2,1,0:T(8,128)(2,1)}, u32[]{:S(2)}, u32[]{:S(2)}) collective-permute-start(bf16[1,256,2048]{2,1,0:T(8,128)(2,1)S(1)} %collective-permute-done.7.refs_3_.refs_2_), channel_id=1, source_target_pairs={{0,1},{1,0},{2,3},{3,2},{4,5},{5,4},{6,7},{7,6},{8,9},{9,8},{10,11... | collective-permute-start | bytes 3145736 | tf_op jit(solution)/shard_map/ppermute | solution.py:531
  29.1 11.7 %collective-permute-start.2 = (bf16[128,1024]{1,0:T(8,128)(2,1)S(1)}, bf16[128,1024]{1,0:T(8,128)(2,1)}, u32[]{:S(2)}, u32[]{:S(2)}) collective-permute-start(bf16[128,1024]{1,0:T(8,128)(2,1)S(1)} %broadcast_select_fusion.1), channel_id=1, source_target_pairs={{0,16},{4,20},{1,17},{5,21},{2,18},{6,22},{3,19},{7,23}} | collective-permute-start | bytes 786440 | tf_op jit(solution)/shard_map/ppermute | solution.py:552
  35.8 9.9 %collective-permute-start.4 = (bf16[128,1024]{1,0:T(8,128)(2,1)S(1)}, bf16[128,1024]{1,0:T(8,128)(2,1)}, u32[]{:S(2)}, u32[]{:S(2)}) collective-permute-start(bf16[128,1024]{1,0:T(8,128)(2,1)S(1)} %broadcast_select_fusion.2), channel_id=1, source_target_pairs={{0,8},{16,24},{1,9},{17,25},{2,10},{18,26},{3,11},{19,27}} | collective-permute-start | bytes 786440 | tf_op jit(solution)/shard_map/ppermute | solution.py:552
  40.8 46.9 %collective-permute-start.20 = (bf16[1,256,2048]{2,1,0:T(8,128)(2,1)S(1)}, bf16[1,256,2048]{2,1,0:T(8,128)(2,1)}, u32[]{:S(2)}, u32[]{:S(2)}) collective-permute-start(bf16[1,256,2048]{2,1,0:T(8,128)(2,1)S(1)} %copy-done.1), channel_id=1, source_target_pairs={{0,1},{1,0},{2,3},{3,2},{4,5},{5,4},{6,7},{7,6},{8,9},{9,8},{10,11... | collective-permute-start | bytes 3145736 | tf_op jit(solution)/shard_map/ppermute | solution.py:531
  45.8 18.6 %collective-permute-start = (bf16[256,1024]{1,0:T(8,128)(2,1)}, bf16[256,1024]{1,0:T(8,128)(2,1)S(1)}, u32[]{:S(2)}, u32[]{:S(2)}) collective-permute-start(bf16[256,1024]{1,0:T(8,128)(2,1)} %pad_maximum_fusion), channel_id=1, source_target_pairs={{0,4},{4,8},{8,12},{12,16},{16,20},{20,24},{24,28},{1,5},{5,9},{9,... | collective-permute-start | bytes 1572872 | tf_op jit(solution)/shard_map/ppermute | solution.py:589
  49.7 38.0 %collective-permute-start.21 = (bf16[1,256,2048]{2,1,0:T(8,128)(2,1)}, bf16[1,256,2048]{2,1,0:T(8,128)(2,1)}, u32[]{:S(2)}, u32[]{:S(2)}) collective-permute-start(bf16[1,256,2048]{2,1,0:T(8,128)(2,1)} %collective-permute-done.19.refs_5_), channel_id=1, source_target_pairs={{0,1},{1,0},{2,3},{3,2},{4,5},{5,4},{6,7},{7,6},{8,9},{9,8},{10,11... | collective-permute-start | bytes 3145736 | tf_op jit(solution)/shard_map/ppermute | solution.py:531
  49.8 14.6 %collective-permute-start.5 = (bf16[128,1024]{1,0:T(8,128)(2,1)S(1)}, bf16[128,1024]{1,0:T(8,128)(2,1)S(1)}, u32[]{:S(2)}, u32[]{:S(2)}) collective-permute-start(bf16[128,1024]{1,0:T(8,128)(2,1)S(1)} %broadcast_select_fusion.3.kept_k_ref), channel_id=1, source_target_pairs={{0,8},{4,12},{16,24},{20,28},{1,9},{5,13},{17,25},{21,29},{2,10},{... | collective-permute-start | bytes 786440 | tf_op jit(solution)/shard_map/ppermute | solution.py:552
  54.6 9.9 %collective-permute-start.6 = (bf16[128,1024]{1,0:T(8,128)(2,1)S(1)}, bf16[128,1024]{1,0:T(8,128)(2,1)}, u32[]{:S(2)}, u32[]{:S(2)}) collective-permute-start(bf16[128,1024]{1,0:T(8,128)(2,1)S(1)} %broadcast_select_fusion.kept_v_ref), channel_id=1, source_target_pairs={{0,4},{8,12},{16,20},{24,28},{1,5},{9,13},{17,21},{25,29},{2,6},{1... | collective-permute-start | bytes 786440 | tf_op jit(solution)/shard_map/ppermute | solution.py:552
  71.0 8.4 %collective-permute-start.16 = (bf16[1,256,512]{2,1,0:T(8,128)(2,1)}, bf16[1,256,512]{2,1,0:T(8,128)(2,1)S(1)}, u32[]{:S(2)}, u32[]{:S(2)}) collective-permute-start(bf16[1,256,512]{2,1,0:T(8,128)(2,1)} %get-tuple-element.37), channel_id=1, source_target_pairs={{0,2},{1,3},{2,0},{3,1},{4,6},{5,7},{6,4},{7,5},{8,10},{9,11},{10,... | collective-permute-start | bytes 786440 | tf_op jit(solution)/shard_map/ppermute | solution.py:531
  79.4 9.5 %collective-permute-start.18 = (bf16[1,256,512]{2,1,0:T(8,128)(2,1)S(1)}, bf16[1,256,512]{2,1,0:T(8,128)(2,1)S(1)}, u32[]{:S(2)}, u32[]{:S(2)}) collective-permute-start(bf16[1,256,512]{2,1,0:T(8,128)(2,1)S(1)} %collective-permute-done.16.refs_1_), channel_id=1, source_target_pairs={{0,1},{1,0},{2,3},{3,2},{4,5},{5,4},{6,7},{7,6},{8,9},{9,8},{10,11... | collective-permute-start | bytes 786440 | tf_op jit(solution)/shard_map/ppermute | solution.py:531
  85.0 10.3 %collective-permute-start.12 = (bf16[128,1024]{1,0:T(8,128)(2,1)}, bf16[128,1024]{1,0:T(8,128)(2,1)S(1)}, u32[]{:S(2)}, u32[]{:S(2)}) collective-permute-start(bf16[128,1024]{1,0:T(8,128)(2,1)} %get-tuple-element.34), channel_id=1, source_target_pairs={{0,4},{4,0},{8,12},{12,8},{16,20},{20,16},{24,28},{28,24},{1,5},{5... | collective-permute-start | bytes 786440 | tf_op jit(solution)/shard_map/ppermute | solution.py:531
  95.2 22.1 %collective-permute-start.22 = (bf16[2,2,256,256]{3,2,1,0:T(8,128)(2,1)}, bf16[2,2,256,256]{3,2,1,0:T(8,128)(2,1)S(1)}, u32[]{:S(2)}, u32[]{:S(2)}) collective-permute-start(bf16[2,2,256,256]{3,2,1,0:T(8,128)(2,1)} %bitcast.52), channel_id=1, source_target_pairs={{0,4},{4,0},{8,12},{12,8},{16,20},{20,16},{24,28},{28,24},{1,5},{5... | collective-permute-start | bytes 1572872 | tf_op jit(solution)/shard_map/ppermute | solution.py:531
  95.4 11.1 %collective-permute-start.13 = (bf16[128,1024]{1,0:T(8,128)(2,1)S(1)}, bf16[128,1024]{1,0:T(8,128)(2,1)S(1)}, u32[]{:S(2)}, u32[]{:S(2)}) collective-permute-start(bf16[128,1024]{1,0:T(8,128)(2,1)S(1)} %fusion), channel_id=1, source_target_pairs={{8,0},{12,4},{24,16},{28,20},{9,1},{13,5},{25,17},{29,21},{10,2},{... | collective-permute-start | bytes 786440 | tf_op jit(solution)/shard_map/ppermute | solution.py:563
  96.7 40.4 %collective-permute-start.10 = (bf16[256,1024]{1,0:T(8,128)(2,1)S(1)}, bf16[256,1024]{1,0:T(8,128)(2,1)S(1)}, u32[]{:S(2)}, u32[]{:S(2)}) collective-permute-start(bf16[256,1024]{1,0:T(8,128)(2,1)S(1)} %copy-done.14), channel_id=1, source_target_pairs={{4,0},{8,4},{12,8},{16,12},{20,16},{24,20},{28,24},{5,1},{9,5},{13... | collective-permute-start | bytes 1572872 | tf_op jit(solution)/shard_map/ppermute | solution.py:599
  106.6 16.1 %collective-permute-start.14 = (bf16[128,1024]{1,0:T(8,128)(2,1)S(1)}, bf16[128,1024]{1,0:T(8,128)(2,1)S(1)}, u32[]{:S(2)}, u32[]{:S(2)}) collective-permute-start(bf16[128,1024]{1,0:T(8,128)(2,1)S(1)} %fusion.2), channel_id=1, source_target_pairs={{16,0},{20,4},{17,1},{21,5},{18,2},{22,6},{19,3},{23,7}} | collective-permute-start | bytes 786440 | tf_op jit(solution)/shard_map/ppermute | solution.py:563
  118.8 9.9 %collective-permute-start.23 = (bf16[2,256,256]{2,1,0:T(8,128)(2,1)S(1)}, bf16[2,256,256]{2,1,0:T(8,128)(2,1)S(1)}, u32[]{:S(2)}, u32[]{:S(2)}) collective-permute-start(bf16[2,256,256]{2,1,0:T(8,128)(2,1)S(1)} %fusion.1), channel_id=1, source_target_pairs={{0,8},{4,12},{8,0},{12,4},{16,24},{20,28},{24,16},{28,20},{1,9},{5... | collective-permute-start | bytes 786440 | tf_op jit(solution)/shard_map/ppermute | solution.py:531
  123.6 19.1 %collective-permute-start.15 = (bf16[128,1024]{1,0:T(8,128)(2,1)S(1)}, bf16[128,1024]{1,0:T(8,128)(2,1)S(1)}, u32[]{:S(2)}, u32[]{:S(2)}) collective-permute-start(bf16[128,1024]{1,0:T(8,128)(2,1)S(1)} %get-tuple-element.41), channel_id=1, source_target_pairs={{4,0},{5,1},{6,2},{7,3}} | collective-permute-start | bytes 786440 | tf_op jit(solution)/shard_map/ppermute | solution.py:565
  128.7 17.0 %collective-permute-start.24 = (bf16[256,256]{1,0:T(8,128)(2,1)S(1)}, bf16[256,256]{1,0:T(8,128)(2,1)S(1)}, u32[]{:S(2)}, u32[]{:S(2)}) collective-permute-start(bf16[256,256]{1,0:T(8,128)(2,1)S(1)} %fusion.3), channel_id=1, source_target_pairs={{0,16},{4,20},{8,24},{12,28},{16,0},{20,4},{24,8},{28,12},{1,17},{... | collective-permute-start | bytes 393224 | tf_op jit(solution)/shard_map/ppermute | solution.py:531
  130.6 6.5 %collective-permute-start.11 = (f32[128,128]{1,0:T(8,128)S(1)}, f32[128,128]{1,0:T(8,128)S(1)}, u32[]{:S(2)}, u32[]{:S(2)}) collective-permute-start(f32[128,128]{1,0:T(8,128)S(1)} %copy-done.16), channel_id=1, source_target_pairs={{4,0},{8,4},{12,8},{16,12},{20,16},{24,20},{28,24},{5,1},{9,5},{13... | collective-permute-start | bytes 196616 | tf_op jit(solution)/shard_map/ppermute | solution.py:602
  (18 other events, 209.9 us)

commit v4 on v3

--- a/solution.py
+++ b/solution.py
@@ -211,13 +211,11 @@
 
 
 def next_kernel(
-    k_ref, v_ref, next_ref, stats_ref, pattern_ref, dk_ref, dv_ref, out_k_ref, out_v_ref
+    blocks, k_ref, v_ref, next_ref, stats_ref, pattern_ref, dk_ref, dv_ref, out_k_ref, out_v_ref
 ):
-    rows = k_ref.shape[0]
-    last = slice(rows - BLK, rows)
     heads = k_ref.shape[1] // HDIM
     total_heads = pl.num_programs(0) * heads
-    block = (lax.axis_index("ctx") + 1) * (rows // BLK)
+    block = (lax.axis_index("ctx") + 1) * blocks
     inside = jnp.minimum(block, pattern_ref.shape[2] - 1)
     lane = lax.broadcasted_iota(jnp.int32, (BLK, BLK), 1)
     stats = stats_ref[...]
@@ -230,18 +228,42 @@
         head = pl.program_id(0) * heads + local
         top, inverse, delta = (column(head + kind * total_heads) for kind in range(3))
         q, grad = next_ref[:BLK, cols], next_ref[BLK:, cols]
-        scores = dot(q, k_ref[last, cols], 1, 1)
+        scores = dot(q, k_ref[:, cols], 1, 1)
         reached = jnp.logical_and(pattern_ref[0, head, inside, 1] == 1, block >= 2)
         probs = jnp.exp2((scores - top) * (ROOT * LOG2_E)) * inverse
         probs = jnp.where(reached, probs, 0.0)
-        dprobs = dot(grad, v_ref[last, cols], 1, 1)
+        dprobs = dot(grad, v_ref[:, cols], 1, 1)
         dscores = (probs * (dprobs - delta)).astype(BF16)
-        dk = dk_ref[last, cols] + dot(dscores, q, 0, 0) * ROOT
-        dv = dv_ref[last, cols] + dot(probs.astype(BF16), grad, 0, 0)
-        out_k_ref[last, cols] = dk.astype(BF16)
-        out_v_ref[last, cols] = dv.astype(BF16)
-    out_k_ref[: rows - BLK] = dk_ref[: rows - BLK].astype(BF16)
-    out_v_ref[: rows - BLK] = dv_ref[: rows - BLK].astype(BF16)
+        dk = dk_ref[:, cols] + dot(dscores, q, 0, 0) * ROOT
+        dv = dv_ref[:, cols] + dot(probs.astype(BF16), grad, 0, 0)
+        out_k_ref[:, cols] = dk.astype(BF16)
+        out_v_ref[:, cols] = dv.astype(BF16)
+
+
+def ends_kernel(k_first_ref, v_first_ref, k_last_ref, v_last_ref, k_ref, v_ref, last_ref):
+    k_ref[...] = k_first_ref[...]
+    v_ref[...] = v_first_ref[...]
+    last_ref[:BLK] = k_last_ref[...]
+    last_ref[BLK:] = v_last_ref[...]
+
+
+def ends_of(k, v):
+    rows, width = k.shape
+    first = pl.BlockSpec((BLK, width), lambda step: (0, 0))
+    last = pl.BlockSpec((BLK, width), lambda step: (rows // BLK - 1, 0))
+    shape = jax.ShapeDtypeStruct
+    return pl.pallas_call(
+        ends_kernel,
+        grid=(1,),
+        in_specs=[first, first, last, last],
+        out_specs=[first, first, pl.BlockSpec((2 * BLK, width), lambda step: (0, 0))],
+        out_shape=[
+            shape((BLK, width), BF16),
+            shape((BLK, width), BF16),
+            shape((2 * BLK, width), BF16),
+        ],
+        name="ends",
+    )(k, v, k, v)
 
 
 def head_spec(rows):
@@ -331,20 +353,22 @@
 
 def next_backward(k, v, following, stats, pattern, dk, dv):
     rows, width = k.shape
+    blocks = rows // BLK
     shape = jax.ShapeDtypeStruct((rows, width), BF16)
-    return pl.pallas_call(
-        next_kernel,
+    last = pl.BlockSpec((BLK, HEADS_STEP * HDIM), lambda step: (blocks - 1, step))
+    return pl.pallas_call(
+        functools.partial(next_kernel, blocks),
         grid=(width // (HEADS_STEP * HDIM),),
         in_specs=[
-            head_spec(rows),
-            head_spec(rows),
+            last,
+            last,
             head_spec(2 * BLK),
             pl.BlockSpec((BLK, BLK), lambda step: (0, 0)),
             whole_smem(pattern.shape),
-            head_spec(rows),
-            head_spec(rows),
-        ],
-        out_specs=[head_spec(rows), head_spec(rows)],
+            last,
+            last,
+        ],
+        out_specs=[last, last],
         out_shape=[shape, shape],
         name="next_backward",
     )(k, v, following, stats, pattern, dk, dv)
@@ -457,7 +481,7 @@
     return pl.pallas_call(
         functools.partial(weight_grad_kernel, scale, len(attn_pieces)),
         grid=(count // 2,),
-        in_specs=[pl.BlockSpec(a.shape, lambda step: (0, 0, 0)) for a in attn_pieces]
+        in_specs=[pl.BlockSpec(memory_space=pltpu.VMEM) for _ in attn_pieces]
         + [pl.BlockSpec(c.shape[:2] + (2 * wanted,), lambda step: (0, 0, step)) for c in cot_pieces],
         out_specs=[out, out],
         out_shape=[
@@ -495,20 +519,21 @@
 
 def finish_kernel(part_k_ref, part_v_ref, own_k_ref, own_v_ref, total_ref, got_ref, out_k_ref, out_v_ref):
     del part_k_ref, part_v_ref
-    first = lax.axis_index("ctx") == 0
+    first = jnp.logical_and(lax.axis_index("ctx") == 0, pl.program_id(0) == 0)
     out_k_ref[...] = (own_k_ref[...] + jnp.where(first, total_ref[...], 0.0)).astype(BF16)
     out_v_ref[...] = (own_v_ref[...] + jnp.where(first, got_ref[...].astype(F32), 0.0)).astype(BF16)
 
 
 def finish(part_k, part_v, own_k, own_v, total, got):
-    width = own_k.shape[1]
-    block = pl.BlockSpec((BLK, width), lambda step: (0, 0))
+    rows, width = own_k.shape
+    block = pl.BlockSpec((BLK, width), lambda step: (step, 0))
+    same = pl.BlockSpec((BLK, width), lambda step: (0, 0))
     whole = pl.BlockSpec(memory_space=pl.ANY)
     shape = jax.ShapeDtypeStruct(part_k.shape, BF16)
     return pl.pallas_call(
         finish_kernel,
-        grid=(1,),
-        in_specs=[whole, whole, block, block, block, block],
+        grid=(rows // BLK - 1,),
+        in_specs=[whole, whole, block, block, same, pl.BlockSpec(memory_space=pltpu.VMEM)],
         out_specs=[block, block],
         out_shape=[shape, shape],
         input_output_aliases={0: 0, 1: 1},
@@ -585,12 +610,12 @@
     bits = bits_of(context_count)
     far_first = bits[:0:-1]
 
-    last = jnp.concatenate([k[rows - BLK :], v[rows - BLK :]], axis=0)
+    first_k, first_v, last = ends_of(k, v)
     before = lax.ppermute(last, "ctx", [(one, one + 1) for one in range(context_count - 1)])
     order_k, order_v = bits[:1] + far_first, far_first + bits[:1]
     last_bits = order_k[-1], order_v[-1]
-    kept_k, got_k = spread_first(k[:BLK], "ctx", context_count, order_k)
-    kept_v, got_v = spread_first(v[:BLK], "ctx", context_count, order_v)
+    kept_k, got_k = spread_first(first_k, "ctx", context_count, order_k)
+    kept_v, got_v = spread_first(first_v, "ctx", context_count, order_v)
     sinks = kept_k, kept_v, got_k, got_v
     weights = gather_pieces(proj_weight, "dp", document_count)
     cots = gather_pieces(cot, "dp", document_count)

time: 148 us -> 148 us (level)
  Pallas kernels: 33.5 us -> 35.6 us
  waiting for transfers between devices: 56.5 us -> 58.1 us
  local copies, waits for them, and re-layouts: 5.93 us -> 4.44 us
    ppermute x6, waiting for transfers between devices: 7.09 us -> 9.52 us  [spread_first(): got = lax.ppermute(value, axis, pairs)]
    pallas_call x2 -> x3, Pallas kernels: 7.15 us -> 9.23 us  [the longest x1 4.76 us: next_backward(): pl.pallas_call(functools.partial(next_kernel, blocks), grid=(width // (HE...]
    slice x1 -> x0, local copies, waits for them, and re-layouts: 1.99 us -> none  [body(): kept_v, got_v = spread_first(v[:BLK], 'ctx', context_count, order_v)]
    unnamed x35 -> x39, local copies, waits for them, and re-layouts: 3.88 us -> 4.38 us
  transfers between devices with their start and end apart: 25 -> 25, of which waited for: 10 -> 11; matrix products, arithmetic and copies ran while one was open for 6% -> 4% of each run, Pallas kernels for 23% -> 24%
where the time goes in v4:
time: 148 us; the launch traced here: 146 us
  waiting for transfers between devices  58.1 us (39%)
  starting transfers between devices  41.8 us (28%)
  Pallas kernels  35.6 us (24%)
  other arithmetic  5.51 us (4%)
  local copies, waits for them, and re-layouts  4.44 us (3%)
    ppermute x13, waiting for transfers between devices, swap(): return lax.ppermute(value, axis, [(one, one ^ bit) for one in range(count)])  39.4 us
    ppermute x6, starting transfers between devices, spread_first(): got = lax.ppermute(value, axis, pairs)  20.8 us
    ppermute x13, starting transfers between devices, swap(): return lax.ppermute(value, axis, [(one, one ^ bit) for one in range(count)])  13.3 us
    ppermute x6, waiting for transfers between devices, spread_first(): got = lax.ppermute(value, axis, pairs)  9.52 us
    ppermute x2, waiting for transfers between devices, sum_to_first(): kept = kept + lax.ppermute(kept.astype(BF16), axis, pairs).astype(F32)  8.45 us
    pallas_call x1, Pallas kernels, attention_forward(): pl.pallas_call(functools.partial(forward_kernel, count, last_bits), grid=...  5.71 us
    pallas_call x1, Pallas kernels, attention_backward(): pl.pallas_call(functools.partial(backward_kernel, last_bits), grid=(width...  5.59 us
    pallas_call x1, Pallas kernels, weight_grad_of(): pl.pallas_call(functools.partial(weight_grad_kernel, scale, len(attn_piec...  5.56 us
  transfers between devices with their start and end apart: 25, of which 11 were waited for; matrix products, arithmetic and copies ran while one was open for 4% of the time, Pallas kernels for 24%

profile of v4, /device:TPU:0, one launch (start us, length us, event | category | flops | bytes accessed | tf_op | source)
XLA Modules:
  0.0 146.4 jit_solution(15741227150680263667)
XLA Ops:
  0.7 3.1 %collective-permute-start.7 = (bf16[1,256,2048]{2,1,0:T(8,128)(2,1)}, bf16[1,256,2048]{2,1,0:T(8,128)(2,1)S(1)}, u32[]{:S(2)}, u32[]{:S(2)}) collective-permute-start(bf16[1,256,2048]{2,1,0:T(8,128)(2,1)} %bitcast.35), channel_id=1, source_target_pairs={{0,2},{1,3},{2,0},{3,1},{4,6},{5,7},{6,4},{7,5},{8,10},{9,11},{10,... | collective-permute-start | bytes 3145736 | tf_op jit(solution)/shard_map/ppermute | solution.py:556
  3.8 2.2 %ends.1 = (bf16[128,1024]{1,0:T(8,128)(2,1)}, bf16[128,1024]{1,0:T(8,128)(2,1)}, bf16[256,1024]{1,0:T(8,128)(2,1)}) custom-call(bf16[256,1024]{1,0:T(8,128)(2,1)} %bitcast.20, bf16[256,1024]{1,0:T(8,128)(2,1)} %bitcast.25, bf16[256,1024]{1,0:T(8,128)(2,1)} %bitcast.21, bf16[256,1024]{1,0:T(8,128)(2,1)} %bitcast.26), custom_call_target="tpu_custom_call" | custom-call | tf_op jit(solution)/shard_map/ends/pallas_call | solution.py:255
  6.0 3.8 %collective-permute-start.1 = (bf16[128,1024]{1,0:T(8,128)(2,1)}, bf16[128,1024]{1,0:T(8,128)(2,1)S(1)}, u32[]{:S(2)}, u32[]{:S(2)}) collective-permute-start(bf16[128,1024]{1,0:T(8,128)(2,1)} %get-tuple-element.27), channel_id=1, source_target_pairs={{0,4},{1,5},{2,6},{3,7}} | collective-permute-start | bytes 786440 | tf_op jit(solution)/shard_map/ppermute | solution.py:577
  9.8 1.8 %collective-permute-start.3 = (bf16[128,1024]{1,0:T(8,128)(2,1)}, bf16[128,1024]{1,0:T(8,128)(2,1)S(1)}, u32[]{:S(2)}, u32[]{:S(2)}) collective-permute-start(bf16[128,1024]{1,0:T(8,128)(2,1)} %get-tuple-element.28), channel_id=1, source_target_pairs={{0,16},{1,17},{2,18},{3,19}} | collective-permute-start | bytes 786440 | tf_op jit(solution)/shard_map/ppermute | solution.py:577
  11.7 16.3 %collective-permute-done.7.refs_3_.refs_2_ = bf16[1,256,2048]{2,1,0:T(8,128)(2,1)S(1)} collective-permute-done((bf16[1,256,2048]{2,1,0:T(8,128)(2,1)}, bf16[1,256,2048]{2,1,0:T(8,128)(2,1)S(1)}, u32[]{:S(2)}, u32[]{:S(2)}) %collective-permute-start.7) | collective-permute-done | bytes 1048608 | tf_op jit(solution)/shard_map/ppermute | solution.py:556
  29.1 5.0 %collective-permute-start.2 = (bf16[128,1024]{1,0:T(8,128)(2,1)S(1)}, bf16[128,1024]{1,0:T(8,128)(2,1)S(1)}, u32[]{:S(2)}, u32[]{:S(2)}) collective-permute-start(bf16[128,1024]{1,0:T(8,128)(2,1)S(1)} %broadcast_select_fusion.1), channel_id=1, source_target_pairs={{0,16},{4,20},{1,17},{5,21},{2,18},{6,22},{3,19},{7,23}} | collective-permute-start | bytes 786440 | tf_op jit(solution)/shard_map/ppermute | solution.py:577
  36.5 4.3 %collective-permute-done.2 = bf16[128,1024]{1,0:T(8,128)(2,1)S(1)} collective-permute-done((bf16[128,1024]{1,0:T(8,128)(2,1)S(1)}, bf16[128,1024]{1,0:T(8,128)(2,1)S(1)}, u32[]{:S(2)}, u32[]{:S(2)}) %collective-permute-start.2) | collective-permute-done | bytes 262176 | tf_op jit(solution)/shard_map/ppermute | solution.py:577
  40.8 5.0 %collective-permute-done.4 = bf16[128,1024]{1,0:T(8,128)(2,1)S(1)} collective-permute-done((bf16[128,1024]{1,0:T(8,128)(2,1)S(1)}, bf16[128,1024]{1,0:T(8,128)(2,1)S(1)}, u32[]{:S(2)}, u32[]{:S(2)}) %collective-permute-start.4) | collective-permute-done | bytes 262176 | tf_op jit(solution)/shard_map/ppermute | solution.py:577
  47.8 1.9 %collective-permute-done.19.refs_5_ = bf16[1,256,2048]{2,1,0:T(8,128)(2,1)} collective-permute-done((bf16[1,256,2048]{2,1,0:T(8,128)(2,1)}, bf16[1,256,2048]{2,1,0:T(8,128)(2,1)}, u32[]{:S(2)}, u32[]{:S(2)}) %collective-permute-start.19) | collective-permute-done | bytes 1048608 | tf_op jit(solution)/shard_map/ppermute | solution.py:556
  49.8 4.8 %collective-permute-start.5 = (bf16[128,1024]{1,0:T(8,128)(2,1)S(1)}, bf16[128,1024]{1,0:T(8,128)(2,1)S(1)}, u32[]{:S(2)}, u32[]{:S(2)}) collective-permute-start(bf16[128,1024]{1,0:T(8,128)(2,1)S(1)} %broadcast_select_fusion.3.kept_k_ref), channel_id=1, source_target_pairs={{0,8},{4,12},{16,24},{20,28},{1,9},{5,13},{17,25},{21,29},{2,10},{... | collective-permute-start | bytes 786440 | tf_op jit(solution)/shard_map/ppermute | solution.py:577
  54.6 4.1 %collective-permute-start.6 = (bf16[128,1024]{1,0:T(8,128)(2,1)S(1)}, bf16[128,1024]{1,0:T(8,128)(2,1)}, u32[]{:S(2)}, u32[]{:S(2)}) collective-permute-start(bf16[128,1024]{1,0:T(8,128)(2,1)S(1)} %broadcast_select_fusion.kept_v_ref), channel_id=1, source_target_pairs={{0,4},{8,12},{16,20},{24,28},{1,5},{9,13},{17,21},{25,29},{2,6},{1... | collective-permute-start | bytes 786440 | tf_op jit(solution)/shard_map/ppermute | solution.py:577
  59.4 5.0 %grad_attn.1 = (bf16[256,1024]{1,0:T(8,128)(2,1)}, bf16[256,1024]{1,0:T(8,128)(2,1)}) custom-call(bf16[256,2048]{1,0:T(8,128)(2,1)} %bitcast.34, bf16[256,1024]{1,0:T(8,128)(2,1)} %bitcast.30, bf16[1,256,2048]{2,1,0:T(8,128)(2,1)} %bitcast.37, bf16[1,256,2048]{2,1,0:T(8,128)(2,1)} %copy-done.2, bf16[1,256,2048]{2,1,0:T(8,128)(2,1)} %collective-permute-done.8.refs_4_.refs_3_, ...), custom_call_target="tpu_custom_call" | custom-call | tf_op jit(solution)/shard_map/grad_attn/pallas_call | solution.py:451
  65.3 5.7 %attention_forward.1 = (bf16[256,1024]{1,0:T(8,128)(2,1)}, f32[8,256,384]{2,1,0:T(8,128)}, f32[128,128]{1,0:T(8,128)}, bf16[1,256,512]{2,1,0:T(8,128)(2,1)}, bf16[1,256,256]{2,1,0:T(8,128)(2,1)}) custom-call(bf16[256,1024]{1,0:T(8,128)(2,1)} %bitcast.31, bf16[256,1024]{1,0:T(8,128)(2,1)} %bitcast.22, bf16[256,1024]{1,0:T(8,128)(2,1)} %bitcast.27, ...), custom_call_target="tpu_custom_call" | custom-call | tf_op jit(solution)/shard_map/attention_forward/pallas_call | solution.py:299
  72.6 6.8 %collective-permute-done.16.refs_1_ = bf16[1,256,512]{2,1,0:T(8,128)(2,1)S(1)} collective-permute-done((bf16[1,256,512]{2,1,0:T(8,128)(2,1)}, bf16[1,256,512]{2,1,0:T(8,128)(2,1)S(1)}, u32[]{:S(2)}, u32[]{:S(2)}) %collective-permute-start.16) | collective-permute-done | bytes 262176 | tf_op jit(solution)/shard_map/ppermute | solution.py:556
  79.4 5.6 %attention_backward.1 = (bf16[256,1024]{1,0:T(8,128)(2,1)}, f32[256,1024]{1,0:T(8,128)}, f32[256,1024]{1,0:T(8,128)}, f32[128,1024]{1,0:T(8,128)}, bf16[128,1024]{1,0:T(8,128)(2,1)}) custom-call(bf16[256,1024]{1,0:T(8,128)(2,1)} %bitcast.32, bf16[256,1024]{1,0:T(8,128)(2,1)} %bitcast.23, bf16[256,1024]{1,0:T(8,128)(2,1)} %bitcast.28, ...), custom_call_target="tpu_custom_call" | custom-call | tf_op jit(solution)/shard_map/attention_backward/pallas_call | solution.py:327
  85.1 3.3 %collective-permute-start.12 = (bf16[128,1024]{1,0:T(8,128)(2,1)}, bf16[128,1024]{1,0:T(8,128)(2,1)S(1)}, u32[]{:S(2)}, u32[]{:S(2)}) collective-permute-start(bf16[128,1024]{1,0:T(8,128)(2,1)} %get-tuple-element.40), channel_id=1, source_target_pairs={{0,4},{4,0},{8,12},{12,8},{16,20},{20,16},{24,28},{28,24},{1,5},{5... | collective-permute-start | bytes 786440 | tf_op jit(solution)/shard_map/ppermute | solution.py:556
  90.4 5.6 %weight_grad.1 = (f32[4,256,256]{2,1,0:T(8,128)}, bf16[4,256,256]{2,1,0:T(8,128)(2,1)}) custom-call(bf16[1,256,1024]{2,1,0:T(8,128)(2,1)} %bitcast.33, bf16[1,256,512]{2,1,0:T(8,128)(2,1)} %copy-done.11, bf16[1,256,256]{2,1,0:T(8,128)(2,1)} %copy-done.13, bf16[1,256,512]{2,1,0:T(8,128)(2,1)} %copy-done.12, bf16[1,256,2048]{2,1,0:T(8,128)(2,1)} %refs_4_.1, ...), custom_call_target="tpu_custom_call" | custom-call | tf_op jit(solution)/shard_map/weight_grad/pallas_call | solution.py:481
  98.8 8.5 %collective-permute-done.13 = bf16[128,1024]{1,0:T(8,128)(2,1)S(1)} collective-permute-done((bf16[128,1024]{1,0:T(8,128)(2,1)S(1)}, bf16[128,1024]{1,0:T(8,128)(2,1)S(1)}, u32[]{:S(2)}, u32[]{:S(2)}) %collective-permute-start.13) | collective-permute-done | bytes 262176 | tf_op jit(solution)/shard_map/ppermute | solution.py:588
  108.7 9.5 %collective-permute-done.22 = bf16[2,2,256,256]{3,2,1,0:T(8,128)(2,1)S(1)} collective-permute-done((bf16[2,2,256,256]{3,2,1,0:T(8,128)(2,1)}, bf16[2,2,256,256]{3,2,1,0:T(8,128)(2,1)S(1)}, u32[]{:S(2)}, u32[]{:S(2)}) %collective-permute-start.22) | collective-permute-done | bytes 524320 | tf_op jit(solution)/shard_map/ppermute | solution.py:556
  119.5 3.9 %collective-permute-start.23 = (bf16[2,256,256]{2,1,0:T(8,128)(2,1)S(1)}, bf16[2,256,256]{2,1,0:T(8,128)(2,1)S(1)}, u32[]{:S(2)}, u32[]{:S(2)}) collective-permute-start(bf16[2,256,256]{2,1,0:T(8,128)(2,1)S(1)} %fusion.1), channel_id=1, source_target_pairs={{0,8},{4,12},{8,0},{12,4},{16,24},{20,28},{24,16},{28,20},{1,9},{5... | collective-permute-start | bytes 786440 | tf_op jit(solution)/shard_map/ppermute | solution.py:556
  125.7 3.7 %collective-permute-done.23 = bf16[2,256,256]{2,1,0:T(8,128)(2,1)S(1)} collective-permute-done((bf16[2,256,256]{2,1,0:T(8,128)(2,1)S(1)}, bf16[2,256,256]{2,1,0:T(8,128)(2,1)S(1)}, u32[]{:S(2)}, u32[]{:S(2)}) %collective-permute-start.23) | collective-permute-done | bytes 262176 | tf_op jit(solution)/shard_map/ppermute | solution.py:556
  131.8 4.6 %projected.1 = bf16[256,2048]{1,0:T(8,128)(2,1)} custom-call(bf16[256,1024]{1,0:T(8,128)(2,1)} %get-tuple-element.30.refs_0_.attn_ref, bf16[1,256,2048]{2,1,0:T(8,128)(2,1)} %bitcast.38, bf16[1,256,2048]{2,1,0:T(8,128)(2,1)} %copy-done.2, bf16[1,256,2048]{2,1,0:T(8,128)(2,1)} %collective-permute-done.8.refs_4_.refs_3_, ...), custom_call_target="tpu_custom_call" | custom-call | tf_op jit(solution)/shard_map/projected/pallas_call | solution.py:462
  137.9 4.8 %next_backward.1 = (bf16[256,1024]{1,0:T(8,128)(2,1)}, bf16[256,1024]{1,0:T(8,128)(2,1)}) custom-call(bf16[256,1024]{1,0:T(8,128)(2,1)} %bitcast.24, bf16[256,1024]{1,0:T(8,128)(2,1)} %bitcast.29, bf16[256,1024]{1,0:T(8,128)(2,1)} %copy-done.7, f32[128,128]{1,0:T(8,128)} %copy-done.14, s32[1,8,16,2]{3,2,1,0:T(8,128)} %copy.13.pattern_ref, ...), custom_call_target="tpu_custom_call" | custom-call | tf_op jit(solution)/shard_map/next_backward/pallas_call | solution.py:359
  143.4 2.3 %finish.1 = (bf16[256,1024]{1,0:T(8,128)(2,1)}, bf16[256,1024]{1,0:T(8,128)(2,1)}) custom-call(bf16[256,1024]{1,0:T(8,128)(2,1)} %get-tuple-element.37.part_k_ref, bf16[256,1024]{1,0:T(8,128)(2,1)} %get-tuple-element.38.part_v_ref, f32[256,1024]{1,0:T(8,128)} %get-tuple-element.35.dk_ref.own_k_ref, ...), custom_call_target="tpu_custom_call", output_to_operand_aliasing={{0}: (0, {}), {1}: (1, {})} | custom-call | tf_op jit(solution)/shard_map/finish/pallas_call | solution.py:533
  (85 shorter events, 24.2 us)
Async XLA Ops:
  0.7 27.3 %collective-permute-start.7 = (bf16[1,256,2048]{2,1,0:T(8,128)(2,1)}, bf16[1,256,2048]{2,1,0:T(8,128)(2,1)S(1)}, u32[]{:S(2)}, u32[]{:S(2)}) collective-permute-start(bf16[1,256,2048]{2,1,0:T(8,128)(2,1)} %bitcast.35), channel_id=1, source_target_pairs={{0,2},{1,3},{2,0},{3,1},{4,6},{5,7},{6,4},{7,5},{8,10},{9,11},{10,... | collective-permute-start | bytes 3145736 | tf_op jit(solution)/shard_map/ppermute | solution.py:556
  3.7 45.9 %collective-permute-start.19 = (bf16[1,256,2048]{2,1,0:T(8,128)(2,1)}, bf16[1,256,2048]{2,1,0:T(8,128)(2,1)}, u32[]{:S(2)}, u32[]{:S(2)}) collective-permute-start(bf16[1,256,2048]{2,1,0:T(8,128)(2,1)} %refs_4_.1), channel_id=1, source_target_pairs={{0,2},{1,3},{2,0},{3,1},{4,6},{5,7},{6,4},{7,5},{8,10},{9,11},{10,... | collective-permute-start | bytes 3145736 | tf_op jit(solution)/shard_map/ppermute | solution.py:556
  6.0 22.0 %collective-permute-start.1 = (bf16[128,1024]{1,0:T(8,128)(2,1)}, bf16[128,1024]{1,0:T(8,128)(2,1)S(1)}, u32[]{:S(2)}, u32[]{:S(2)}) collective-permute-start(bf16[128,1024]{1,0:T(8,128)(2,1)} %get-tuple-element.27), channel_id=1, source_target_pairs={{0,4},{1,5},{2,6},{3,7}} | collective-permute-start | bytes 786440 | tf_op jit(solution)/shard_map/ppermute | solution.py:577
  9.8 24.4 %collective-permute-start.3 = (bf16[128,1024]{1,0:T(8,128)(2,1)}, bf16[128,1024]{1,0:T(8,128)(2,1)S(1)}, u32[]{:S(2)}, u32[]{:S(2)}) collective-permute-start(bf16[128,1024]{1,0:T(8,128)(2,1)} %get-tuple-element.28), channel_id=1, source_target_pairs={{0,16},{1,17},{2,18},{3,19}} | collective-permute-start | bytes 786440 | tf_op jit(solution)/shard_map/ppermute | solution.py:577
  11.6 38.2 %collective-permute-start.8 = (bf16[1,256,2048]{2,1,0:T(8,128)(2,1)}, bf16[1,256,2048]{2,1,0:T(8,128)(2,1)}, u32[]{:S(2)}, u32[]{:S(2)}) collective-permute-start(bf16[1,256,2048]{2,1,0:T(8,128)(2,1)} %bitcast.36), channel_id=1, source_target_pairs={{0,1},{1,0},{2,3},{3,2},{4,5},{5,4},{6,7},{7,6},{8,9},{9,8},{10,11... | collective-permute-start | bytes 3145736 | tf_op jit(solution)/shard_map/ppermute | solution.py:556
  27.9 26.6 %collective-permute-start.9 = (bf16[1,256,2048]{2,1,0:T(8,128)(2,1)S(1)}, bf16[1,256,2048]{2,1,0:T(8,128)(2,1)}, u32[]{:S(2)}, u32[]{:S(2)}) collective-permute-start(bf16[1,256,2048]{2,1,0:T(8,128)(2,1)S(1)} %collective-permute-done.7.refs_3_.refs_2_), channel_id=1, source_target_pairs={{0,1},{1,0},{2,3},{3,2},{4,5},{5,4},{6,7},{7,6},{8,9},{9,8},{10,11... | collective-permute-start | bytes 3145736 | tf_op jit(solution)/shard_map/ppermute | solution.py:556
  29.1 11.7 %collective-permute-start.2 = (bf16[128,1024]{1,0:T(8,128)(2,1)S(1)}, bf16[128,1024]{1,0:T(8,128)(2,1)S(1)}, u32[]{:S(2)}, u32[]{:S(2)}) collective-permute-start(bf16[128,1024]{1,0:T(8,128)(2,1)S(1)} %broadcast_select_fusion.1), channel_id=1, source_target_pairs={{0,16},{4,20},{1,17},{5,21},{2,18},{6,22},{3,19},{7,23}} | collective-permute-start | bytes 786440 | tf_op jit(solution)/shard_map/ppermute | solution.py:577
  35.2 10.6 %collective-permute-start.4 = (bf16[128,1024]{1,0:T(8,128)(2,1)S(1)}, bf16[128,1024]{1,0:T(8,128)(2,1)S(1)}, u32[]{:S(2)}, u32[]{:S(2)}) collective-permute-start(bf16[128,1024]{1,0:T(8,128)(2,1)S(1)} %broadcast_select_fusion.2), channel_id=1, source_target_pairs={{0,8},{16,24},{1,9},{17,25},{2,10},{18,26},{3,11},{19,27}} | collective-permute-start | bytes 786440 | tf_op jit(solution)/shard_map/ppermute | solution.py:577
  40.8 47.6 %collective-permute-start.20 = (bf16[1,256,2048]{2,1,0:T(8,128)(2,1)S(1)}, bf16[1,256,2048]{2,1,0:T(8,128)(2,1)}, u32[]{:S(2)}, u32[]{:S(2)}) collective-permute-start(bf16[1,256,2048]{2,1,0:T(8,128)(2,1)S(1)} %copy-done.1), channel_id=1, source_target_pairs={{0,1},{1,0},{2,3},{3,2},{4,5},{5,4},{6,7},{7,6},{8,9},{9,8},{10,11... | collective-permute-start | bytes 3145736 | tf_op jit(solution)/shard_map/ppermute | solution.py:556
  46.5 17.9 %collective-permute-start = (bf16[256,1024]{1,0:T(8,128)(2,1)}, bf16[256,1024]{1,0:T(8,128)(2,1)S(1)}, u32[]{:S(2)}, u32[]{:S(2)}) collective-permute-start(bf16[256,1024]{1,0:T(8,128)(2,1)} %get-tuple-element.26), channel_id=1, source_target_pairs={{0,4},{4,8},{8,12},{12,16},{16,20},{20,24},{24,28},{1,5},{5,9},{9,... | collective-permute-start | bytes 1572872 | tf_op jit(solution)/shard_map/ppermute | solution.py:614
  49.7 38.8 %collective-permute-start.21 = (bf16[1,256,2048]{2,1,0:T(8,128)(2,1)}, bf16[1,256,2048]{2,1,0:T(8,128)(2,1)}, u32[]{:S(2)}, u32[]{:S(2)}) collective-permute-start(bf16[1,256,2048]{2,1,0:T(8,128)(2,1)} %collective-permute-done.19.refs_5_), channel_id=1, source_target_pairs={{0,1},{1,0},{2,3},{3,2},{4,5},{5,4},{6,7},{7,6},{8,9},{9,8},{10,11... | collective-permute-start | bytes 3145736 | tf_op jit(solution)/shard_map/ppermute | solution.py:556
  49.8 14.6 %collective-permute-start.5 = (bf16[128,1024]{1,0:T(8,128)(2,1)S(1)}, bf16[128,1024]{1,0:T(8,128)(2,1)S(1)}, u32[]{:S(2)}, u32[]{:S(2)}) collective-permute-start(bf16[128,1024]{1,0:T(8,128)(2,1)S(1)} %broadcast_select_fusion.3.kept_k_ref), channel_id=1, source_target_pairs={{0,8},{4,12},{16,24},{20,28},{1,9},{5,13},{17,25},{21,29},{2,10},{... | collective-permute-start | bytes 786440 | tf_op jit(solution)/shard_map/ppermute | solution.py:577
  54.6 10.1 %collective-permute-start.6 = (bf16[128,1024]{1,0:T(8,128)(2,1)S(1)}, bf16[128,1024]{1,0:T(8,128)(2,1)}, u32[]{:S(2)}, u32[]{:S(2)}) collective-permute-start(bf16[128,1024]{1,0:T(8,128)(2,1)S(1)} %broadcast_select_fusion.kept_v_ref), channel_id=1, source_target_pairs={{0,4},{8,12},{16,20},{24,28},{1,5},{9,13},{17,21},{25,29},{2,6},{1... | collective-permute-start | bytes 786440 | tf_op jit(solution)/shard_map/ppermute | solution.py:577
  71.0 8.4 %collective-permute-start.16 = (bf16[1,256,512]{2,1,0:T(8,128)(2,1)}, bf16[1,256,512]{2,1,0:T(8,128)(2,1)S(1)}, u32[]{:S(2)}, u32[]{:S(2)}) collective-permute-start(bf16[1,256,512]{2,1,0:T(8,128)(2,1)} %get-tuple-element.43), channel_id=1, source_target_pairs={{0,2},{1,3},{2,0},{3,1},{4,6},{5,7},{6,4},{7,5},{8,10},{9,11},{10,... | collective-permute-start | bytes 786440 | tf_op jit(solution)/shard_map/ppermute | solution.py:556
  79.4 10.3 %collective-permute-start.18 = (bf16[1,256,512]{2,1,0:T(8,128)(2,1)S(1)}, bf16[1,256,512]{2,1,0:T(8,128)(2,1)S(1)}, u32[]{:S(2)}, u32[]{:S(2)}) collective-permute-start(bf16[1,256,512]{2,1,0:T(8,128)(2,1)S(1)} %collective-permute-done.16.refs_1_), channel_id=1, source_target_pairs={{0,1},{1,0},{2,3},{3,2},{4,5},{5,4},{6,7},{7,6},{8,9},{9,8},{10,11... | collective-permute-start | bytes 786440 | tf_op jit(solution)/shard_map/ppermute | solution.py:556
  85.1 11.1 %collective-permute-start.12 = (bf16[128,1024]{1,0:T(8,128)(2,1)}, bf16[128,1024]{1,0:T(8,128)(2,1)S(1)}, u32[]{:S(2)}, u32[]{:S(2)}) collective-permute-start(bf16[128,1024]{1,0:T(8,128)(2,1)} %get-tuple-element.40), channel_id=1, source_target_pairs={{0,4},{4,0},{8,12},{12,8},{16,20},{20,16},{24,28},{28,24},{1,5},{5... | collective-permute-start | bytes 786440 | tf_op jit(solution)/shard_map/ppermute | solution.py:556
  96.0 22.1 %collective-permute-start.22 = (bf16[2,2,256,256]{3,2,1,0:T(8,128)(2,1)}, bf16[2,2,256,256]{3,2,1,0:T(8,128)(2,1)S(1)}, u32[]{:S(2)}, u32[]{:S(2)}) collective-permute-start(bf16[2,2,256,256]{3,2,1,0:T(8,128)(2,1)} %bitcast.44), channel_id=1, source_target_pairs={{0,4},{4,0},{8,12},{12,8},{16,20},{20,16},{24,28},{28,24},{1,5},{5... | collective-permute-start | bytes 1572872 | tf_op jit(solution)/shard_map/ppermute | solution.py:556
  96.2 11.1 %collective-permute-start.13 = (bf16[128,1024]{1,0:T(8,128)(2,1)S(1)}, bf16[128,1024]{1,0:T(8,128)(2,1)S(1)}, u32[]{:S(2)}, u32[]{:S(2)}) collective-permute-start(bf16[128,1024]{1,0:T(8,128)(2,1)S(1)} %fusion), channel_id=1, source_target_pairs={{8,0},{12,4},{24,16},{28,20},{9,1},{13,5},{25,17},{29,21},{10,2},{... | collective-permute-start | bytes 786440 | tf_op jit(solution)/shard_map/ppermute | solution.py:588
  97.5 39.6 %collective-permute-start.10 = (bf16[256,1024]{1,0:T(8,128)(2,1)S(1)}, bf16[256,1024]{1,0:T(8,128)(2,1)S(1)}, u32[]{:S(2)}, u32[]{:S(2)}) collective-permute-start(bf16[256,1024]{1,0:T(8,128)(2,1)S(1)} %copy-done.16), channel_id=1, source_target_pairs={{4,0},{8,4},{12,8},{16,12},{20,16},{24,20},{28,24},{5,1},{9,5},{13... | collective-permute-start | bytes 1572872 | tf_op jit(solution)/shard_map/ppermute | solution.py:624
  107.4 16.1 %collective-permute-start.14 = (bf16[128,1024]{1,0:T(8,128)(2,1)S(1)}, bf16[128,1024]{1,0:T(8,128)(2,1)S(1)}, u32[]{:S(2)}, u32[]{:S(2)}) collective-permute-start(bf16[128,1024]{1,0:T(8,128)(2,1)S(1)} %fusion.2), channel_id=1, source_target_pairs={{16,0},{20,4},{17,1},{21,5},{18,2},{22,6},{19,3},{23,7}} | collective-permute-start | bytes 786440 | tf_op jit(solution)/shard_map/ppermute | solution.py:588
  119.5 9.9 %collective-permute-start.23 = (bf16[2,256,256]{2,1,0:T(8,128)(2,1)S(1)}, bf16[2,256,256]{2,1,0:T(8,128)(2,1)S(1)}, u32[]{:S(2)}, u32[]{:S(2)}) collective-permute-start(bf16[2,256,256]{2,1,0:T(8,128)(2,1)S(1)} %fusion.1), channel_id=1, source_target_pairs={{0,8},{4,12},{8,0},{12,4},{16,24},{20,28},{24,16},{28,20},{1,9},{5... | collective-permute-start | bytes 786440 | tf_op jit(solution)/shard_map/ppermute | solution.py:556
  124.4 18.2 %collective-permute-start.15 = (bf16[128,1024]{1,0:T(8,128)(2,1)S(1)}, bf16[128,1024]{1,0:T(8,128)(2,1)S(1)}, u32[]{:S(2)}, u32[]{:S(2)}) collective-permute-start(bf16[128,1024]{1,0:T(8,128)(2,1)S(1)} %get-tuple-element.47), channel_id=1, source_target_pairs={{4,0},{5,1},{6,2},{7,3}} | collective-permute-start | bytes 786440 | tf_op jit(solution)/shard_map/ppermute | solution.py:590
  129.5 16.1 %collective-permute-start.24 = (bf16[256,256]{1,0:T(8,128)(2,1)S(1)}, bf16[256,256]{1,0:T(8,128)(2,1)S(1)}, u32[]{:S(2)}, u32[]{:S(2)}) collective-permute-start(bf16[256,256]{1,0:T(8,128)(2,1)S(1)} %fusion.3), channel_id=1, source_target_pairs={{0,16},{4,20},{8,24},{12,28},{16,0},{20,4},{24,8},{28,12},{1,17},{... | collective-permute-start | bytes 393224 | tf_op jit(solution)/shard_map/ppermute | solution.py:556
  130.6 6.5 %collective-permute-start.11 = (f32[128,128]{1,0:T(8,128)S(1)}, f32[128,128]{1,0:T(8,128)S(1)}, u32[]{:S(2)}, u32[]{:S(2)}) collective-permute-start(f32[128,128]{1,0:T(8,128)S(1)} %copy-done.18), channel_id=1, source_target_pairs={{4,0},{8,4},{12,8},{16,12},{20,16},{24,20},{28,24},{5,1},{9,5},{13... | collective-permute-start | bytes 196616 | tf_op jit(solution)/shard_map/ppermute | solution.py:627
  (20 other events, 216.6 us)

commit v5 on v4

--- a/solution.py
+++ b/solution.py
@@ -14,6 +14,7 @@
 
 WIN = 2
 HEADS_STEP = 4
+NEAR_K, NEAR_V = 0, 2
 
 ROWS_STEP = 64
 LOG2_E = math.log2(math.e)
@@ -566,6 +567,11 @@
     return pieces
 
 
+def spread_orders(count):
+    near, far_first = bits_of(count)[:1], bits_of(count)[:0:-1]
+    return tuple(far_first[:at] + near + far_first[at:] for at in (NEAR_K, NEAR_V))
+
+
 def spread_first(value, axis, count, order):
     mine = lax.axis_index(axis)
     covered = 0
@@ -607,12 +613,10 @@
 def body(context_count, document_count, queries, keys, values, cotangent, proj_weight, pattern):
     q, k, v, cot = queries[0], keys[0], values[0], cotangent[0]
     rows, _ = q.shape
-    bits = bits_of(context_count)
-    far_first = bits[:0:-1]
 
     first_k, first_v, last = ends_of(k, v)
     before = lax.ppermute(last, "ctx", [(one, one + 1) for one in range(context_count - 1)])
-    order_k, order_v = bits[:1] + far_first, far_first + bits[:1]
+    order_k, order_v = spread_orders(context_count)
     last_bits = order_k[-1], order_v[-1]
     kept_k, got_k = spread_first(first_k, "ctx", context_count, order_k)
     kept_v, got_v = spread_first(first_v, "ctx", context_count, order_v)

time: 148 us -> 148 us (level)
  no operation moved by 1% of the time
where the time goes in v5:
time: 148 us; the launch traced here: 146 us
  waiting for transfers between devices  58.1 us (39%)
  starting transfers between devices  41.8 us (28%)
  Pallas kernels  35.6 us (24%)
  other arithmetic  5.51 us (4%)
  local copies, waits for them, and re-layouts  4.44 us (3%)
    ppermute x13, waiting for transfers between devices, swap(): return lax.ppermute(value, axis, [(one, one ^ bit) for one in range(count)])  39.4 us
    ppermute x6, starting transfers between devices, spread_first(): got = lax.ppermute(value, axis, pairs)  20.8 us
    ppermute x13, starting transfers between devices, swap(): return lax.ppermute(value, axis, [(one, one ^ bit) for one in range(count)])  13.3 us
    ppermute x6, waiting for transfers between devices, spread_first(): got = lax.ppermute(value, axis, pairs)  9.52 us
    ppermute x2, waiting for transfers between devices, sum_to_first(): kept = kept + lax.ppermute(kept.astype(BF16), axis, pairs).astype(F32)  8.45 us
    pallas_call x1, Pallas kernels, attention_forward(): pl.pallas_call(functools.partial(forward_kernel, count, last_bits), grid=...  5.71 us
    pallas_call x1, Pallas kernels, attention_backward(): pl.pallas_call(functools.partial(backward_kernel, last_bits), grid=(width...  5.59 us
    pallas_call x1, Pallas kernels, weight_grad_of(): pl.pallas_call(functools.partial(weight_grad_kernel, scale, len(attn_piec...  5.56 us
  transfers between devices with their start and end apart: 25, of which 11 were waited for; matrix products, arithmetic and copies ran while one was open for 4% of the time, Pallas kernels for 24%

profile of v5, /device:TPU:0, one launch (start us, length us, event | category | flops | bytes accessed | tf_op | source)
XLA Modules:
  0.0 146.4 jit_solution(15741227150680263667)
XLA Ops:
  0.7 3.1 %collective-permute-start.7 = (bf16[1,256,2048]{2,1,0:T(8,128)(2,1)}, bf16[1,256,2048]{2,1,0:T(8,128)(2,1)S(1)}, u32[]{:S(2)}, u32[]{:S(2)}) collective-permute-start(bf16[1,256,2048]{2,1,0:T(8,128)(2,1)} %bitcast.35), channel_id=1, source_target_pairs={{0,2},{1,3},{2,0},{3,1},{4,6},{5,7},{6,4},{7,5},{8,10},{9,11},{10,... | collective-permute-start | bytes 3145736 | tf_op jit(solution)/shard_map/ppermute | solution.py:557
  3.8 2.2 %ends.1 = (bf16[128,1024]{1,0:T(8,128)(2,1)}, bf16[128,1024]{1,0:T(8,128)(2,1)}, bf16[256,1024]{1,0:T(8,128)(2,1)}) custom-call(bf16[256,1024]{1,0:T(8,128)(2,1)} %bitcast.20, bf16[256,1024]{1,0:T(8,128)(2,1)} %bitcast.25, bf16[256,1024]{1,0:T(8,128)(2,1)} %bitcast.21, bf16[256,1024]{1,0:T(8,128)(2,1)} %bitcast.26), custom_call_target="tpu_custom_call" | custom-call | tf_op jit(solution)/shard_map/ends/pallas_call | solution.py:256
  6.0 3.8 %collective-permute-start.1 = (bf16[128,1024]{1,0:T(8,128)(2,1)}, bf16[128,1024]{1,0:T(8,128)(2,1)S(1)}, u32[]{:S(2)}, u32[]{:S(2)}) collective-permute-start(bf16[128,1024]{1,0:T(8,128)(2,1)} %get-tuple-element.27), channel_id=1, source_target_pairs={{0,4},{1,5},{2,6},{3,7}} | collective-permute-start | bytes 786440 | tf_op jit(solution)/shard_map/ppermute | solution.py:583
  9.8 1.8 %collective-permute-start.3 = (bf16[128,1024]{1,0:T(8,128)(2,1)}, bf16[128,1024]{1,0:T(8,128)(2,1)S(1)}, u32[]{:S(2)}, u32[]{:S(2)}) collective-permute-start(bf16[128,1024]{1,0:T(8,128)(2,1)} %get-tuple-element.28), channel_id=1, source_target_pairs={{0,16},{1,17},{2,18},{3,19}} | collective-permute-start | bytes 786440 | tf_op jit(solution)/shard_map/ppermute | solution.py:583
  11.7 16.3 %collective-permute-done.7.refs_3_.refs_2_ = bf16[1,256,2048]{2,1,0:T(8,128)(2,1)S(1)} collective-permute-done((bf16[1,256,2048]{2,1,0:T(8,128)(2,1)}, bf16[1,256,2048]{2,1,0:T(8,128)(2,1)S(1)}, u32[]{:S(2)}, u32[]{:S(2)}) %collective-permute-start.7) | collective-permute-done | bytes 1048608 | tf_op jit(solution)/shard_map/ppermute | solution.py:557
  29.1 5.0 %collective-permute-start.2 = (bf16[128,1024]{1,0:T(8,128)(2,1)S(1)}, bf16[128,1024]{1,0:T(8,128)(2,1)S(1)}, u32[]{:S(2)}, u32[]{:S(2)}) collective-permute-start(bf16[128,1024]{1,0:T(8,128)(2,1)S(1)} %broadcast_select_fusion.1), channel_id=1, source_target_pairs={{0,16},{4,20},{1,17},{5,21},{2,18},{6,22},{3,19},{7,23}} | collective-permute-start | bytes 786440 | tf_op jit(solution)/shard_map/ppermute | solution.py:583
  36.5 4.3 %collective-permute-done.2 = bf16[128,1024]{1,0:T(8,128)(2,1)S(1)} collective-permute-done((bf16[128,1024]{1,0:T(8,128)(2,1)S(1)}, bf16[128,1024]{1,0:T(8,128)(2,1)S(1)}, u32[]{:S(2)}, u32[]{:S(2)}) %collective-permute-start.2) | collective-permute-done | bytes 262176 | tf_op jit(solution)/shard_map/ppermute | solution.py:583
  40.8 5.0 %collective-permute-done.4 = bf16[128,1024]{1,0:T(8,128)(2,1)S(1)} collective-permute-done((bf16[128,1024]{1,0:T(8,128)(2,1)S(1)}, bf16[128,1024]{1,0:T(8,128)(2,1)S(1)}, u32[]{:S(2)}, u32[]{:S(2)}) %collective-permute-start.4) | collective-permute-done | bytes 262176 | tf_op jit(solution)/shard_map/ppermute | solution.py:583
  47.8 1.9 %collective-permute-done.19.refs_5_ = bf16[1,256,2048]{2,1,0:T(8,128)(2,1)} collective-permute-done((bf16[1,256,2048]{2,1,0:T(8,128)(2,1)}, bf16[1,256,2048]{2,1,0:T(8,128)(2,1)}, u32[]{:S(2)}, u32[]{:S(2)}) %collective-permute-start.19) | collective-permute-done | bytes 1048608 | tf_op jit(solution)/shard_map/ppermute | solution.py:557
  49.8 4.8 %collective-permute-start.5 = (bf16[128,1024]{1,0:T(8,128)(2,1)S(1)}, bf16[128,1024]{1,0:T(8,128)(2,1)S(1)}, u32[]{:S(2)}, u32[]{:S(2)}) collective-permute-start(bf16[128,1024]{1,0:T(8,128)(2,1)S(1)} %broadcast_select_fusion.3.kept_k_ref), channel_id=1, source_target_pairs={{0,8},{4,12},{16,24},{20,28},{1,9},{5,13},{17,25},{21,29},{2,10},{... | collective-permute-start | bytes 786440 | tf_op jit(solution)/shard_map/ppermute | solution.py:583
  54.6 4.1 %collective-permute-start.6 = (bf16[128,1024]{1,0:T(8,128)(2,1)S(1)}, bf16[128,1024]{1,0:T(8,128)(2,1)}, u32[]{:S(2)}, u32[]{:S(2)}) collective-permute-start(bf16[128,1024]{1,0:T(8,128)(2,1)S(1)} %broadcast_select_fusion.kept_v_ref), channel_id=1, source_target_pairs={{0,4},{8,12},{16,20},{24,28},{1,5},{9,13},{17,21},{25,29},{2,6},{1... | collective-permute-start | bytes 786440 | tf_op jit(solution)/shard_map/ppermute | solution.py:583
  59.4 5.0 %grad_attn.1 = (bf16[256,1024]{1,0:T(8,128)(2,1)}, bf16[256,1024]{1,0:T(8,128)(2,1)}) custom-call(bf16[256,2048]{1,0:T(8,128)(2,1)} %bitcast.34, bf16[256,1024]{1,0:T(8,128)(2,1)} %bitcast.30, bf16[1,256,2048]{2,1,0:T(8,128)(2,1)} %bitcast.37, bf16[1,256,2048]{2,1,0:T(8,128)(2,1)} %copy-done.2, bf16[1,256,2048]{2,1,0:T(8,128)(2,1)} %collective-permute-done.8.refs_4_.refs_3_, ...), custom_call_target="tpu_custom_call" | custom-call | tf_op jit(solution)/shard_map/grad_attn/pallas_call | solution.py:452
  65.3 5.7 %attention_forward.1 = (bf16[256,1024]{1,0:T(8,128)(2,1)}, f32[8,256,384]{2,1,0:T(8,128)}, f32[128,128]{1,0:T(8,128)}, bf16[1,256,512]{2,1,0:T(8,128)(2,1)}, bf16[1,256,256]{2,1,0:T(8,128)(2,1)}) custom-call(bf16[256,1024]{1,0:T(8,128)(2,1)} %bitcast.31, bf16[256,1024]{1,0:T(8,128)(2,1)} %bitcast.22, bf16[256,1024]{1,0:T(8,128)(2,1)} %bitcast.27, ...), custom_call_target="tpu_custom_call" | custom-call | tf_op jit(solution)/shard_map/attention_forward/pallas_call | solution.py:300
  72.6 6.8 %collective-permute-done.16.refs_1_ = bf16[1,256,512]{2,1,0:T(8,128)(2,1)S(1)} collective-permute-done((bf16[1,256,512]{2,1,0:T(8,128)(2,1)}, bf16[1,256,512]{2,1,0:T(8,128)(2,1)S(1)}, u32[]{:S(2)}, u32[]{:S(2)}) %collective-permute-start.16) | collective-permute-done | bytes 262176 | tf_op jit(solution)/shard_map/ppermute | solution.py:557
  79.4 5.6 %attention_backward.1 = (bf16[256,1024]{1,0:T(8,128)(2,1)}, f32[256,1024]{1,0:T(8,128)}, f32[256,1024]{1,0:T(8,128)}, f32[128,1024]{1,0:T(8,128)}, bf16[128,1024]{1,0:T(8,128)(2,1)}) custom-call(bf16[256,1024]{1,0:T(8,128)(2,1)} %bitcast.32, bf16[256,1024]{1,0:T(8,128)(2,1)} %bitcast.23, bf16[256,1024]{1,0:T(8,128)(2,1)} %bitcast.28, ...), custom_call_target="tpu_custom_call" | custom-call | tf_op jit(solution)/shard_map/attention_backward/pallas_call | solution.py:328
  85.1 3.3 %collective-permute-start.12 = (bf16[128,1024]{1,0:T(8,128)(2,1)}, bf16[128,1024]{1,0:T(8,128)(2,1)S(1)}, u32[]{:S(2)}, u32[]{:S(2)}) collective-permute-start(bf16[128,1024]{1,0:T(8,128)(2,1)} %get-tuple-element.40), channel_id=1, source_target_pairs={{0,4},{4,0},{8,12},{12,8},{16,20},{20,16},{24,28},{28,24},{1,5},{5... | collective-permute-start | bytes 786440 | tf_op jit(solution)/shard_map/ppermute | solution.py:557
  90.4 5.6 %weight_grad.1 = (f32[4,256,256]{2,1,0:T(8,128)}, bf16[4,256,256]{2,1,0:T(8,128)(2,1)}) custom-call(bf16[1,256,1024]{2,1,0:T(8,128)(2,1)} %bitcast.33, bf16[1,256,512]{2,1,0:T(8,128)(2,1)} %copy-done.11, bf16[1,256,256]{2,1,0:T(8,128)(2,1)} %copy-done.13, bf16[1,256,512]{2,1,0:T(8,128)(2,1)} %copy-done.12, bf16[1,256,2048]{2,1,0:T(8,128)(2,1)} %refs_4_.1, ...), custom_call_target="tpu_custom_call" | custom-call | tf_op jit(solution)/shard_map/weight_grad/pallas_call | solution.py:482
  98.8 8.5 %collective-permute-done.13 = bf16[128,1024]{1,0:T(8,128)(2,1)S(1)} collective-permute-done((bf16[128,1024]{1,0:T(8,128)(2,1)S(1)}, bf16[128,1024]{1,0:T(8,128)(2,1)S(1)}, u32[]{:S(2)}, u32[]{:S(2)}) %collective-permute-start.13) | collective-permute-done | bytes 262176 | tf_op jit(solution)/shard_map/ppermute | solution.py:594
  108.7 9.5 %collective-permute-done.22 = bf16[2,2,256,256]{3,2,1,0:T(8,128)(2,1)S(1)} collective-permute-done((bf16[2,2,256,256]{3,2,1,0:T(8,128)(2,1)}, bf16[2,2,256,256]{3,2,1,0:T(8,128)(2,1)S(1)}, u32[]{:S(2)}, u32[]{:S(2)}) %collective-permute-start.22) | collective-permute-done | bytes 524320 | tf_op jit(solution)/shard_map/ppermute | solution.py:557
  119.5 3.9 %collective-permute-start.23 = (bf16[2,256,256]{2,1,0:T(8,128)(2,1)S(1)}, bf16[2,256,256]{2,1,0:T(8,128)(2,1)S(1)}, u32[]{:S(2)}, u32[]{:S(2)}) collective-permute-start(bf16[2,256,256]{2,1,0:T(8,128)(2,1)S(1)} %fusion.1), channel_id=1, source_target_pairs={{0,8},{4,12},{8,0},{12,4},{16,24},{20,28},{24,16},{28,20},{1,9},{5... | collective-permute-start | bytes 786440 | tf_op jit(solution)/shard_map/ppermute | solution.py:557
  125.7 3.7 %collective-permute-done.23 = bf16[2,256,256]{2,1,0:T(8,128)(2,1)S(1)} collective-permute-done((bf16[2,256,256]{2,1,0:T(8,128)(2,1)S(1)}, bf16[2,256,256]{2,1,0:T(8,128)(2,1)S(1)}, u32[]{:S(2)}, u32[]{:S(2)}) %collective-permute-start.23) | collective-permute-done | bytes 262176 | tf_op jit(solution)/shard_map/ppermute | solution.py:557
  131.8 4.6 %projected.1 = bf16[256,2048]{1,0:T(8,128)(2,1)} custom-call(bf16[256,1024]{1,0:T(8,128)(2,1)} %get-tuple-element.30.refs_0_.attn_ref, bf16[1,256,2048]{2,1,0:T(8,128)(2,1)} %bitcast.38, bf16[1,256,2048]{2,1,0:T(8,128)(2,1)} %copy-done.2, bf16[1,256,2048]{2,1,0:T(8,128)(2,1)} %collective-permute-done.8.refs_4_.refs_3_, ...), custom_call_target="tpu_custom_call" | custom-call | tf_op jit(solution)/shard_map/projected/pallas_call | solution.py:463
  137.9 4.8 %next_backward.1 = (bf16[256,1024]{1,0:T(8,128)(2,1)}, bf16[256,1024]{1,0:T(8,128)(2,1)}) custom-call(bf16[256,1024]{1,0:T(8,128)(2,1)} %bitcast.24, bf16[256,1024]{1,0:T(8,128)(2,1)} %bitcast.29, bf16[256,1024]{1,0:T(8,128)(2,1)} %copy-done.7, f32[128,128]{1,0:T(8,128)} %copy-done.14, s32[1,8,16,2]{3,2,1,0:T(8,128)} %copy.13.pattern_ref, ...), custom_call_target="tpu_custom_call" | custom-call | tf_op jit(solution)/shard_map/next_backward/pallas_call | solution.py:360
  143.4 2.3 %finish.1 = (bf16[256,1024]{1,0:T(8,128)(2,1)}, bf16[256,1024]{1,0:T(8,128)(2,1)}) custom-call(bf16[256,1024]{1,0:T(8,128)(2,1)} %get-tuple-element.37.part_k_ref, bf16[256,1024]{1,0:T(8,128)(2,1)} %get-tuple-element.38.part_v_ref, f32[256,1024]{1,0:T(8,128)} %get-tuple-element.35.dk_ref.own_k_ref, ...), custom_call_target="tpu_custom_call", output_to_operand_aliasing={{0}: (0, {}), {1}: (1, {})} | custom-call | tf_op jit(solution)/shard_map/finish/pallas_call | solution.py:534
  (85 shorter events, 24.2 us)
Async XLA Ops:
  0.7 27.3 %collective-permute-start.7 = (bf16[1,256,2048]{2,1,0:T(8,128)(2,1)}, bf16[1,256,2048]{2,1,0:T(8,128)(2,1)S(1)}, u32[]{:S(2)}, u32[]{:S(2)}) collective-permute-start(bf16[1,256,2048]{2,1,0:T(8,128)(2,1)} %bitcast.35), channel_id=1, source_target_pairs={{0,2},{1,3},{2,0},{3,1},{4,6},{5,7},{6,4},{7,5},{8,10},{9,11},{10,... | collective-permute-start | bytes 3145736 | tf_op jit(solution)/shard_map/ppermute | solution.py:557
  3.7 45.9 %collective-permute-start.19 = (bf16[1,256,2048]{2,1,0:T(8,128)(2,1)}, bf16[1,256,2048]{2,1,0:T(8,128)(2,1)}, u32[]{:S(2)}, u32[]{:S(2)}) collective-permute-start(bf16[1,256,2048]{2,1,0:T(8,128)(2,1)} %refs_4_.1), channel_id=1, source_target_pairs={{0,2},{1,3},{2,0},{3,1},{4,6},{5,7},{6,4},{7,5},{8,10},{9,11},{10,... | collective-permute-start | bytes 3145736 | tf_op jit(solution)/shard_map/ppermute | solution.py:557
  6.0 22.0 %collective-permute-start.1 = (bf16[128,1024]{1,0:T(8,128)(2,1)}, bf16[128,1024]{1,0:T(8,128)(2,1)S(1)}, u32[]{:S(2)}, u32[]{:S(2)}) collective-permute-start(bf16[128,1024]{1,0:T(8,128)(2,1)} %get-tuple-element.27), channel_id=1, source_target_pairs={{0,4},{1,5},{2,6},{3,7}} | collective-permute-start | bytes 786440 | tf_op jit(solution)/shard_map/ppermute | solution.py:583
  9.8 24.4 %collective-permute-start.3 = (bf16[128,1024]{1,0:T(8,128)(2,1)}, bf16[128,1024]{1,0:T(8,128)(2,1)S(1)}, u32[]{:S(2)}, u32[]{:S(2)}) collective-permute-start(bf16[128,1024]{1,0:T(8,128)(2,1)} %get-tuple-element.28), channel_id=1, source_target_pairs={{0,16},{1,17},{2,18},{3,19}} | collective-permute-start | bytes 786440 | tf_op jit(solution)/shard_map/ppermute | solution.py:583
  11.6 38.2 %collective-permute-start.8 = (bf16[1,256,2048]{2,1,0:T(8,128)(2,1)}, bf16[1,256,2048]{2,1,0:T(8,128)(2,1)}, u32[]{:S(2)}, u32[]{:S(2)}) collective-permute-start(bf16[1,256,2048]{2,1,0:T(8,128)(2,1)} %bitcast.36), channel_id=1, source_target_pairs={{0,1},{1,0},{2,3},{3,2},{4,5},{5,4},{6,7},{7,6},{8,9},{9,8},{10,11... | collective-permute-start | bytes 3145736 | tf_op jit(solution)/shard_map/ppermute | solution.py:557
  27.9 26.6 %collective-permute-start.9 = (bf16[1,256,2048]{2,1,0:T(8,128)(2,1)S(1)}, bf16[1,256,2048]{2,1,0:T(8,128)(2,1)}, u32[]{:S(2)}, u32[]{:S(2)}) collective-permute-start(bf16[1,256,2048]{2,1,0:T(8,128)(2,1)S(1)} %collective-permute-done.7.refs_3_.refs_2_), channel_id=1, source_target_pairs={{0,1},{1,0},{2,3},{3,2},{4,5},{5,4},{6,7},{7,6},{8,9},{9,8},{10,11... | collective-permute-start | bytes 3145736 | tf_op jit(solution)/shard_map/ppermute | solution.py:557
  29.1 11.7 %collective-permute-start.2 = (bf16[128,1024]{1,0:T(8,128)(2,1)S(1)}, bf16[128,1024]{1,0:T(8,128)(2,1)S(1)}, u32[]{:S(2)}, u32[]{:S(2)}) collective-permute-start(bf16[128,1024]{1,0:T(8,128)(2,1)S(1)} %broadcast_select_fusion.1), channel_id=1, source_target_pairs={{0,16},{4,20},{1,17},{5,21},{2,18},{6,22},{3,19},{7,23}} | collective-permute-start | bytes 786440 | tf_op jit(solution)/shard_map/ppermute | solution.py:583
  35.2 10.6 %collective-permute-start.4 = (bf16[128,1024]{1,0:T(8,128)(2,1)S(1)}, bf16[128,1024]{1,0:T(8,128)(2,1)S(1)}, u32[]{:S(2)}, u32[]{:S(2)}) collective-permute-start(bf16[128,1024]{1,0:T(8,128)(2,1)S(1)} %broadcast_select_fusion.2), channel_id=1, source_target_pairs={{0,8},{16,24},{1,9},{17,25},{2,10},{18,26},{3,11},{19,27}} | collective-permute-start | bytes 786440 | tf_op jit(solution)/shard_map/ppermute | solution.py:583
  40.8 47.6 %collective-permute-start.20 = (bf16[1,256,2048]{2,1,0:T(8,128)(2,1)S(1)}, bf16[1,256,2048]{2,1,0:T(8,128)(2,1)}, u32[]{:S(2)}, u32[]{:S(2)}) collective-permute-start(bf16[1,256,2048]{2,1,0:T(8,128)(2,1)S(1)} %copy-done.1), channel_id=1, source_target_pairs={{0,1},{1,0},{2,3},{3,2},{4,5},{5,4},{6,7},{7,6},{8,9},{9,8},{10,11... | collective-permute-start | bytes 3145736 | tf_op jit(solution)/shard_map/ppermute | solution.py:557
  46.5 17.9 %collective-permute-start = (bf16[256,1024]{1,0:T(8,128)(2,1)}, bf16[256,1024]{1,0:T(8,128)(2,1)S(1)}, u32[]{:S(2)}, u32[]{:S(2)}) collective-permute-start(bf16[256,1024]{1,0:T(8,128)(2,1)} %get-tuple-element.26), channel_id=1, source_target_pairs={{0,4},{4,8},{8,12},{12,16},{16,20},{20,24},{24,28},{1,5},{5,9},{9,... | collective-permute-start | bytes 1572872 | tf_op jit(solution)/shard_map/ppermute | solution.py:618
  49.7 38.8 %collective-permute-start.21 = (bf16[1,256,2048]{2,1,0:T(8,128)(2,1)}, bf16[1,256,2048]{2,1,0:T(8,128)(2,1)}, u32[]{:S(2)}, u32[]{:S(2)}) collective-permute-start(bf16[1,256,2048]{2,1,0:T(8,128)(2,1)} %collective-permute-done.19.refs_5_), channel_id=1, source_target_pairs={{0,1},{1,0},{2,3},{3,2},{4,5},{5,4},{6,7},{7,6},{8,9},{9,8},{10,11... | collective-permute-start | bytes 3145736 | tf_op jit(solution)/shard_map/ppermute | solution.py:557
  49.8 14.6 %collective-permute-start.5 = (bf16[128,1024]{1,0:T(8,128)(2,1)S(1)}, bf16[128,1024]{1,0:T(8,128)(2,1)S(1)}, u32[]{:S(2)}, u32[]{:S(2)}) collective-permute-start(bf16[128,1024]{1,0:T(8,128)(2,1)S(1)} %broadcast_select_fusion.3.kept_k_ref), channel_id=1, source_target_pairs={{0,8},{4,12},{16,24},{20,28},{1,9},{5,13},{17,25},{21,29},{2,10},{... | collective-permute-start | bytes 786440 | tf_op jit(solution)/shard_map/ppermute | solution.py:583
  54.6 10.1 %collective-permute-start.6 = (bf16[128,1024]{1,0:T(8,128)(2,1)S(1)}, bf16[128,1024]{1,0:T(8,128)(2,1)}, u32[]{:S(2)}, u32[]{:S(2)}) collective-permute-start(bf16[128,1024]{1,0:T(8,128)(2,1)S(1)} %broadcast_select_fusion.kept_v_ref), channel_id=1, source_target_pairs={{0,4},{8,12},{16,20},{24,28},{1,5},{9,13},{17,21},{25,29},{2,6},{1... | collective-permute-start | bytes 786440 | tf_op jit(solution)/shard_map/ppermute | solution.py:583
  71.0 8.4 %collective-permute-start.16 = (bf16[1,256,512]{2,1,0:T(8,128)(2,1)}, bf16[1,256,512]{2,1,0:T(8,128)(2,1)S(1)}, u32[]{:S(2)}, u32[]{:S(2)}) collective-permute-start(bf16[1,256,512]{2,1,0:T(8,128)(2,1)} %get-tuple-element.43), channel_id=1, source_target_pairs={{0,2},{1,3},{2,0},{3,1},{4,6},{5,7},{6,4},{7,5},{8,10},{9,11},{10,... | collective-permute-start | bytes 786440 | tf_op jit(solution)/shard_map/ppermute | solution.py:557
  79.4 10.3 %collective-permute-start.18 = (bf16[1,256,512]{2,1,0:T(8,128)(2,1)S(1)}, bf16[1,256,512]{2,1,0:T(8,128)(2,1)S(1)}, u32[]{:S(2)}, u32[]{:S(2)}) collective-permute-start(bf16[1,256,512]{2,1,0:T(8,128)(2,1)S(1)} %collective-permute-done.16.refs_1_), channel_id=1, source_target_pairs={{0,1},{1,0},{2,3},{3,2},{4,5},{5,4},{6,7},{7,6},{8,9},{9,8},{10,11... | collective-permute-start | bytes 786440 | tf_op jit(solution)/shard_map/ppermute | solution.py:557
  85.1 11.1 %collective-permute-start.12 = (bf16[128,1024]{1,0:T(8,128)(2,1)}, bf16[128,1024]{1,0:T(8,128)(2,1)S(1)}, u32[]{:S(2)}, u32[]{:S(2)}) collective-permute-start(bf16[128,1024]{1,0:T(8,128)(2,1)} %get-tuple-element.40), channel_id=1, source_target_pairs={{0,4},{4,0},{8,12},{12,8},{16,20},{20,16},{24,28},{28,24},{1,5},{5... | collective-permute-start | bytes 786440 | tf_op jit(solution)/shard_map/ppermute | solution.py:557
  96.0 22.1 %collective-permute-start.22 = (bf16[2,2,256,256]{3,2,1,0:T(8,128)(2,1)}, bf16[2,2,256,256]{3,2,1,0:T(8,128)(2,1)S(1)}, u32[]{:S(2)}, u32[]{:S(2)}) collective-permute-start(bf16[2,2,256,256]{3,2,1,0:T(8,128)(2,1)} %bitcast.44), channel_id=1, source_target_pairs={{0,4},{4,0},{8,12},{12,8},{16,20},{20,16},{24,28},{28,24},{1,5},{5... | collective-permute-start | bytes 1572872 | tf_op jit(solution)/shard_map/ppermute | solution.py:557
  96.2 11.1 %collective-permute-start.13 = (bf16[128,1024]{1,0:T(8,128)(2,1)S(1)}, bf16[128,1024]{1,0:T(8,128)(2,1)S(1)}, u32[]{:S(2)}, u32[]{:S(2)}) collective-permute-start(bf16[128,1024]{1,0:T(8,128)(2,1)S(1)} %fusion), channel_id=1, source_target_pairs={{8,0},{12,4},{24,16},{28,20},{9,1},{13,5},{25,17},{29,21},{10,2},{... | collective-permute-start | bytes 786440 | tf_op jit(solution)/shard_map/ppermute | solution.py:594
  97.5 39.6 %collective-permute-start.10 = (bf16[256,1024]{1,0:T(8,128)(2,1)S(1)}, bf16[256,1024]{1,0:T(8,128)(2,1)S(1)}, u32[]{:S(2)}, u32[]{:S(2)}) collective-permute-start(bf16[256,1024]{1,0:T(8,128)(2,1)S(1)} %copy-done.16), channel_id=1, source_target_pairs={{4,0},{8,4},{12,8},{16,12},{20,16},{24,20},{28,24},{5,1},{9,5},{13... | collective-permute-start | bytes 1572872 | tf_op jit(solution)/shard_map/ppermute | solution.py:628
  107.4 16.1 %collective-permute-start.14 = (bf16[128,1024]{1,0:T(8,128)(2,1)S(1)}, bf16[128,1024]{1,0:T(8,128)(2,1)S(1)}, u32[]{:S(2)}, u32[]{:S(2)}) collective-permute-start(bf16[128,1024]{1,0:T(8,128)(2,1)S(1)} %fusion.2), channel_id=1, source_target_pairs={{16,0},{20,4},{17,1},{21,5},{18,2},{22,6},{19,3},{23,7}} | collective-permute-start | bytes 786440 | tf_op jit(solution)/shard_map/ppermute | solution.py:594
  119.5 9.9 %collective-permute-start.23 = (bf16[2,256,256]{2,1,0:T(8,128)(2,1)S(1)}, bf16[2,256,256]{2,1,0:T(8,128)(2,1)S(1)}, u32[]{:S(2)}, u32[]{:S(2)}) collective-permute-start(bf16[2,256,256]{2,1,0:T(8,128)(2,1)S(1)} %fusion.1), channel_id=1, source_target_pairs={{0,8},{4,12},{8,0},{12,4},{16,24},{20,28},{24,16},{28,20},{1,9},{5... | collective-permute-start | bytes 786440 | tf_op jit(solution)/shard_map/ppermute | solution.py:557
  124.4 18.2 %collective-permute-start.15 = (bf16[128,1024]{1,0:T(8,128)(2,1)S(1)}, bf16[128,1024]{1,0:T(8,128)(2,1)S(1)}, u32[]{:S(2)}, u32[]{:S(2)}) collective-permute-start(bf16[128,1024]{1,0:T(8,128)(2,1)S(1)} %get-tuple-element.47), channel_id=1, source_target_pairs={{4,0},{5,1},{6,2},{7,3}} | collective-permute-start | bytes 786440 | tf_op jit(solution)/shard_map/ppermute | solution.py:596
  129.5 16.1 %collective-permute-start.24 = (bf16[256,256]{1,0:T(8,128)(2,1)S(1)}, bf16[256,256]{1,0:T(8,128)(2,1)S(1)}, u32[]{:S(2)}, u32[]{:S(2)}) collective-permute-start(bf16[256,256]{1,0:T(8,128)(2,1)S(1)} %fusion.3), channel_id=1, source_target_pairs={{0,16},{4,20},{8,24},{12,28},{16,0},{20,4},{24,8},{28,12},{1,17},{... | collective-permute-start | bytes 393224 | tf_op jit(solution)/shard_map/ppermute | solution.py:557
  130.6 6.5 %collective-permute-start.11 = (f32[128,128]{1,0:T(8,128)S(1)}, f32[128,128]{1,0:T(8,128)S(1)}, u32[]{:S(2)}, u32[]{:S(2)}) collective-permute-start(f32[128,128]{1,0:T(8,128)S(1)} %copy-done.18), channel_id=1, source_target_pairs={{4,0},{8,4},{12,8},{16,12},{20,16},{24,20},{28,24},{5,1},{9,5},{13... | collective-permute-start | bytes 196616 | tf_op jit(solution)/shard_map/ppermute | solution.py:631
  (20 other events, 216.6 us)
